TPU v7x, 32 devices: a whole 2x2x4 slice. The times are simulated.
32 devices in a mesh: ens: 2 (over x), lat: 4 (over y, core), lon: 4 (over z).
Axes of the slice: x: 2, y: 2, z: 4, core: 2. Of those that a mesh axis runs over, the one named last changes fastest.
Arguments:
- field_in: bfloat16 [64, 512, 256], P(('ens', 'lat'), 'lon'), parts along dimension 0, may hold values from -6 to 6
- quadrature: float32 [32, 3, 8, 129], P('lat'), may hold values from -6 to 6
- half_width: int32 [32], P('lat'), may hold values from 1 to 64, as said below
- mixing: bfloat16 [8, 256, 256], replicated, may hold values from -0.125 to 0.125
- cotangent: bfloat16 [64, 512, 256], P(('ens', 'lat'), 'lon'), parts along dimension 0, may hold values from -6 to 6
Outputs:
- field_out: bfloat16 [64, 512, 256], P(('ens', 'lat'), 'lon'), parts along dimension 0
- input_grad: bfloat16 [64, 512, 256], P(('ens', 'lat'), 'lon'), parts along dimension 0
- weight_grad: float32 [8, 512, 256], P('lon', 'ens'), parts along dimension 1
There are 2 independent parts, one for each index of `ens`. A program takes and returns all parts, laid end to end along the dimension named above; an argument that names none is the same for every part. Nothing has to cross between parts.
Inputs may be any that keep to these rules, and one draw needn't show every extreme that they name: `half_width`: 64 is reached at the polar rows in every draw.
All inputs are finite; a program needn't handle non-finite values.
Results may differ from a plain program's by a relative error of at most 0.0058.
Values may be sent and summed in bfloat16 or wider, within the bound.
No kernel may reach another device: no remote copies, remote signals or barrier semaphores. Data moves between devices by JAX's collectives and lax.ppermute only.
A program may use at most 128 MiB of HBM per device.

v0:
```python
import jax
import jax.numpy as jnp
from jax import lax
from jax.sharding import PartitionSpec as P


def extended_2(array, sides, width, wrap):
    for axis, dim in sides:
        count, length = (lax.axis_size(axis), array.shape[dim])
        up = [(i, (i + 1) % count) for i in range(count if wrap else count - 1)]
        down = [(j, i) for i, j in up]
        last = lax.slice_in_dim(array, length - width, length, axis=dim)
        leading = lax.slice_in_dim(array, 0, width, axis=dim)
        before = lax.ppermute(last, axis, up)
        after = lax.ppermute(leading, axis, down)
        array = jnp.concatenate([before, array, after], axis=dim)
    return array


def passed_along(block, axis, distance):
    devices = range(lax.axis_size(axis))
    route = [((i - distance) % len(devices), i) for i in devices]
    return lax.ppermute(block, axis, route)


def from_behind(value, axis, steps):
    count = lax.axis_size(axis)
    leading, last = (max(0, -steps), min(count, count - steps))
    return lax.ppermute(value, axis, [(source, source + steps) for source in range(leading, last)])


def scaled_basis(quadrature, half_width, half_span):
    tap_count = quadrature.shape[-1]
    offsets = jnp.abs(jnp.arange(tap_count, dtype=jnp.int32) - half_span)
    counts = 3.0 * (2.0 * half_width.astype(jnp.float32) + 1.0)
    factor = 1.0 / jnp.sqrt(counts)
    inside = (offsets[None, :] <= half_width[:, None]).astype(jnp.float32)
    return (quadrature * factor[:, None, None, None] * inside[:, None, None, :]).astype(
        jnp.bfloat16
    )


def band_matrix(coefficients, out_cols, span_cols):
    tap_count = coefficients.shape[-1]
    leading = coefficients.shape[:-1]
    filler = jnp.zeros(leading + (span_cols + 1 - tap_count,), coefficients.dtype)
    padded = jnp.concatenate([coefficients, filler], axis=-1)
    repeated = jnp.tile(padded, (1,) * len(leading) + (out_cols,))
    return repeated[..., : out_cols * span_cols].reshape(leading + (out_cols, span_cols))


def block_width():
    return 128


def windows(source, axis):
    pieces = [source]
    return jnp.stack(pieces, axis=axis)


def filter_rows(basis, extended):
    lat_rows = basis.shape[0]
    tap_count = basis.shape[-1]
    out_cols = extended.shape[1] - tap_count + 1
    width = block_width()
    window = width + tap_count - 1
    banded = band_matrix(basis, width, window)
    stacked = jnp.stack(
        [extended[0:lat_rows], extended[1 : lat_rows + 1], extended[2 : lat_rows + 2]], axis=1
    )
    pieces = windows(stacked, 2)
    result = jnp.einsum("arkjq,arbqc->abjkc", banded, pieces, preferred_element_type=jnp.float32)
    return result.reshape(lat_rows, out_cols, result.shape[3], result.shape[4])


def on_device(field_in, quadrature, half_width, mixing, cotangent):
    lat_rows, lon_cols, channels = field_in.shape
    kernels = mixing.shape[0]
    tap_count = quadrature.shape[-1]
    half_span = (tap_count - 1) // 2
    basis = scaled_basis(quadrature, half_width, half_span)
    widened = extended_2(field_in, (("lon", 1),), half_span, True)
    extended = extended_2(widened, (("lat", 0),), 1, False)
    filtered = filter_rows(basis, extended)
    filtered = filtered.astype(jnp.bfloat16)
    flat_filtered = filtered.reshape(lat_rows * lon_cols, kernels * channels)
    flat_mixing = mixing.reshape(kernels * channels, channels)
    field_out = (
        jnp.dot(flat_filtered, flat_mixing, preferred_element_type=jnp.float32)
        .astype(jnp.bfloat16)
        .reshape(lat_rows, lon_cols, channels)
    )
    flat_grad = cotangent.reshape(lat_rows * lon_cols, channels)
    partial_grad = lax.dot_general(
        flat_filtered, flat_grad, (((0,), (0,)), ((), ())), preferred_element_type=jnp.float32
    ).reshape(kernels, channels, channels)
    own_share = lax.psum_scatter(partial_grad, "lon", scatter_dimension=0, tiled=True)
    weight_grad = lax.psum(own_share, "lat")
    width = block_width()
    count = lon_cols // width
    window = width + tap_count - 1
    mixed_grad = lax.dot_general(
        flat_grad, flat_mixing, (((1,), (1,)), ((), ())), preferred_element_type=jnp.float32
    )
    mixed_grad = mixed_grad.astype(jnp.bfloat16).reshape(lat_rows, count, width, kernels, channels)
    banded = band_matrix(basis, width, window)
    blocks = jnp.einsum(
        "arkjq,abjkc->arbqc", banded, mixed_grad, preferred_element_type=jnp.float32
    )
    spread = blocks[:, :, 0]
    field_sum = (
        jnp.pad(spread[:, 0], ((0, 2), (0, 0), (0, 0)))
        + jnp.pad(spread[:, 1], ((1, 1), (0, 0), (0, 0)))
        + jnp.pad(spread[:, 2], ((2, 0), (0, 0), (0, 0)))
    )
    left_rim = field_sum[:, :half_span]
    right_rim = field_sum[:, half_span + lon_cols :]
    middle = field_sum[:, half_span : half_span + lon_cols]
    from_right = passed_along(left_rim.astype(jnp.bfloat16), "lon", -1).astype(left_rim.dtype)
    from_left = passed_along(right_rim.astype(jnp.bfloat16), "lon", 1).astype(right_rim.dtype)
    middle = (
        middle
        + jnp.pad(from_right, ((0, 0), (lon_cols - half_span, 0), (0, 0)))
        + jnp.pad(from_left, ((0, 0), (0, lon_cols - half_span), (0, 0)))
    )
    top_row = middle[0]
    bottom_row = middle[lat_rows + 1]
    core_rows = middle[1 : lat_rows + 1]
    from_below = from_behind(top_row, "lat", -1)
    from_above = from_behind(bottom_row, "lat", 1)
    input_sum = (
        core_rows
        + jnp.pad(from_above[None], ((0, lat_rows - 1), (0, 0), (0, 0)))
        + jnp.pad(from_below[None], ((lat_rows - 1, 0), (0, 0), (0, 0)))
    )
    input_grad = input_sum.astype(jnp.bfloat16)
    return (field_out, input_grad, weight_grad)


def solution(mesh):
    return jax.shard_map(
        on_device,
        mesh=mesh,
        in_specs=(
            P(("ens", "lat"), "lon", None),
            P("lat", None, None, None),
            P("lat"),
            P(),
            P(("ens", "lat"), "lon", None),
        ),
        out_specs=(
            P(("ens", "lat"), "lon", None),
            P(("ens", "lat"), "lon", None),
            P("lon", "ens", None),
        ),
        check_vma=False,
    )
```

profile of v0, /device:TPU:0, one launch (start us, length us, event | category | flops | bytes accessed | tf_op | source)
XLA Modules:
  0.0 211.5 jit_solution(12953288491444245854)
XLA Ops:
  7.2 0.0 copy-start
  7.2 0.0 reduce-scatter.2.cloned.1.call-start
  7.2 1.4 copy.18
  8.7 1.0 fusion.18
  9.7 3.1 %collective-permute-start = (bf16[8,64,256]{1,2,0:T(8,128)(2,1)}, bf16[8,64,256]{1,2,0:T(8,128)(2,1)S(1)}, u32[]{:S(2)}, u32[]{:S(2)}) collective-permute-start(bf16[8,64,256]{1,2,0:T(8,128)(2,1)} %get-tuple-element.16), channel_id=1, source_target_pairs={{0,1},{1,2},{2,3},{3,0},{4,5},{5,6},{6,7},{7,4},{8,9},{9,10},{10,1... | collective-permute-start | bytes 786440 | tf_op jit(solution)/shard_map/ppermute | solution.py:14
  12.7 2.0 collective-permute-start.1
  14.8 0.1 compare_convert_fusion
  14.8 0.1 multiply_convert_fusion
  15.0 6.8 %tile.4 = bf16[8,3,8,128,257]{4,3,2,1,0:T(8,128)(2,1)} broadcast(bf16[8,3,8,257]{3,2,1,0:T(8,128)(2,1)S(1)} %concatenate.17), dimensions={0,1,2,4} | broadcast | bytes 12730752 | tf_op jit(solution)/shard_map/tile | solution.py:48
  21.8 29.5 %tile.5 = bf16[8,3,8,32896]{3,2,1,0:T(8,128)(2,1)} reshape(bf16[8,3,8,128,257]{4,3,2,1,0:T(8,128)(2,1)} %tile.4) | data formatting | bytes 25264128 | tf_op jit(solution)/shard_map/tile | solution.py:48
  51.3 6.1 %slice.73 = bf16[8,3,8,32768]{3,2,1,0:T(8,128)(2,1)S(1)} slice(bf16[8,3,8,32896]{3,2,1,0:T(8,128)(2,1)} %tile.5), slice={[0:8], [0:3], [0:8], [0:32768]} | slice | bytes 25165824 | tf_op jit(solution)/shard_map/slice | solution.py:49
  57.4 8.2 %copy.41 = bf16[24,8,128,256]{3,2,1,0:T(8,128)(2,1)} copy(bf16[24,8,128,256]{3,1,2,0:T(8,128)(2,1)S(1)} %bitcast.98) | data formatting | bytes 25165824
  65.7 0.1 copy-done.1
  65.7 0.0 collective-permute-done
  65.7 0.0 collective-permute-done.1
  65.7 0.6 pad_maximum_fusion.6
  66.4 1.5 collective-permute-start.2
  67.9 1.3 collective-permute-start.3
  69.2 0.6 fusion.28
  69.8 0.0 collective-permute-done.2
  69.8 3.1 %collective-permute-done.3 = bf16[1,256,256]{1,2,0:T(8,128)(2,1)S(1)} collective-permute-done((bf16[1,256,256]{1,2,0:T(8,128)(2,1)S(1)}, bf16[1,256,256]{1,2,0:T(8,128)(2,1)S(1)}, u32[]{:S(2)}, u32[]{:S(2)}) %collective-permute-start.3) | collective-permute-done | bytes 131104 | tf_op jit(solution)/shard_map/ppermute | solution.py:15
  72.9 2.2 %fusion.13 = (bf16[8,1,256,256]{2,3,1,0:T(8,128)(2,1)}, bf16[8,1,256,256]{2,3,1,0:T(8,128)(2,1)}) fusion(bf16[1,256,256]{1,2,0:T(8,128)(2,1)S(1)} %collective-permute-done.2, bf16[8,64,256]{1,2,0:T(8,128)(2,1)S(1)} %collective-permute-done.1, bf16[8,128,256]{1,2,0:T(8,128)(2,1)S(1)} %copy.18, bf16[8,64,256]{1,2,0:T(8,128)(2,1)S(1)} %collective-permute-done, ...), kind=kLoop, calls=%fused_computation.27 | loop fusion | flops 8388608 | bytes 3407872 | tf_op jit(solution)/shard_map/stack | solution.py:68
  75.1 8.5 %fusion = bf16[8,1,128,8,256]{2,4,3,0,1:T(8,128)(2,1)} fusion(bf16[8,3,8,128,256]{4,3,2,1,0:T(8,128)(2,1)} %bitcast.105, bf16[8,1,256,256]{2,3,1,0:T(8,128)(2,1)} %get-tuple-element.9, bf16[8,1,256,256]{2,3,1,0:T(8,128)(2,1)S(1)} %fusion.28, bf16[8,1,256,256]{2,3,1,0:T(8,128)(2,1)} %get-tuple-element.8), kind=kOutput, calls=%fused_computation.1 | convolution fusion | flops 3232759808 | bytes 19922944 | tf_op jit(solution)/shard_map/arkjq,arbqc->abjkc/dot_general | solution.py:72
  83.5 6.8 %copy.24 = bf16[8,1,128,8,256]{4,3,2,0,1:T(8,128)(2,1)} copy(bf16[8,1,128,8,256]{2,4,3,0,1:T(8,128)(2,1)} %fusion) | data formatting | bytes 8388608 | tf_op jit(solution)/shard_map/convert_element_type | solution.py:85
  90.3 5.7 %copy.42 = bf16[128,8,8,256]{3,1,2,0:T(8,128)(2,1)} copy(bf16[128,8,8,256]{3,2,1,0:T(8,128)(2,1)} %bitcast.104) | data formatting | bytes 8388608
  96.0 6.4 %copy.38 = bf16[2048,1024]{1,0:T(8,128)(2,1)} copy(bf16[2048,1024]{0,1:T(8,128)(2,1)} %bitcast.102) | data formatting | bytes 8388608 | tf_op jit(solution)/shard_map/dot_general | solution.py:94
  102.5 4.8 %fusion.19 = f32[8,256,256]{2,1,0:T(8,128)} fusion(bf16[8,256,1024]{2,1,0:T(8,128)(2,1)} %bitcast.106, bf16[1024,256,1]{1,0,2:T(8,128)(2,1)S(1)} %bitcast.107), kind=kOutput, calls=%fused_computation.42 | convolution fusion | flops 1073741824 | bytes 6815744 | tf_op jit(solution)/shard_map/dot_general | solution.py:94
  107.2 0.0 reduce-scatter.2.cloned.1.call-update
  107.3 0.2 all-reduce.10.cloned.1.call-start
  107.5 1.3 convolution_convert_fusion
  108.8 3.5 %copy.43 = bf16[128,8,8,256]{3,2,1,0:T(8,128)(2,1)} copy(bf16[128,8,8,256]{3,1,2,0:T(8,128)(2,1)S(1)} %bitcast.100) | data formatting | bytes 8388608
  112.3 12.7 %fusion.8 = f32[8,3,256,256]{3,2,1,0:T(8,128)} fusion(bf16[8,3,8,128,256]{4,2,3,1,0:T(8,128)(2,1)} %bitcast.99, bf16[8,128,8,256]{3,2,1,0:T(8,128)(2,1)} %bitcast.101), kind=kOutput, calls=%fused_computation.11 | convolution fusion | flops 3221225472 | bytes 23068672 | tf_op jit(solution)/shard_map/arkjq,abjkc->arbqc/dot_general | solution.py:107
  125.0 3.5 %slice_bitcast_fusion.2 = (f32[8,256,256]{2,1,0:T(8,128)S(1)}, f32[8,256,256]{2,1,0:T(8,128)S(1)}, f32[8,256,256]{2,1,0:T(8,128)S(1)}) fusion(f32[8,3,256,256]{3,2,1,0:T(8,128)} %fusion.8), kind=kLoop, calls=%fused_computation.15 | loop fusion | bytes 12582912 | tf_op jit(solution)/shard_map/squeeze | solution.py:112
  128.6 0.6 fusion.15
  129.2 0.1 fusion.16
  129.2 1.8 collective-permute-start.4
  131.1 0.2 collective-permute-start.5
  131.3 27.8 %collective-permute-done.4 = bf16[10,64,256]{2,1,0:T(8,128)(2,1)S(1)} collective-permute-done((bf16[10,64,256]{2,1,0:T(8,128)(2,1)S(1)}, bf16[10,64,256]{2,1,0:T(8,128)(2,1)S(1)}, u32[]{:S(2)}, u32[]{:S(2)}) %collective-permute-start.4) | collective-permute-done | bytes 327712 | tf_op jit(solution)/shard_map/ppermute | solution.py:23
  159.2 1.4 collective-permute-done.5
  160.5 0.1 fusion.9
  160.7 4.6 %collective-permute-start.6 = (f32[128,256]{1,0:T(8,128)S(1)}, f32[128,256]{1,0:T(8,128)S(1)}, u32[]{:S(2)}, u32[]{:S(2)}) collective-permute-start(f32[128,256]{1,0:T(8,128)S(1)} %get-tuple-element.10), channel_id=1, source_target_pairs={{0,4},{4,8},{8,12},{1,5},{5,9},{9,13},{2,6},{6,10},{10,14},{3,7},{... | collective-permute-start | bytes 393224 | tf_op jit(solution)/shard_map/ppermute | solution.py:29
  165.3 1.3 collective-permute-start.7
  166.6 2.1 convolution_convert_fusion.1
  168.7 0.0 all-reduce.10.cloned.1.call-update
  168.7 0.6 collective-permute-done.7
  169.3 0.9 fusion.11
  170.2 32.6 %all-reduce.10.cloned.1.call-done = f32[2,256,256]{2,1,0:T(8,128)} async-done(((f32[2,256,256]{2,1,0:T(8,128)}), f32[2,256,256]{2,1,0:T(8,128)}) %all-reduce.10.cloned.1.call-update) | async-done | bytes 524304 | tf_op jit(solution)/shard_map/psum | solution.py:98
  202.8 1.9 copy.45
  (17 shorter events, 0.1 us)
Async XLA Ops:
  7.2 100.3 %copy-start = (bf16[8,256,256]{2,1,0:T(8,128)(2,1)S(1)}, bf16[8,256,256]{2,1,0:T(8,128)(2,1)}, u32[]{:S(2)}) copy-start(bf16[8,256,256]{2,1,0:T(8,128)(2,1)} %param.8) | copy-start | bytes 3145732
  7.2 7.6 %copy-start.5 = (s32[8]{0:T(128)S(1)}, s32[8]{0:T(128)}, u32[]{:S(2)}) copy-start(s32[8]{0:T(128)} %param.7) | copy-start | bytes 100
  7.2 7.7 %copy-start.4 = (f32[8,3,8,129]{3,2,1,0:T(8,128)S(1)}, f32[8,3,8,129]{3,2,1,0:T(8,128)}, u32[]{:S(2)}) copy-start(f32[8,3,8,129]{3,2,1,0:T(8,128)} %param.6) | copy-start | bytes 297220
  7.2 161.5 %reduce-scatter.2.cloned.1.call-start = ((), (), s32[]{:S(2)}) async-start(), calls=%async_computation.1 | async-start | bytes 2621440 | tf_op jit(solution)/shard_map/reduce_scatter | solution.py:97
  9.7 56.0 %collective-permute-start = (bf16[8,64,256]{1,2,0:T(8,128)(2,1)}, bf16[8,64,256]{1,2,0:T(8,128)(2,1)S(1)}, u32[]{:S(2)}, u32[]{:S(2)}) collective-permute-start(bf16[8,64,256]{1,2,0:T(8,128)(2,1)} %get-tuple-element.16), channel_id=1, source_target_pairs={{0,1},{1,2},{2,3},{3,0},{4,5},{5,6},{6,7},{7,4},{8,9},{9,10},{10,1... | collective-permute-start | bytes 786440 | tf_op jit(solution)/shard_map/ppermute | solution.py:14
  12.7 53.0 %collective-permute-start.1 = (bf16[8,64,256]{1,2,0:T(8,128)(2,1)S(1)}, bf16[8,64,256]{1,2,0:T(8,128)(2,1)S(1)}, u32[]{:S(2)}, u32[]{:S(2)}) collective-permute-start(bf16[8,64,256]{1,2,0:T(8,128)(2,1)S(1)} %get-tuple-element.17), channel_id=1, source_target_pairs={{1,0},{2,1},{3,2},{0,3},{5,4},{6,5},{7,6},{4,7},{9,8},{10,9},{11,1... | collective-permute-start | bytes 786440 | tf_op jit(solution)/shard_map/ppermute | solution.py:15
  57.4 8.3 %copy-start.1 = (bf16[8,3,8,32768]{3,2,1,0:T(8,128)(2,1)}, bf16[8,3,8,32768]{3,2,1,0:T(8,128)(2,1)S(1)}, u32[]{:S(2)}) copy-start(bf16[8,3,8,32768]{3,2,1,0:T(8,128)(2,1)S(1)} %slice.73) | copy-start | bytes 37748740
  66.4 3.4 %collective-permute-start.2 = (bf16[1,256,256]{1,2,0:T(8,128)(2,1)S(1)}, bf16[1,256,256]{1,2,0:T(8,128)(2,1)S(1)}, u32[]{:S(2)}, u32[]{:S(2)}) collective-permute-start(bf16[1,256,256]{1,2,0:T(8,128)(2,1)S(1)} %get-tuple-element.14), channel_id=1, source_target_pairs={{0,4},{4,8},{8,12},{1,5},{5,9},{9,13},{2,6},{6,10},{10,14},{3,7},{... | collective-permute-start | bytes 393224 | tf_op jit(solution)/shard_map/ppermute | solution.py:14
  67.9 5.0 %collective-permute-start.3 = (bf16[1,256,256]{1,2,0:T(8,128)(2,1)S(1)}, bf16[1,256,256]{1,2,0:T(8,128)(2,1)S(1)}, u32[]{:S(2)}, u32[]{:S(2)}) collective-permute-start(bf16[1,256,256]{1,2,0:T(8,128)(2,1)S(1)} %get-tuple-element.15), channel_id=1, source_target_pairs={{4,0},{8,4},{12,8},{5,1},{9,5},{13,9},{6,2},{10,6},{14,10},{7,3},{... | collective-permute-start | bytes 393224 | tf_op jit(solution)/shard_map/ppermute | solution.py:15
  96.0 6.4 %copy-start.3 = (bf16[8,128,256]{2,1,0:T(8,128)(2,1)S(1)}, bf16[8,128,256]{2,1,0:T(8,128)(2,1)}, u32[]{:S(2)}) copy-start(bf16[8,128,256]{2,1,0:T(8,128)(2,1)} %param.9) | copy-start | bytes 1572868
  107.3 95.5 %all-reduce.10.cloned.1.call-start = ((), (), s32[]{:S(2)}) async-start(), calls=%async_computation.2 | async-start | bytes 1048576 | tf_op jit(solution)/shard_map/psum | solution.py:98
  129.2 37.4 %copy-start.2 = (bf16[128,8,8,256]{3,1,2,0:T(8,128)(2,1)S(1)}, bf16[128,8,8,256]{3,1,2,0:T(8,128)(2,1)}, u32[]{:S(2)}) copy-start(bf16[128,8,8,256]{3,1,2,0:T(8,128)(2,1)} %copy.42) | copy-start | bytes 12582916
  129.2 29.9 %collective-permute-start.4 = (bf16[10,64,256]{2,1,0:T(8,128)(2,1)S(1)}, bf16[10,64,256]{2,1,0:T(8,128)(2,1)S(1)}, u32[]{:S(2)}, u32[]{:S(2)}) collective-permute-start(bf16[10,64,256]{2,1,0:T(8,128)(2,1)S(1)} %get-tuple-element.12), channel_id=1, source_target_pairs={{1,0},{2,1},{3,2},{0,3},{5,4},{6,5},{7,6},{4,7},{9,8},{10,9},{11,1... | collective-permute-start | bytes 983048 | tf_op jit(solution)/shard_map/ppermute | solution.py:23
  131.1 29.4 %collective-permute-start.5 = (bf16[10,64,256]{2,1,0:T(8,128)(2,1)S(1)}, bf16[10,64,256]{2,1,0:T(8,128)(2,1)S(1)}, u32[]{:S(2)}, u32[]{:S(2)}) collective-permute-start(bf16[10,64,256]{2,1,0:T(8,128)(2,1)S(1)} %get-tuple-element.13), channel_id=1, source_target_pairs={{3,0},{0,1},{1,2},{2,3},{7,4},{4,5},{5,6},{6,7},{11,8},{8,9},{9,10... | collective-permute-start | bytes 983048 | tf_op jit(solution)/shard_map/ppermute | solution.py:23
  160.7 8.0 %collective-permute-start.6 = (f32[128,256]{1,0:T(8,128)S(1)}, f32[128,256]{1,0:T(8,128)S(1)}, u32[]{:S(2)}, u32[]{:S(2)}) collective-permute-start(f32[128,256]{1,0:T(8,128)S(1)} %get-tuple-element.10), channel_id=1, source_target_pairs={{0,4},{4,8},{8,12},{1,5},{5,9},{9,13},{2,6},{6,10},{10,14},{3,7},{... | collective-permute-start | bytes 393224 | tf_op jit(solution)/shard_map/ppermute | solution.py:29
  165.3 4.0 %collective-permute-start.7 = (f32[128,256]{1,0:T(8,128)S(1)}, f32[128,256]{1,0:T(8,128)S(1)}, u32[]{:S(2)}, u32[]{:S(2)}) collective-permute-start(f32[128,256]{1,0:T(8,128)S(1)} %get-tuple-element.11), channel_id=1, source_target_pairs={{4,0},{8,4},{12,8},{5,1},{9,5},{13,9},{6,2},{10,6},{14,10},{7,3},{... | collective-permute-start | bytes 393224 | tf_op jit(solution)/shard_map/ppermute | solution.py:29
Sparse Core Ops, SparseCore 0:
  107.4 59.3 reduce-scatter.1
  169.1 33.6 all-reduce.9
where the time goes:
time: 213 us; the launch traced here: 211 us
  local copies, waits for them, and re-layouts  81.1 us (38%)
  waiting for transfers between devices  65.6 us (31%)
  matrix products  29.3 us (14%)
  starting transfers between devices  16.1 us (8%)
  between operations  14.2 us (7%)
  other arithmetic  5.18 us (2%)
    another operation x2, local copies, waits for them, and re-layouts, band_matrix(): repeated = jnp.tile(padded, (1,) * len(leading) + (out_cols,))  36.3 us
    psum x1, waiting for transfers between devices, on_device(): weight_grad = lax.psum(own_share, 'lat')  32.6 us
    ppermute x2, waiting for transfers between devices, passed_along(): return lax.ppermute(block, axis, route)  29.2 us
    unnamed x17, local copies, waits for them, and re-layouts  20.8 us
    dot_general x1, matrix products, on_device(): jnp.einsum('arkjq,abjkc->arbqc', banded, mixed_grad, preferred_element_ty...  12.7 us
    dot_general x1, matrix products, filter_rows(): jnp.einsum('arkjq,arbqc->abjkc', banded, pieces, preferred_element_type=j...  8.48 us
    convert_element_type x1, local copies, waits for them, and re-layouts, on_device(): filtered = filtered.astype(jnp.bfloat16)  6.78 us
    dot_general x1, local copies, waits for them, and re-layouts, on_device(): lax.dot_general(flat_filtered, flat_grad, (((0,), (0,)), ((), ())), prefe...  6.44 us
  transfers between devices with their start and end apart: 10, of which 5 were waited for; matrix products, arithmetic and copies ran while one was open for 36% of the time, Pallas kernels for 0%

commit v1 on v0

v1 whole, which is shorter than its diff:
```python
import functools

import jax
import jax.numpy as jnp
from jax import lax
from jax.experimental import pallas as pl
from jax.experimental.pallas import tpu as pltpu
from jax.sharding import PartitionSpec as P


BLOCK = 32
LANES = 128
DEPTH = 256


def ring(axis, distance):
    count = lax.axis_size(axis)
    return [(i, (i + distance) % count) for i in range(count)]


def line(axis, distance):
    count = lax.axis_size(axis)
    return [(i, i + distance) for i in range(count) if 0 <= i + distance < count]


def swap(axis, mask):
    return [(i, i ^ mask) for i in range(lax.axis_size(axis))]


IN_VMEM = pl.BlockSpec(memory_space=pltpu.VMEM)
IN_SMEM = pl.BlockSpec(memory_space=pltpu.SMEM)
IN_HBM = pl.BlockSpec(memory_space=pltpu.HBM)


def near(array):
    return pltpu.with_memory_space_constraint(array, pltpu.VMEM)


def kernel_call(body, operands, outs, scratch, mib, scalars=0, far=(), far_out=False, alias=None):
    specs = [IN_SMEM] * scalars
    given = list(operands[:scalars])
    for i, operand in enumerate(operands[scalars:], scalars):
        specs.append(IN_HBM if i in far else IN_VMEM)
        given.append(operand if i in far else near(operand))
    single = not isinstance(outs, list)
    place = IN_HBM if far_out else IN_VMEM
    return pl.pallas_call(
        body,
        in_specs=specs,
        out_specs=place if single else [place] * len(outs),
        out_shape=outs,
        scratch_shapes=scratch,
        input_output_aliases=alias or {},
        compiler_params=pltpu.CompilerParams(vmem_limit_bytes=mib << 20),
    )(*given)


def packed_taps(pieces, window, total):
    kernels = pieces[0].shape[0]
    packed = None
    for r, piece in enumerate(pieces):
        wide = jnp.concatenate([piece, jnp.zeros((kernels, total - piece.shape[1]), piece.dtype)], 1)
        wide = pltpu.roll(wide, r * window, 1) if r else wide
        packed = wide if packed is None else packed + wide
    return packed


def spread_bands(packed, bands, row):
    kernels, total = packed.shape
    for k in range(kernels):
        rows = jnp.broadcast_to(packed[k : k + 1, :], (BLOCK, total))
        rolled = pltpu.roll(rows, 0, 1, stride=1, stride_axis=0)
        bands[row, k * BLOCK : (k + 1) * BLOCK, :] = rolled.astype(bands.dtype)


def bands_kernel(half_width, quadrature, bands, edges):
    rows, three, kernels, taps = quadrature.shape
    window = taps - 1 + BLOCK
    middle = (taps - 1) // 2
    lane = lax.broadcasted_iota(jnp.int32, (kernels, LANES), 1)
    for row in range(rows):
        reach = jnp.full((kernels, LANES), half_width[row], jnp.int32)
        factor = 1.0 / jnp.sqrt(3.0 * (2.0 * reach.astype(jnp.float32) + 1.0))
        head_inside = (jnp.abs(lane - middle) <= reach).astype(jnp.float32)
        tail_inside = ((lane < taps - LANES) & (lane + LANES - middle <= reach)).astype(
            jnp.float32
        )
        pieces = []
        for r in range(three):
            head = quadrature[row, r, :, 0:LANES] * factor * head_inside
            last = jnp.broadcast_to(quadrature[row, r, :, LANES:taps], (kernels, LANES))
            tail = last * factor * tail_inside
            piece = jnp.concatenate([head, tail], axis=1).astype(jnp.bfloat16)
            if row == rows - 1 and r == three - 1:
                edges[0] = piece
            if row == 0 and r == 0:
                edges[1] = piece
            pieces.append(piece.astype(jnp.float32))
        spread_bands(packed_taps(pieces, window, bands.shape[2]), bands, row)


def band_matrices(half_width, quadrature):
    rows, three, kernels, taps = quadrature.shape
    total = -(-three * (taps - 1 + BLOCK) // DEPTH) * DEPTH
    return kernel_call(
        bands_kernel,
        [half_width, quadrature],
        [
            pltpu.VMEM((rows, kernels * BLOCK, total), jnp.bfloat16),
            pltpu.VMEM((2, kernels, 2 * LANES), jnp.bfloat16),
        ],
        [],
        8,
        scalars=1,
    )


def split_rows(rows):
    part = max(1, rows // 4)
    outer = list(range(part)) + list(range(rows - part, rows))
    return outer, list(range(part, rows - part))


def rims_kernel(groups, array, *refs):
    *outs, edges, sems = refs
    rows, cols = array.shape[0], array.shape[1]
    rim = outs[0].shape[1]
    copies = []
    for g, group in enumerate(groups):
        place = 0
        while place < len(group):
            size = 1
            while place + size < len(group) and group[place + size] == group[place] + size:
                size += 1
            source = array.at[pl.ds(group[place], size)]
            for side, first in ((0, cols - rim), (1, 0)):
                copies.append(
                    (
                        source.at[:, pl.ds(first, rim), :],
                        outs[2 * g + side].at[pl.ds(place, size)],
                    )
                )
            place += size
    copies.append((array.at[0], edges.at[0]))
    copies.append((array.at[rows - 1], edges.at[1]))
    copies = [pltpu.make_async_copy(*c, sems.at[i]) for i, c in enumerate(copies)]
    for copy in copies:
        copy.start()
    for copy in copies:
        copy.wait()


def rims(array, rim, groups):
    _, cols, chans = array.shape
    outs = [
        pltpu.VMEM((len(group), rim, chans), jnp.bfloat16) for group in groups for _ in range(2)
    ]
    outs.append(pltpu.VMEM((2, cols, chans), jnp.bfloat16))
    return kernel_call(
        functools.partial(rims_kernel, groups),
        [array],
        outs,
        [pltpu.SemaphoreType.DMA((16,))],
        4,
        far=(0,),
    )


def edges_kernel(picks, own, left, right, *rest):
    *basis, bottom_row, top_row = rest
    rim, cols = left.shape[1], own.shape[1]
    for i, out in ((1, bottom_row), (0, top_row)):
        out[0:rim] = left[picks[i]]
        out[rim : rim + cols] = own[i]
        out[rim + cols : 2 * rim + cols] = right[picks[i]]
        if basis:
            out[2 * rim + cols :] = basis[0][1 - i]


def edge_rows(own, left, right, picks, basis):
    _, cols, chans = own.shape
    span = cols + 2 * left.shape[1] + (basis[0].shape[1] if basis else 0)
    outs = [pltpu.VMEM((span, chans), jnp.bfloat16)] * 2
    return kernel_call(
        functools.partial(edges_kernel, picks), [own, left, right, *basis], outs, [], 4
    )


def fill_extended(ext, own, top, bottom, groups, sides):
    rows, cols = own.shape[0], own.shape[1]
    rim = sides[0].shape[1]
    span = ext.shape[1]
    ext[0] = top[0:span]
    ext[rows + 1] = bottom[0:span]
    ext[1 : rows + 1, rim : rim + cols, :] = own[...]
    for g, group in enumerate(groups):
        for i, row in enumerate(group):
            ext[row + 1, 0:rim, :] = sides[2 * g][i]
            ext[row + 1, rim + cols :, :] = sides[2 * g + 1][i]


def filter_rows(bands, ext, cols, write):
    rows, height, total = bands.shape
    reach = ext.shape[1] - cols + BLOCK
    spare = total - 3 * reach

    def one(row, carry):
        for g in range(cols // BLOCK):
            first = g * BLOCK
            pieces = [ext[row + r, first : first + reach, :] for r in range(3)]
            if spare:
                pieces.append(ext[row, 0:spare, :])
            source = jnp.concatenate(pieces, axis=0)
            result = jnp.dot(bands[row], source, preferred_element_type=jnp.float32)
            result = result.astype(jnp.bfloat16)
            start = pl.multiple_of(row * cols + first, BLOCK)
            for k in range(height // BLOCK):
                write(start, k, result[k * BLOCK : (k + 1) * BLOCK])
        return carry

    lax.fori_loop(0, rows, one, 0)


def forward_kernel(n_lat, groups, ids, bands, own, top, bottom, cot, *rest):
    *sides, filt, keep, send, ext, grad = rest
    _, cols, chans = own.shape
    kernels = grad.shape[0]
    fill_extended(ext, own, top, bottom, groups, sides)

    def write(start, k, value):
        filt[pl.ds(start, BLOCK), k * chans : (k + 1) * chans] = value

    filter_rows(bands, ext, cols, write)
    for k in range(kernels):
        grad[k] = lax.dot_general(
            filt[:, k * chans : (k + 1) * chans],
            cot[...],
            (((0,), (0,)), ((), ())),
            preferred_element_type=jnp.float32,
        )
    lat, lon = ids[0], ids[1]
    n_lon, share, piece = keep.shape[1], keep.shape[2], keep.shape[3]
    bits = n_lat.bit_length() - 1
    for m in range(n_lat):
        slot = sum(((m >> b) & 1) << (bits - 1 - b) for b in range(bits))
        start = pl.multiple_of((lat ^ slot) * piece, piece)
        for s in range(n_lon):
            first = lax.rem(lon + s, n_lon) * share
            value = grad[pl.ds(first, share), pl.ds(start, piece), :]
            if m < n_lat // 2:
                keep[m, s] = value
            else:
                send[m - n_lat // 2, s] = value.astype(send.dtype)


def forward(ids, bands, own, top, bottom, cot, groups, sides, kernels, n_lat, n_lon):
    rows, cols, chans = own.shape
    rim = sides[0].shape[1]
    parts = (n_lat // 2, n_lon, kernels // n_lon, chans // n_lat, chans)
    return kernel_call(
        functools.partial(forward_kernel, n_lat, groups),
        [ids, bands, own, top, bottom, cot, *sides],
        [
            pltpu.VMEM((rows * cols, kernels * chans), jnp.bfloat16),
            pltpu.VMEM(parts, jnp.float32),
            pltpu.VMEM(parts, jnp.bfloat16),
        ],
        [
            pltpu.VMEM((rows + 2, cols + 2 * rim, chans), jnp.bfloat16),
            pltpu.VMEM((kernels, chans, chans), jnp.float32),
        ],
        20,
        scalars=1,
    )


def mix_kernel(filt, mixing, out):
    out[...] = jnp.dot(filt[...], mixing[...], preferred_element_type=jnp.float32).astype(out.dtype)


def mirror(size):
    across = lax.broadcasted_iota(jnp.int32, (size, size), 0)
    down = lax.broadcasted_iota(jnp.int32, (size, size), 1)
    return (across + down == size - 1).astype(jnp.float32).astype(jnp.bfloat16)


def adjoint_band(window, above, here, below):
    total = here.shape[1]
    sources = [below, here, above]
    lane = lax.broadcasted_iota(jnp.int32, (here.shape[0], LANES), 1)
    tiles = []
    for first in range(0, total, LANES):
        r = min(first // window, 2)
        tile = sources[r][:, first : first + LANES]
        cut = (r + 1) * window - first
        if r < 2 and cut < LANES:
            following = sources[r + 1][:, first : first + LANES]
            tile = jnp.where(lane < cut, tile, following)
        tiles.append(tile)
    return jnp.concatenate(tiles, axis=1)


def adjoint_row(band, reversed_rows, cols, write):
    span = reversed_rows[0].shape[0]
    reach = span - cols + BLOCK
    spare = band.shape[1] - 3 * reach
    for g in range(cols // BLOCK):
        first = g * BLOCK
        pieces = [source[first : first + reach, :] for source in reversed_rows]
        if spare:
            pieces.append(reversed_rows[0][0:spare, :])
        result = jnp.dot(
            band, jnp.concatenate(pieces, axis=0), preferred_element_type=jnp.float32
        ).astype(jnp.bfloat16)
        for k in range(result.shape[0] // BLOCK):
            write(first, k, result[k * BLOCK : (k + 1) * BLOCK])


def mixed_back(filt, mixing, stage, cols):
    kernels = mixing.shape[0]
    total = None
    for k in range(kernels):
        term = lax.dot_general(
            filt[k], mixing[k], (((1,), (1,)), ((), ())), preferred_element_type=jnp.float32
        )
        total = term if total is None else total + term
    total = total.astype(jnp.bfloat16)
    flip = mirror(cols)
    for i in range(stage.shape[0]):
        row = jnp.dot(flip, total[i * cols : (i + 1) * cols], preferred_element_type=jnp.float32)
        stage[i] = row.astype(stage.dtype)


def backward_inner_kernel(window, bands, own, mixing, left, right, out, reverse, filt, stage, sem):
    rows, cols, _ = own.shape
    flip = mirror(reverse.shape[1])

    def turn(row, carry):
        line = jnp.concatenate([left[row], own[row], right[row]], axis=0)
        reverse[row] = jnp.dot(flip, line, preferred_element_type=jnp.float32).astype(
            reverse.dtype
        )
        return carry

    lax.fori_loop(0, rows, turn, 0)

    def one(step, carry):
        row = step + 1
        band = adjoint_band(window, bands[row - 1], bands[row], bands[row + 1])
        base = step * cols

        def write(first, k, value):
            filt[k, pl.ds(pl.multiple_of(base + first, BLOCK), BLOCK), :] = value

        lines = [reverse.at[row + 1], reverse.at[row], reverse.at[row - 1]]
        adjoint_row(band, lines, cols, write)
        return carry

    lax.fori_loop(0, rows - 2, one, 0)
    mixed_back(filt, mixing, stage, cols)
    copy = pltpu.make_async_copy(stage, out.at[pl.ds(1, rows - 2)], sem)
    copy.start()
    copy.wait()


def backward_inner(bands, own, mixing, left, right, window):
    rows, cols, outs = own.shape
    span = cols + 2 * left.shape[1]
    kernels, chans, _ = mixing.shape
    return kernel_call(
        functools.partial(backward_inner_kernel, window),
        [bands, own, mixing, left, right],
        jax.ShapeDtypeStruct((rows, cols, chans), jnp.bfloat16),
        [
            pltpu.VMEM((rows, span, outs), jnp.bfloat16),
            pltpu.VMEM((kernels, (rows - 2) * cols, outs), jnp.bfloat16),
            pltpu.VMEM((rows - 2, cols, chans), jnp.bfloat16),
            pltpu.SemaphoreType.DMA(()),
        ],
        16,
        far_out=True,
    )


def backward_edges_kernel(
    window, bands, top, bottom, mixing, left, right, edges, given, out,
    reverse, extra, filt, stage, sems
):
    rows = bands.shape[0]
    cols = stage.shape[1]
    span = reverse.shape[1]
    flip = mirror(span)
    lines = [top[0:span]]
    for i, row in enumerate((0, 1, rows - 2, rows - 1)):
        lines.append(jnp.concatenate([left[row], edges[i], right[row]], axis=0))
    lines.append(bottom[0:span])
    for i, line in enumerate(lines):
        reverse[i] = jnp.dot(flip, line, preferred_element_type=jnp.float32).astype(reverse.dtype)
    none = jnp.zeros((top.shape[0] - span, 2 * LANES), jnp.float32)
    above = top[span:, :].astype(jnp.float32)
    below = bottom[span:, :].astype(jnp.float32)
    spread_bands(packed_taps([none, none, above], window, bands.shape[2]), extra, 0)
    spread_bands(packed_taps([below, none, none], window, bands.shape[2]), extra, 1)
    picks = (
        (extra[0], bands[0], bands[1], 1),
        (bands[rows - 2], bands[rows - 1], extra[1], 4),
    )
    for i, (one, two, three, at) in enumerate(picks):
        band = adjoint_band(window, one, two, three)

        def write(first, k, value, base=i * cols):
            filt[k, base + first : base + first + BLOCK, :] = value

        adjoint_row(band, [reverse.at[at + 1], reverse.at[at], reverse.at[at - 1]], cols, write)
    mixed_back(filt, mixing, stage, cols)
    copies = [
        pltpu.make_async_copy(stage.at[i], out.at[row], sems.at[i])
        for i, row in enumerate((0, rows - 1))
    ]
    for copy in copies:
        copy.start()
    for copy in copies:
        copy.wait()


def backward_edges(bands, top, bottom, mixing, left, right, edges, given, window):
    _, cols, chans = given.shape
    span = cols + 2 * left.shape[1]
    kernels, _, outs = mixing.shape
    return kernel_call(
        functools.partial(backward_edges_kernel, window),
        [bands, top, bottom, mixing, left, right, edges, given],
        jax.ShapeDtypeStruct(given.shape, given.dtype),
        [
            pltpu.VMEM((6, span, outs), jnp.bfloat16),
            pltpu.VMEM((2,) + bands.shape[1:], jnp.bfloat16),
            pltpu.VMEM((kernels, 2 * cols, outs), jnp.bfloat16),
            pltpu.VMEM((2, cols, chans), jnp.bfloat16),
            pltpu.SemaphoreType.DMA((2,)),
        ],
        16,
        far=(7,),
        far_out=True,
        alias={7: 0},
    )


def assemble_kernel(ids, mine, other, out):
    half, _, piece, _ = mine.shape
    count = 2 * half
    bits = count.bit_length() - 1
    for slot in range(count):
        m = sum(((slot >> b) & 1) << (bits - 1 - b) for b in range(bits))
        source = mine[m] if m < half else other[m - half]
        start = pl.multiple_of((ids[0] ^ slot) * piece, piece)
        out[:, pl.ds(start, piece), :] = source.astype(out.dtype)


def assemble(ids, mine, other):
    half, share, piece, chans = mine.shape
    return kernel_call(
        assemble_kernel,
        [ids, mine, other],
        jax.ShapeDtypeStruct((share, 2 * half * piece, chans), jnp.float32),
        [],
        4,
        scalars=1,
    )


def reduced_gradient(ids, keep, send):
    n_lat, n_lon = lax.axis_size("lat"), lax.axis_size("lon")
    mask = 1
    while True:
        other = lax.ppermute(send, "lat", swap("lat", mask))
        total = keep + other.astype(jnp.float32)
        mask *= 2
        if mask >= n_lat:
            break
        half = total.shape[0] // 2
        keep, send = total[:half], total[half:].astype(jnp.bfloat16)
    total = total[0]
    wire = total.astype(jnp.bfloat16)
    piece = total[0]
    for s in range(1, n_lon):
        other = lax.ppermute(wire[s], "lon", ring("lon", s))
        piece = piece + other.astype(jnp.float32)
    pieces = piece.astype(jnp.bfloat16)[None]
    while mask > 1:
        mask //= 2
        other = lax.ppermute(pieces, "lat", swap("lat", mask))
        if mask > 1:
            pieces = jnp.concatenate([pieces, other], axis=0)
    return assemble(ids, pieces, other)


def on_device(field_in, quadrature, half_width, mixing, cotangent):
    rows, cols, chans = field_in.shape
    kernels, _, outs = mixing.shape
    taps = quadrature.shape[-1]
    rim = (taps - 1) // 2
    n_lat, n_lon = lax.axis_size("lat"), lax.axis_size("lon")
    ids = jnp.stack([lax.axis_index("lat"), lax.axis_index("lon")]).astype(jnp.int32)
    groups = split_rows(rows)
    outer = groups[0]

    def beside(pair):
        left = lax.ppermute(pair[0], "lon", ring("lon", 1))
        right = lax.ppermute(pair[1], "lon", ring("lon", -1))
        return [left, right]

    def bands_beside(pair):
        top = lax.ppermute(pair[0], "lat", line("lat", 1))
        bottom = lax.ppermute(pair[1], "lat", line("lat", -1))
        return top, bottom

    window = taps - 1 + BLOCK
    *sides, own_edges = rims(field_in, rim, groups)
    outer_sides = beside(sides[0:2])
    inner_sides = beside(sides[2:4])
    bands, basis_edges = band_matrices(half_width, quadrature)
    picks = (0, len(outer) - 1)
    sent = edge_rows(own_edges, *outer_sides, picks, [])
    f_top, f_bottom = bands_beside(sent)
    *sides, cot_edges = rims(cotangent, rim, [range(rows)])
    g_left, g_right = beside(sides)

    filtered, keep, send = forward(
        ids,
        bands,
        field_in,
        f_top,
        f_bottom,
        cotangent.reshape(rows * cols, outs),
        groups,
        outer_sides + inner_sides,
        kernels,
        n_lat,
        n_lon,
    )
    weight_grad = reduced_gradient(ids, keep, send)
    field_out = kernel_call(
        mix_kernel,
        [filtered, mixing.reshape(kernels * chans, outs)],
        jax.ShapeDtypeStruct((rows * cols, outs), jnp.bfloat16),
        [],
        8,
    )
    sent = edge_rows(cot_edges, g_left, g_right, (0, rows - 1), [basis_edges])
    g_top, g_bottom = bands_beside(sent)
    input_grad = backward_inner(bands, cotangent, mixing, g_left, g_right, window)
    near_edges = jnp.concatenate([cotangent[:2], cotangent[rows - 2 :]], axis=0)
    input_grad = backward_edges(
        bands, g_top, g_bottom, mixing, g_left, g_right, near_edges, input_grad, window
    )
    return (
        field_out.reshape(rows, cols, outs),
        input_grad,
        weight_grad,
    )


def solution(mesh):
    return jax.shard_map(
        on_device,
        mesh=mesh,
        in_specs=(
            P(("ens", "lat"), "lon", None),
            P("lat", None, None, None),
            P("lat"),
            P(),
            P(("ens", "lat"), "lon", None),
        ),
        out_specs=(
            P(("ens", "lat"), "lon", None),
            P(("ens", "lat"), "lon", None),
            P("lon", "ens", None),
        ),
        check_vma=False,
    )
```

time: 213 us -> 80.4 us (0.38)
  local copies, waits for them, and re-layouts: 81.1 us -> 4.77 us
  waiting for transfers between devices: 65.6 us -> 23.3 us
  matrix products: 29.3 us -> 0 us
  Pallas kernels: 0 us -> 21.1 us
  starting transfers between devices: 16.1 us -> 29.7 us
  between operations: 14.2 us -> 0.86 us
  other arithmetic: 5.18 us -> 0.37 us
    another operation x2 -> x0, local copies, waits for them, and re-layouts: 36.3 us -> none  [band_matrix(): repeated = jnp.tile(padded, (1,) * len(leading) + (out_cols,))]
    psum x1 -> x0, waiting for transfers between devices: 32.6 us -> none  [on_device(): weight_grad = lax.psum(own_share, 'lat')]
    dot_general x5 -> x0, matrix products: 29.3 us -> none  [the longest x1 12.7 us: on_device(): jnp.einsum('arkjq,abjkc->arbqc', banded, mixed_grad, preferred_element_ty...]
    pallas_call x0 -> x10, Pallas kernels: none -> 21.1 us  [kernel_call(): pl.pallas_call(body, in_specs=specs, out_specs=place if single else [plac...]
    unnamed x17 -> x12, local copies, waits for them, and re-layouts: 20.8 us -> 4.7 us
    ppermute x8 -> x17, starting transfers between devices: 15.8 us -> 29.7 us  [the longest x3 7.26 us: beside(): right = lax.ppermute(pair[1], 'lon', ring('lon', -1))]
    ppermute x8 -> x17, waiting for transfers between devices: 33 us -> 23.3 us  [the longest x2 8.63 us: reduced_gradient(): other = lax.ppermute(send, 'lat', swap('lat', mask))]
    slice x4 -> x2, local copies, waits for them, and re-layouts: 7.2 us -> 0.05 us  [the longest x1 0.03 us: reduced_gradient(): keep, send = (total[:half], total[half:].astype(jnp.bfloat16))]
  transfers between devices with their start and end apart: 10 -> 17, of which waited for: 5 -> 7; matrix products, arithmetic and copies ran while one was open for 36% -> 0% of each run, Pallas kernels for 0% -> 17%
where the time goes in v1:
time: 80.4 us; the launch traced here: 80.1 us
  starting transfers between devices  29.7 us (37%)
  waiting for transfers between devices  23.3 us (29%)
  Pallas kernels  21.1 us (26%)
  local copies, waits for them, and re-layouts  4.77 us (6%)
  between operations  0.86 us (1%)
    pallas_call x10, Pallas kernels, kernel_call(): pl.pallas_call(body, in_specs=specs, out_specs=place if single else [plac...  21.1 us
    ppermute x2, waiting for transfers between devices, reduced_gradient(): other = lax.ppermute(send, 'lat', swap('lat', mask))  8.63 us
    ppermute x3, waiting for transfers between devices, reduced_gradient(): other = lax.ppermute(wire[s], 'lon', ring('lon', s))  7.6 us
    ppermute x3, starting transfers between devices, beside(): right = lax.ppermute(pair[1], 'lon', ring('lon', -1))  7.26 us
    ppermute x3, waiting for transfers between devices, beside(): right = lax.ppermute(pair[1], 'lon', ring('lon', -1))  6.56 us
    ppermute x3, starting transfers between devices, beside(): left = lax.ppermute(pair[0], 'lon', ring('lon', 1))  5.64 us
    ppermute x2, starting transfers between devices, reduced_gradient(): other = lax.ppermute(send, 'lat', swap('lat', mask))  5.17 us
    unnamed x12, local copies, waits for them, and re-layouts  4.7 us
  transfers between devices with their start and end apart: 17, of which 7 were waited for; matrix products, arithmetic and copies ran while one was open for 0% of the time, Pallas kernels for 17%

profile of v1, /device:TPU:0, one launch (start us, length us, event | category | flops | bytes accessed | tf_op | source)
XLA Modules:
  0.0 80.1 jit_solution(11118970451249645537)
XLA Ops:
  0.6 0.0 copy-start.2
  0.6 1.0 %copy-done.2 = bf16[8,128,256]{2,1,0:T(8,128)(2,1)S(1)} copy-done((bf16[8,128,256]{2,1,0:T(8,128)(2,1)S(1)}, bf16[8,128,256]{2,1,0:T(8,128)(2,1)}, u32[]{:S(2)}) %copy-start.2) | copy-done | bytes 524312
  1.7 0.6 shard_map.77
  2.2 3.1 %collective-permute-start = (bf16[4,64,256]{2,1,0:T(8,128)(2,1)S(1)}, bf16[4,64,256]{2,1,0:T(8,128)(2,1)S(1)}, u32[]{:S(2)}, u32[]{:S(2)}) collective-permute-start(bf16[4,64,256]{2,1,0:T(8,128)(2,1)S(1)} %get-tuple-element.22), channel_id=1, source_target_pairs={{0,1},{1,2},{2,3},{3,0},{4,5},{5,6},{6,7},{7,4},{8,9},{9,10},{10,1... | collective-permute-start | bytes 393224 | tf_op jit(solution)/shard_map/ppermute | solution.py:508
  5.3 2.1 %collective-permute-start.1 = (bf16[4,64,256]{2,1,0:T(8,128)(2,1)S(1)}, bf16[4,64,256]{2,1,0:T(8,128)(2,1)S(1)}, u32[]{:S(2)}, u32[]{:S(2)}) collective-permute-start(bf16[4,64,256]{2,1,0:T(8,128)(2,1)S(1)} %get-tuple-element.23), channel_id=1, source_target_pairs={{0,3},{1,0},{2,1},{3,2},{4,7},{5,4},{6,5},{7,6},{8,11},{9,8},{10,9... | collective-permute-start | bytes 393224 | tf_op jit(solution)/shard_map/ppermute | solution.py:509
  7.4 0.0 collective-permute-start.4
  7.4 3.8 %collective-permute-start.5 = (bf16[4,64,256]{2,1,0:T(8,128)(2,1)S(1)}, bf16[4,64,256]{2,1,0:T(8,128)(2,1)S(1)}, u32[]{:S(2)}, u32[]{:S(2)}) collective-permute-start(bf16[4,64,256]{2,1,0:T(8,128)(2,1)S(1)} %get-tuple-element.27), channel_id=1, source_target_pairs={{0,3},{1,0},{2,1},{3,2},{4,7},{5,4},{6,5},{7,6},{8,11},{9,8},{10,9... | collective-permute-start | bytes 393224 | tf_op jit(solution)/shard_map/ppermute | solution.py:509
  11.3 0.5 collective-permute-done.left.rest_0_
  11.7 2.9 %collective-permute-done.1.right.rest_1_ = bf16[4,64,256]{2,1,0:T(8,128)(2,1)S(1)} collective-permute-done((bf16[4,64,256]{2,1,0:T(8,128)(2,1)S(1)}, bf16[4,64,256]{2,1,0:T(8,128)(2,1)S(1)}, u32[]{:S(2)}, u32[]{:S(2)}) %collective-permute-start.1) | collective-permute-done | bytes 131104 | tf_op jit(solution)/shard_map/ppermute | solution.py:509
  14.7 1.3 %collective-permute-start.2 = (bf16[256,256]{1,0:T(8,128)(2,1)S(1)}, bf16[256,256]{1,0:T(8,128)(2,1)S(1)}, u32[]{:S(2)}, u32[]{:S(2)}) collective-permute-start(bf16[256,256]{1,0:T(8,128)(2,1)S(1)} %get-tuple-element.24), channel_id=1, source_target_pairs={{0,4},{4,8},{8,12},{1,5},{5,9},{9,13},{2,6},{6,10},{10,14},{3,7},{... | collective-permute-start | bytes 393224 | tf_op jit(solution)/shard_map/ppermute | solution.py:513
  16.0 1.3 %collective-permute-start.3 = (bf16[256,256]{1,0:T(8,128)(2,1)S(1)}, bf16[256,256]{1,0:T(8,128)(2,1)S(1)}, u32[]{:S(2)}, u32[]{:S(2)}) collective-permute-start(bf16[256,256]{1,0:T(8,128)(2,1)S(1)} %get-tuple-element.25), channel_id=1, source_target_pairs={{4,0},{8,4},{12,8},{5,1},{9,5},{13,9},{6,2},{10,6},{14,10},{7,3},{... | collective-permute-start | bytes 393224 | tf_op jit(solution)/shard_map/ppermute | solution.py:514
  17.3 0.0 copy-start.4
  17.3 0.9 %copy-done.4 = f32[8,3,8,129]{3,2,1,0:T(8,128)S(1)} copy-done((f32[8,3,8,129]{3,2,1,0:T(8,128)S(1)}, f32[8,3,8,129]{3,2,1,0:T(8,128)}, u32[]{:S(2)}) %copy-start.4) | copy-done | bytes 99096
  18.2 0.7 copy-done.5
  18.8 2.2 %shard_map.76 = (bf16[8,256,512]{2,1,0:T(8,128)(2,1)S(1)}, bf16[2,8,256]{2,1,0:T(8,128)(2,1)S(1)}) custom-call(s32[8]{0:T(128)S(1)} %copy-done.5, f32[8,3,8,129]{3,2,1,0:T(8,128)S(1)} %copy-done.4), custom_call_target="tpu_custom_call" | custom-call | tf_op jit(solution)/shard_map/pallas_call | solution.py:47
  21.0 0.1 pad_add_fusion.ids
  21.1 0.0 collective-permute-done.4.rest_2_
  21.1 0.0 collective-permute-done.5.rest_3_
  21.1 0.1 collective-permute-done.3.bottom
  21.2 1.0 %copy-done.1 = bf16[8,128,256]{2,1,0:T(8,128)(2,1)S(1)} copy-done((bf16[8,128,256]{2,1,0:T(8,128)(2,1)S(1)}, bf16[8,128,256]{2,1,0:T(8,128)(2,1)}, u32[]{:S(2)}) %copy-start.1) | copy-done | bytes 524312
  22.2 1.0 %copy-done.3 = bf16[8,128,256]{2,1,0:T(8,128)(2,1)S(1)} copy-done((bf16[8,128,256]{2,1,0:T(8,128)(2,1)S(1)}, bf16[8,128,256]{2,1,0:T(8,128)(2,1)}, u32[]{:S(2)}) %copy-start.3) | copy-done | bytes 524312
  23.3 5.7 %shard_map.79 = (bf16[1024,2048]{1,0:T(8,128)(2,1)S(1)}, f32[2,4,2,64,256]{4,3,2,1,0:T(8,128)S(1)}, bf16[2,4,2,64,256]{4,3,2,1,0:T(8,128)(2,1)S(1)}) custom-call(s32[2]{0:T(128)S(1)} %pad_add_fusion.ids, bf16[8,256,512]{2,1,0:T(8,128)(2,1)S(1)} %get-tuple-element.20.bands, bf16[8,128,256]{2,1,0:T(8,128)(2,1)S(1)} %copy-done.3, ...), custom_call_target="tpu_custom_call" | custom-call | tf_op jit(solution)/shard_map/pallas_call | solution.py:47
  29.0 0.0 copy-start
  29.0 3.6 %collective-permute-start.10 = (bf16[2,4,2,64,256]{4,3,2,1,0:T(8,128)(2,1)S(1)}, bf16[2,4,2,64,256]{4,3,2,1,0:T(8,128)(2,1)S(1)}, u32[]{:S(2)}, u32[]{:S(2)}) collective-permute-start(bf16[2,4,2,64,256]{4,3,2,1,0:T(8,128)(2,1)S(1)} %get-tuple-element.36), channel_id=1, source_target_pairs={{0,4},{4,0},{8,12},{12,8},{1,5},{5,1},{9,13},{13,9},{2,6},{6,2},{1... | collective-permute-start | bytes 1572872 | tf_op jit(solution)/shard_map/ppermute | solution.py:475
  32.6 1.5 %collective-permute-done.10 = bf16[2,4,2,64,256]{4,3,2,1,0:T(8,128)(2,1)S(1)} collective-permute-done((bf16[2,4,2,64,256]{4,3,2,1,0:T(8,128)(2,1)S(1)}, bf16[2,4,2,64,256]{4,3,2,1,0:T(8,128)(2,1)S(1)}, u32[]{:S(2)}, u32[]{:S(2)}) %collective-permute-start.10) | collective-permute-done | bytes 524320 | tf_op jit(solution)/shard_map/ppermute | solution.py:475
  34.1 0.1 convert_add_fusion
  34.3 1.6 %collective-permute-start.11 = (bf16[1,4,2,64,256]{4,3,2,1,0:T(8,128)(2,1)S(1)}, bf16[1,4,2,64,256]{4,3,2,1,0:T(8,128)(2,1)S(1)}, u32[]{:S(2)}, u32[]{:S(2)}) collective-permute-start(bf16[1,4,2,64,256]{4,3,2,1,0:T(8,128)(2,1)S(1)} %slice.59), channel_id=1, source_target_pairs={{0,8},{4,12},{8,0},{12,4},{1,9},{5,13},{9,1},{13,5},{2,10},{6,14},... | collective-permute-start | bytes 786440 | tf_op jit(solution)/shard_map/ppermute | solution.py:475
  35.9 7.1 %collective-permute-done.11 = bf16[1,4,2,64,256]{4,3,2,1,0:T(8,128)(2,1)S(1)} collective-permute-done((bf16[1,4,2,64,256]{4,3,2,1,0:T(8,128)(2,1)S(1)}, bf16[1,4,2,64,256]{4,3,2,1,0:T(8,128)(2,1)S(1)}, u32[]{:S(2)}, u32[]{:S(2)}) %collective-permute-start.11) | collective-permute-done | bytes 262176 | tf_op jit(solution)/shard_map/ppermute | solution.py:475
  43.0 0.1 fusion.5
  43.1 1.8 %collective-permute-start.14 = (bf16[2,64,256]{2,1,0:T(8,128)(2,1)S(1)}, bf16[2,64,256]{2,1,0:T(8,128)(2,1)S(1)}, u32[]{:S(2)}, u32[]{:S(2)}) collective-permute-start(bf16[2,64,256]{2,1,0:T(8,128)(2,1)S(1)} %get-tuple-element.42), channel_id=1, source_target_pairs={{0,3},{1,0},{2,1},{3,2},{4,7},{5,4},{6,5},{7,6},{8,11},{9,8},{10,9... | collective-permute-start | bytes 196616 | tf_op jit(solution)/shard_map/ppermute | solution.py:486
  44.8 0.3 collective-permute-start.13
  45.2 0.7 collective-permute-start.12
  45.8 0.3 shard_map.81
  46.2 2.5 %collective-permute-start.6 = (bf16[8,64,256]{2,1,0:T(8,128)(2,1)S(1)}, bf16[8,64,256]{2,1,0:T(8,128)(2,1)S(1)}, u32[]{:S(2)}, u32[]{:S(2)}) collective-permute-start(bf16[8,64,256]{2,1,0:T(8,128)(2,1)S(1)} %get-tuple-element.30), channel_id=1, source_target_pairs={{0,1},{1,2},{2,3},{3,0},{4,5},{5,6},{6,7},{7,4},{8,9},{9,10},{10,1... | collective-permute-start | bytes 786440 | tf_op jit(solution)/shard_map/ppermute | solution.py:508
  48.7 1.3 %collective-permute-start.7 = (bf16[8,64,256]{2,1,0:T(8,128)(2,1)S(1)}, bf16[8,64,256]{2,1,0:T(8,128)(2,1)S(1)}, u32[]{:S(2)}, u32[]{:S(2)}) collective-permute-start(bf16[8,64,256]{2,1,0:T(8,128)(2,1)S(1)} %get-tuple-element.31), channel_id=1, source_target_pairs={{0,3},{1,0},{2,1},{3,2},{4,7},{5,4},{6,5},{7,6},{8,11},{9,8},{10,9... | collective-permute-start | bytes 786440 | tf_op jit(solution)/shard_map/ppermute | solution.py:509
  50.1 7.6 %collective-permute-done.13 = bf16[2,64,256]{2,1,0:T(8,128)(2,1)S(1)} collective-permute-done((bf16[2,64,256]{2,1,0:T(8,128)(2,1)S(1)}, bf16[2,64,256]{2,1,0:T(8,128)(2,1)S(1)}, u32[]{:S(2)}, u32[]{:S(2)}) %collective-permute-start.13) | collective-permute-done | bytes 65568 | tf_op jit(solution)/shard_map/ppermute | solution.py:486
  57.7 1.2 %collective-permute-start.15 = (bf16[1,2,64,256]{3,2,1,0:T(8,128)(2,1)S(1)}, bf16[1,2,64,256]{3,2,1,0:T(8,128)(2,1)S(1)}, u32[]{:S(2)}, u32[]{:S(2)}) collective-permute-start(bf16[1,2,64,256]{3,2,1,0:T(8,128)(2,1)S(1)} %fusion.4), channel_id=1, source_target_pairs={{0,8},{4,12},{8,0},{12,4},{1,9},{5,13},{9,1},{13,5},{2,10},{6,14},... | collective-permute-start | bytes 196616 | tf_op jit(solution)/shard_map/ppermute | solution.py:491
  58.9 3.6 %collective-permute-done.7.right = bf16[8,64,256]{2,1,0:T(8,128)(2,1)S(1)} collective-permute-done((bf16[8,64,256]{2,1,0:T(8,128)(2,1)S(1)}, bf16[8,64,256]{2,1,0:T(8,128)(2,1)S(1)}, u32[]{:S(2)}, u32[]{:S(2)}) %collective-permute-start.7) | collective-permute-done | bytes 262176 | tf_op jit(solution)/shard_map/ppermute | solution.py:509
  62.6 1.6 %collective-permute-start.8 = (bf16[264,256]{1,0:T(8,128)(2,1)S(1)}, bf16[264,256]{1,0:T(8,128)(2,1)S(1)}, u32[]{:S(2)}, u32[]{:S(2)}) collective-permute-start(bf16[264,256]{1,0:T(8,128)(2,1)S(1)} %get-tuple-element.33), channel_id=1, source_target_pairs={{0,4},{4,8},{8,12},{1,5},{5,9},{9,13},{2,6},{6,10},{10,14},{3,7},{... | collective-permute-start | bytes 405512 | tf_op jit(solution)/shard_map/ppermute | solution.py:513
  64.1 1.3 %collective-permute-start.9 = (bf16[264,256]{1,0:T(8,128)(2,1)S(1)}, bf16[264,256]{1,0:T(8,128)(2,1)S(1)}, u32[]{:S(2)}, u32[]{:S(2)}) collective-permute-start(bf16[264,256]{1,0:T(8,128)(2,1)S(1)} %get-tuple-element.34), channel_id=1, source_target_pairs={{4,0},{8,4},{12,8},{5,1},{9,5},{13,9},{6,2},{10,6},{14,10},{7,3},{... | collective-permute-start | bytes 405512 | tf_op jit(solution)/shard_map/ppermute | solution.py:514
  65.4 0.0 collective-permute-done.15
  65.5 2.3 %collective-permute-start.16 = (bf16[2,2,64,256]{3,2,1,0:T(8,128)(2,1)S(1)}, bf16[2,2,64,256]{3,2,1,0:T(8,128)(2,1)S(1)}, u32[]{:S(2)}, u32[]{:S(2)}) collective-permute-start(bf16[2,2,64,256]{3,2,1,0:T(8,128)(2,1)S(1)} %pad_maximum_fusion.1.mine), channel_id=1, source_target_pairs={{0,4},{4,0},{8,12},{12,8},{1,5},{5,1},{9,13},{13,9},{2,6},{6,2},{1... | collective-permute-start | bytes 393224 | tf_op jit(solution)/shard_map/ppermute | solution.py:491
  67.8 2.1 %shard_map.80 = bf16[1024,256]{1,0:T(8,128)(2,1)} custom-call(bf16[1024,2048]{1,0:T(8,128)(2,1)S(1)} %get-tuple-element.28.filt, bf16[2048,256]{1,0:T(8,128)(2,1)S(1)} %bitcast.25), custom_call_target="tpu_custom_call" | custom-call | tf_op jit(solution)/shard_map/pallas_call | solution.py:47
  69.8 6.3 %shard_map.83.given = bf16[8,128,256]{2,1,0:T(8,128)(2,1)} custom-call(bf16[8,256,512]{2,1,0:T(8,128)(2,1)S(1)} %get-tuple-element.20.bands, bf16[8,128,256]{2,1,0:T(8,128)(2,1)S(1)} %copy-done.1, bf16[8,256,256]{2,1,0:T(8,128)(2,1)S(1)} %copy-done, bf16[8,64,256]{2,1,0:T(8,128)(2,1)S(1)} %collective-permute-done.6.left, ...), custom_call_target="tpu_custom_call" | custom-call | tf_op jit(solution)/shard_map/pallas_call | solution.py:47
  76.1 0.0 collective-permute-done.8.top
  76.1 0.0 collective-permute-done.9.bottom
  76.2 2.5 %shard_map.84 = bf16[8,128,256]{2,1,0:T(8,128)(2,1)} custom-call(bf16[8,256,512]{2,1,0:T(8,128)(2,1)S(1)} %get-tuple-element.20.bands, bf16[264,256]{1,0:T(8,128)(2,1)S(1)} %collective-permute-done.8.top, bf16[264,256]{1,0:T(8,128)(2,1)S(1)} %collective-permute-done.9.bottom, bf16[8,256,256]{2,1,0:T(8,128)(2,1)S(1)} %copy-done, ...), custom_call_target="tpu_custom_call", output_to_operand_aliasing={{}: (7, {})} | custom-call | tf_op jit(solution)/shard_map/pallas_call | solution.py:47
  78.7 1.4 %shard_map.85 = f32[2,256,256]{2,1,0:T(8,128)} custom-call(s32[2]{0:T(128)S(1)} %pad_add_fusion.ids, bf16[2,2,64,256]{3,2,1,0:T(8,128)(2,1)S(1)} %pad_maximum_fusion.1.mine, bf16[2,2,64,256]{3,2,1,0:T(8,128)(2,1)S(1)} %collective-permute-done.16.other), custom_call_target="tpu_custom_call" | custom-call | tf_op jit(solution)/shard_map/pallas_call | solution.py:47
  (17 shorter events, 0.2 us)
Async XLA Ops:
  0.6 1.0 %copy-start.2 = (bf16[8,128,256]{2,1,0:T(8,128)(2,1)S(1)}, bf16[8,128,256]{2,1,0:T(8,128)(2,1)}, u32[]{:S(2)}) copy-start(bf16[8,128,256]{2,1,0:T(8,128)(2,1)} %own.2) | copy-start | bytes 1572868
  2.2 9.5 %collective-permute-start = (bf16[4,64,256]{2,1,0:T(8,128)(2,1)S(1)}, bf16[4,64,256]{2,1,0:T(8,128)(2,1)S(1)}, u32[]{:S(2)}, u32[]{:S(2)}) collective-permute-start(bf16[4,64,256]{2,1,0:T(8,128)(2,1)S(1)} %get-tuple-element.22), channel_id=1, source_target_pairs={{0,1},{1,2},{2,3},{3,0},{4,5},{5,6},{6,7},{7,4},{8,9},{9,10},{10,1... | collective-permute-start | bytes 393224 | tf_op jit(solution)/shard_map/ppermute | solution.py:508
  5.3 9.3 %collective-permute-start.1 = (bf16[4,64,256]{2,1,0:T(8,128)(2,1)S(1)}, bf16[4,64,256]{2,1,0:T(8,128)(2,1)S(1)}, u32[]{:S(2)}, u32[]{:S(2)}) collective-permute-start(bf16[4,64,256]{2,1,0:T(8,128)(2,1)S(1)} %get-tuple-element.23), channel_id=1, source_target_pairs={{0,3},{1,0},{2,1},{3,2},{4,7},{5,4},{6,5},{7,6},{8,11},{9,8},{10,9... | collective-permute-start | bytes 393224 | tf_op jit(solution)/shard_map/ppermute | solution.py:509
  7.4 13.7 %collective-permute-start.4 = (bf16[4,64,256]{2,1,0:T(8,128)(2,1)S(1)}, bf16[4,64,256]{2,1,0:T(8,128)(2,1)S(1)}, u32[]{:S(2)}, u32[]{:S(2)}) collective-permute-start(bf16[4,64,256]{2,1,0:T(8,128)(2,1)S(1)} %get-tuple-element.26), channel_id=1, source_target_pairs={{0,1},{1,2},{2,3},{3,0},{4,5},{5,6},{6,7},{7,4},{8,9},{9,10},{10,1... | collective-permute-start | bytes 393224 | tf_op jit(solution)/shard_map/ppermute | solution.py:508
  7.4 13.7 %collective-permute-start.5 = (bf16[4,64,256]{2,1,0:T(8,128)(2,1)S(1)}, bf16[4,64,256]{2,1,0:T(8,128)(2,1)S(1)}, u32[]{:S(2)}, u32[]{:S(2)}) collective-permute-start(bf16[4,64,256]{2,1,0:T(8,128)(2,1)S(1)} %get-tuple-element.27), channel_id=1, source_target_pairs={{0,3},{1,0},{2,1},{3,2},{4,7},{5,4},{6,5},{7,6},{8,11},{9,8},{10,9... | collective-permute-start | bytes 393224 | tf_op jit(solution)/shard_map/ppermute | solution.py:509
  14.7 6.5 %collective-permute-start.2 = (bf16[256,256]{1,0:T(8,128)(2,1)S(1)}, bf16[256,256]{1,0:T(8,128)(2,1)S(1)}, u32[]{:S(2)}, u32[]{:S(2)}) collective-permute-start(bf16[256,256]{1,0:T(8,128)(2,1)S(1)} %get-tuple-element.24), channel_id=1, source_target_pairs={{0,4},{4,8},{8,12},{1,5},{5,9},{9,13},{2,6},{6,10},{10,14},{3,7},{... | collective-permute-start | bytes 393224 | tf_op jit(solution)/shard_map/ppermute | solution.py:513
  16.0 5.2 %collective-permute-start.3 = (bf16[256,256]{1,0:T(8,128)(2,1)S(1)}, bf16[256,256]{1,0:T(8,128)(2,1)S(1)}, u32[]{:S(2)}, u32[]{:S(2)}) collective-permute-start(bf16[256,256]{1,0:T(8,128)(2,1)S(1)} %get-tuple-element.25), channel_id=1, source_target_pairs={{4,0},{8,4},{12,8},{5,1},{9,5},{13,9},{6,2},{10,6},{14,10},{7,3},{... | collective-permute-start | bytes 393224 | tf_op jit(solution)/shard_map/ppermute | solution.py:514
  17.3 0.9 %copy-start.4 = (f32[8,3,8,129]{3,2,1,0:T(8,128)S(1)}, f32[8,3,8,129]{3,2,1,0:T(8,128)}, u32[]{:S(2)}) copy-start(f32[8,3,8,129]{3,2,1,0:T(8,128)} %quadrature.1) | copy-start | bytes 297220
  18.2 0.7 copy-start.5
  21.2 1.0 %copy-start.1 = (bf16[8,128,256]{2,1,0:T(8,128)(2,1)S(1)}, bf16[8,128,256]{2,1,0:T(8,128)(2,1)}, u32[]{:S(2)}) copy-start(bf16[8,128,256]{2,1,0:T(8,128)(2,1)} %own.3) | copy-start | bytes 1572868
  22.2 1.0 %copy-start.3 = (bf16[8,128,256]{2,1,0:T(8,128)(2,1)S(1)}, bf16[8,128,256]{2,1,0:T(8,128)(2,1)}, u32[]{:S(2)}) copy-start(bf16[8,128,256]{2,1,0:T(8,128)(2,1)} %own.2) | copy-start | bytes 1572868
  29.0 38.8 %copy-start = (bf16[8,256,256]{2,1,0:T(8,128)(2,1)S(1)}, bf16[8,256,256]{2,1,0:T(8,128)(2,1)}, u32[]{:S(2)}) copy-start(bf16[8,256,256]{2,1,0:T(8,128)(2,1)} %mixing.3) | copy-start | bytes 3145732
  29.0 5.1 %collective-permute-start.10 = (bf16[2,4,2,64,256]{4,3,2,1,0:T(8,128)(2,1)S(1)}, bf16[2,4,2,64,256]{4,3,2,1,0:T(8,128)(2,1)S(1)}, u32[]{:S(2)}, u32[]{:S(2)}) collective-permute-start(bf16[2,4,2,64,256]{4,3,2,1,0:T(8,128)(2,1)S(1)} %get-tuple-element.36), channel_id=1, source_target_pairs={{0,4},{4,0},{8,12},{12,8},{1,5},{5,1},{9,13},{13,9},{2,6},{6,2},{1... | collective-permute-start | bytes 1572872 | tf_op jit(solution)/shard_map/ppermute | solution.py:475
  34.3 8.7 %collective-permute-start.11 = (bf16[1,4,2,64,256]{4,3,2,1,0:T(8,128)(2,1)S(1)}, bf16[1,4,2,64,256]{4,3,2,1,0:T(8,128)(2,1)S(1)}, u32[]{:S(2)}, u32[]{:S(2)}) collective-permute-start(bf16[1,4,2,64,256]{4,3,2,1,0:T(8,128)(2,1)S(1)} %slice.59), channel_id=1, source_target_pairs={{0,8},{4,12},{8,0},{12,4},{1,9},{5,13},{9,1},{13,5},{2,10},{6,14},... | collective-permute-start | bytes 786440 | tf_op jit(solution)/shard_map/ppermute | solution.py:475
  43.1 7.0 %collective-permute-start.14 = (bf16[2,64,256]{2,1,0:T(8,128)(2,1)S(1)}, bf16[2,64,256]{2,1,0:T(8,128)(2,1)S(1)}, u32[]{:S(2)}, u32[]{:S(2)}) collective-permute-start(bf16[2,64,256]{2,1,0:T(8,128)(2,1)S(1)} %get-tuple-element.42), channel_id=1, source_target_pairs={{0,3},{1,0},{2,1},{3,2},{4,7},{5,4},{6,5},{7,6},{8,11},{9,8},{10,9... | collective-permute-start | bytes 196616 | tf_op jit(solution)/shard_map/ppermute | solution.py:486
  44.8 12.8 %collective-permute-start.13 = (bf16[2,64,256]{2,1,0:T(8,128)(2,1)S(1)}, bf16[2,64,256]{2,1,0:T(8,128)(2,1)S(1)}, u32[]{:S(2)}, u32[]{:S(2)}) collective-permute-start(bf16[2,64,256]{2,1,0:T(8,128)(2,1)S(1)} %get-tuple-element.43), channel_id=1, source_target_pairs={{0,2},{1,3},{2,0},{3,1},{4,6},{5,7},{6,4},{7,5},{8,10},{9,11},{10,... | collective-permute-start | bytes 196616 | tf_op jit(solution)/shard_map/ppermute | solution.py:486
  45.2 12.5 %collective-permute-start.12 = (bf16[2,64,256]{2,1,0:T(8,128)(2,1)S(1)}, bf16[2,64,256]{2,1,0:T(8,128)(2,1)S(1)}, u32[]{:S(2)}, u32[]{:S(2)}) collective-permute-start(bf16[2,64,256]{2,1,0:T(8,128)(2,1)S(1)} %get-tuple-element.41), channel_id=1, source_target_pairs={{0,1},{1,2},{2,3},{3,0},{4,5},{5,6},{6,7},{7,4},{8,9},{9,10},{10,1... | collective-permute-start | bytes 196616 | tf_op jit(solution)/shard_map/ppermute | solution.py:486
  46.2 12.7 %collective-permute-start.6 = (bf16[8,64,256]{2,1,0:T(8,128)(2,1)S(1)}, bf16[8,64,256]{2,1,0:T(8,128)(2,1)S(1)}, u32[]{:S(2)}, u32[]{:S(2)}) collective-permute-start(bf16[8,64,256]{2,1,0:T(8,128)(2,1)S(1)} %get-tuple-element.30), channel_id=1, source_target_pairs={{0,1},{1,2},{2,3},{3,0},{4,5},{5,6},{6,7},{7,4},{8,9},{9,10},{10,1... | collective-permute-start | bytes 786440 | tf_op jit(solution)/shard_map/ppermute | solution.py:508
  48.7 13.8 %collective-permute-start.7 = (bf16[8,64,256]{2,1,0:T(8,128)(2,1)S(1)}, bf16[8,64,256]{2,1,0:T(8,128)(2,1)S(1)}, u32[]{:S(2)}, u32[]{:S(2)}) collective-permute-start(bf16[8,64,256]{2,1,0:T(8,128)(2,1)S(1)} %get-tuple-element.31), channel_id=1, source_target_pairs={{0,3},{1,0},{2,1},{3,2},{4,7},{5,4},{6,5},{7,6},{8,11},{9,8},{10,9... | collective-permute-start | bytes 786440 | tf_op jit(solution)/shard_map/ppermute | solution.py:509
  57.7 7.7 %collective-permute-start.15 = (bf16[1,2,64,256]{3,2,1,0:T(8,128)(2,1)S(1)}, bf16[1,2,64,256]{3,2,1,0:T(8,128)(2,1)S(1)}, u32[]{:S(2)}, u32[]{:S(2)}) collective-permute-start(bf16[1,2,64,256]{3,2,1,0:T(8,128)(2,1)S(1)} %fusion.4), channel_id=1, source_target_pairs={{0,8},{4,12},{8,0},{12,4},{1,9},{5,13},{9,1},{13,5},{2,10},{6,14},... | collective-permute-start | bytes 196616 | tf_op jit(solution)/shard_map/ppermute | solution.py:491
  62.6 13.6 %collective-permute-start.8 = (bf16[264,256]{1,0:T(8,128)(2,1)S(1)}, bf16[264,256]{1,0:T(8,128)(2,1)S(1)}, u32[]{:S(2)}, u32[]{:S(2)}) collective-permute-start(bf16[264,256]{1,0:T(8,128)(2,1)S(1)} %get-tuple-element.33), channel_id=1, source_target_pairs={{0,4},{4,8},{8,12},{1,5},{5,9},{9,13},{2,6},{6,10},{10,14},{3,7},{... | collective-permute-start | bytes 405512 | tf_op jit(solution)/shard_map/ppermute | solution.py:513
  64.1 12.0 %collective-permute-start.9 = (bf16[264,256]{1,0:T(8,128)(2,1)S(1)}, bf16[264,256]{1,0:T(8,128)(2,1)S(1)}, u32[]{:S(2)}, u32[]{:S(2)}) collective-permute-start(bf16[264,256]{1,0:T(8,128)(2,1)S(1)} %get-tuple-element.34), channel_id=1, source_target_pairs={{4,0},{8,4},{12,8},{5,1},{9,5},{13,9},{6,2},{10,6},{14,10},{7,3},{... | collective-permute-start | bytes 405512 | tf_op jit(solution)/shard_map/ppermute | solution.py:514
  65.5 13.2 %collective-permute-start.16 = (bf16[2,2,64,256]{3,2,1,0:T(8,128)(2,1)S(1)}, bf16[2,2,64,256]{3,2,1,0:T(8,128)(2,1)S(1)}, u32[]{:S(2)}, u32[]{:S(2)}) collective-permute-start(bf16[2,2,64,256]{3,2,1,0:T(8,128)(2,1)S(1)} %pad_maximum_fusion.1.mine), channel_id=1, source_target_pairs={{0,4},{4,0},{8,12},{12,8},{1,5},{5,1},{9,13},{13,9},{2,6},{6,2},{1... | collective-permute-start | bytes 393224 | tf_op jit(solution)/shard_map/ppermute | solution.py:491

commit v2 on v1

--- a/solution.py
+++ b/solution.py
@@ -38,10 +38,10 @@
 
 def kernel_call(body, operands, outs, scratch, mib, scalars=0, far=(), far_out=False, alias=None):
     specs = [IN_SMEM] * scalars
-    given = list(operands[:scalars])
+    given = [pltpu.with_memory_space_constraint(x, pltpu.HBM) for x in operands[:scalars]]
     for i, operand in enumerate(operands[scalars:], scalars):
         specs.append(IN_HBM if i in far else IN_VMEM)
-        given.append(operand if i in far else near(operand))
+        given.append(pltpu.with_memory_space_constraint(operand, pltpu.HBM) if i in far else near(operand))
     single = not isinstance(outs, list)
     place = IN_HBM if far_out else IN_VMEM
     return pl.pallas_call(
@@ -73,18 +73,22 @@
         bands[row, k * BLOCK : (k + 1) * BLOCK, :] = rolled.astype(bands.dtype)
 
 
-def bands_kernel(half_width, quadrature, bands, edges):
+def bands_kernel(reach, quadrature, field, cot, bands, edges, field_near, cot_near, sems):
+    copies = [
+        pltpu.make_async_copy(field, field_near, sems.at[0]),
+        pltpu.make_async_copy(cot, cot_near, sems.at[1]),
+    ]
+    for copy in copies:
+        copy.start()
     rows, three, kernels, taps = quadrature.shape
     window = taps - 1 + BLOCK
     middle = (taps - 1) // 2
     lane = lax.broadcasted_iota(jnp.int32, (kernels, LANES), 1)
     for row in range(rows):
-        reach = jnp.full((kernels, LANES), half_width[row], jnp.int32)
-        factor = 1.0 / jnp.sqrt(3.0 * (2.0 * reach.astype(jnp.float32) + 1.0))
-        head_inside = (jnp.abs(lane - middle) <= reach).astype(jnp.float32)
-        tail_inside = ((lane < taps - LANES) & (lane + LANES - middle <= reach)).astype(
-            jnp.float32
-        )
+        half = jnp.broadcast_to(reach[row : row + 1, :], (kernels, LANES))
+        factor = 1.0 / jnp.sqrt(3.0 * (2.0 * half.astype(jnp.float32) + 1.0))
+        head_inside = (jnp.abs(lane - middle) <= half).astype(jnp.float32)
+        tail_inside = ((lane < taps - LANES) & (lane + LANES - middle <= half)).astype(jnp.float32)
         pieces = []
         for r in range(three):
             head = quadrature[row, r, :, 0:LANES] * factor * head_inside
@@ -97,21 +101,25 @@
                 edges[1] = piece
             pieces.append(piece.astype(jnp.float32))
         spread_bands(packed_taps(pieces, window, bands.shape[2]), bands, row)
-
-
-def band_matrices(half_width, quadrature):
+    for copy in copies:
+        copy.wait()
+
+
+def band_matrices(reach, quadrature, field, cot):
     rows, three, kernels, taps = quadrature.shape
     total = -(-three * (taps - 1 + BLOCK) // DEPTH) * DEPTH
     return kernel_call(
         bands_kernel,
-        [half_width, quadrature],
+        [reach, quadrature, field, cot],
         [
             pltpu.VMEM((rows, kernels * BLOCK, total), jnp.bfloat16),
             pltpu.VMEM((2, kernels, 2 * LANES), jnp.bfloat16),
+            pltpu.VMEM(field.shape, field.dtype),
+            pltpu.VMEM(cot.shape, cot.dtype),
         ],
-        [],
-        8,
-        scalars=1,
+        [pltpu.SemaphoreType.DMA((2,))],
+        10,
+        far=(2, 3),
     )
 
 
@@ -121,8 +129,7 @@
     return outer, list(range(part, rows - part))
 
 
-def rims_kernel(groups, array, *refs):
-    *outs, edges, sems = refs
+def rim_copies(groups, array, outs, edges):
     rows, cols = array.shape[0], array.shape[1]
     rim = outs[0].shape[1]
     copies = []
@@ -134,32 +141,68 @@
                 size += 1
             source = array.at[pl.ds(group[place], size)]
             for side, first in ((0, cols - rim), (1, 0)):
-                copies.append(
-                    (
-                        source.at[:, pl.ds(first, rim), :],
-                        outs[2 * g + side].at[pl.ds(place, size)],
-                    )
-                )
+                target = outs[2 * g + side].at[pl.ds(place, size)]
+                copies.append((source.at[:, pl.ds(first, rim), :], target))
             place += size
     copies.append((array.at[0], edges.at[0]))
     copies.append((array.at[rows - 1], edges.at[1]))
+    return copies
+
+
+def run_copies(copies, sems, between=None):
     copies = [pltpu.make_async_copy(*c, sems.at[i]) for i, c in enumerate(copies)]
     for copy in copies:
         copy.start()
+    if between:
+        between()
     for copy in copies:
         copy.wait()
 
 
-def rims(array, rim, groups):
+def first_kernel(groups, half_width, array, quadrature, *refs):
+    *outs, edges, taps_near, reach, sems = refs
+
+    def spread_reach():
+        for row in range(reach.shape[0]):
+            reach[row : row + 1, :] = jnp.full((1, LANES), half_width[row], jnp.int32)
+
+    copies = rim_copies(groups, array, outs, edges)
+    run_copies(copies + [(quadrature, taps_near)], sems, spread_reach)
+
+
+def rims_kernel(groups, array, *refs):
+    *outs, edges, sems = refs
+    run_copies(rim_copies(groups, array, outs, edges), sems)
+
+
+def rim_shapes(array, rim, groups):
     _, cols, chans = array.shape
     outs = [
         pltpu.VMEM((len(group), rim, chans), jnp.bfloat16) for group in groups for _ in range(2)
     ]
-    outs.append(pltpu.VMEM((2, cols, chans), jnp.bfloat16))
+    return outs + [pltpu.VMEM((2, cols, chans), jnp.bfloat16)]
+
+
+def first_rims(half_width, array, quadrature, rim, groups):
+    outs = rim_shapes(array, rim, groups)
+    outs.append(pltpu.VMEM(quadrature.shape, jnp.float32))
+    outs.append(pltpu.VMEM((half_width.shape[0], LANES), jnp.int32))
+    return kernel_call(
+        functools.partial(first_kernel, groups),
+        [half_width, array, quadrature],
+        outs,
+        [pltpu.SemaphoreType.DMA((16,))],
+        6,
+        scalars=1,
+        far=(1, 2),
+    )
+
+
+def rims(array, rim, groups):
     return kernel_call(
         functools.partial(rims_kernel, groups),
         [array],
-        outs,
+        rim_shapes(array, rim, groups),
         [pltpu.SemaphoreType.DMA((16,))],
         4,
         far=(0,),
@@ -316,22 +359,7 @@
             write(first, k, result[k * BLOCK : (k + 1) * BLOCK])
 
 
-def mixed_back(filt, mixing, stage, cols):
-    kernels = mixing.shape[0]
-    total = None
-    for k in range(kernels):
-        term = lax.dot_general(
-            filt[k], mixing[k], (((1,), (1,)), ((), ())), preferred_element_type=jnp.float32
-        )
-        total = term if total is None else total + term
-    total = total.astype(jnp.bfloat16)
-    flip = mirror(cols)
-    for i in range(stage.shape[0]):
-        row = jnp.dot(flip, total[i * cols : (i + 1) * cols], preferred_element_type=jnp.float32)
-        stage[i] = row.astype(stage.dtype)
-
-
-def backward_inner_kernel(window, bands, own, mixing, left, right, out, reverse, filt, stage, sem):
+def backward_inner_kernel(window, bands, own, left, right, filt, reverse):
     rows, cols, _ = own.shape
     flip = mirror(reverse.shape[1])
 
@@ -357,42 +385,30 @@
         return carry
 
     lax.fori_loop(0, rows - 2, one, 0)
-    mixed_back(filt, mixing, stage, cols)
-    copy = pltpu.make_async_copy(stage, out.at[pl.ds(1, rows - 2)], sem)
-    copy.start()
-    copy.wait()
-
-
-def backward_inner(bands, own, mixing, left, right, window):
+
+
+def backward_inner(bands, own, left, right, window):
     rows, cols, outs = own.shape
     span = cols + 2 * left.shape[1]
-    kernels, chans, _ = mixing.shape
+    kernels = bands.shape[1] // BLOCK
     return kernel_call(
         functools.partial(backward_inner_kernel, window),
-        [bands, own, mixing, left, right],
-        jax.ShapeDtypeStruct((rows, cols, chans), jnp.bfloat16),
-        [
-            pltpu.VMEM((rows, span, outs), jnp.bfloat16),
-            pltpu.VMEM((kernels, (rows - 2) * cols, outs), jnp.bfloat16),
-            pltpu.VMEM((rows - 2, cols, chans), jnp.bfloat16),
-            pltpu.SemaphoreType.DMA(()),
-        ],
-        16,
-        far_out=True,
+        [bands, own, left, right],
+        pltpu.VMEM((kernels, (rows - 2) * cols, outs), jnp.bfloat16),
+        [pltpu.VMEM((rows, span, outs), jnp.bfloat16)],
+        12,
     )
 
 
 def backward_edges_kernel(
-    window, bands, top, bottom, mixing, left, right, edges, given, out,
-    reverse, extra, filt, stage, sems
+    window, bands, top, bottom, mixing, left, right, own, inner, out, reverse, extra, filt
 ):
-    rows = bands.shape[0]
-    cols = stage.shape[1]
+    rows, cols, _ = own.shape
     span = reverse.shape[1]
     flip = mirror(span)
     lines = [top[0:span]]
-    for i, row in enumerate((0, 1, rows - 2, rows - 1)):
-        lines.append(jnp.concatenate([left[row], edges[i], right[row]], axis=0))
+    for row in (0, 1, rows - 2, rows - 1):
+        lines.append(jnp.concatenate([left[row], own[row], right[row]], axis=0))
     lines.append(bottom[0:span])
     for i, line in enumerate(lines):
         reverse[i] = jnp.dot(flip, line, preferred_element_type=jnp.float32).astype(reverse.dtype)
@@ -412,36 +428,35 @@
             filt[k, base + first : base + first + BLOCK, :] = value
 
         adjoint_row(band, [reverse.at[at + 1], reverse.at[at], reverse.at[at - 1]], cols, write)
-    mixed_back(filt, mixing, stage, cols)
-    copies = [
-        pltpu.make_async_copy(stage.at[i], out.at[row], sems.at[i])
-        for i, row in enumerate((0, rows - 1))
-    ]
-    for copy in copies:
-        copy.start()
-    for copy in copies:
-        copy.wait()
-
-
-def backward_edges(bands, top, bottom, mixing, left, right, edges, given, window):
-    _, cols, chans = given.shape
+    turned = mirror(cols)
+    for source, where in ((inner, range(1, rows - 1)), (filt, (0, rows - 1))):
+        total = None
+        for k in range(mixing.shape[0]):
+            term = lax.dot_general(
+                source[k], mixing[k], (((1,), (1,)), ((), ())), preferred_element_type=jnp.float32
+            )
+            total = term if total is None else total + term
+        total = total.astype(jnp.bfloat16)
+        for i, row in enumerate(where):
+            part = total[i * cols : (i + 1) * cols]
+            part = jnp.dot(turned, part, preferred_element_type=jnp.float32)
+            out[row] = part.astype(out.dtype)
+
+
+def backward_edges(bands, top, bottom, mixing, left, right, own, inner, window):
+    rows, cols, outs = own.shape
     span = cols + 2 * left.shape[1]
-    kernels, _, outs = mixing.shape
+    kernels, chans, _ = mixing.shape
     return kernel_call(
         functools.partial(backward_edges_kernel, window),
-        [bands, top, bottom, mixing, left, right, edges, given],
-        jax.ShapeDtypeStruct(given.shape, given.dtype),
+        [bands, top, bottom, mixing, left, right, own, inner],
+        jax.ShapeDtypeStruct((rows, cols, chans), jnp.bfloat16),
         [
             pltpu.VMEM((6, span, outs), jnp.bfloat16),
             pltpu.VMEM((2,) + bands.shape[1:], jnp.bfloat16),
             pltpu.VMEM((kernels, 2 * cols, outs), jnp.bfloat16),
-            pltpu.VMEM((2, cols, chans), jnp.bfloat16),
-            pltpu.SemaphoreType.DMA((2,)),
         ],
         16,
-        far=(7,),
-        far_out=True,
-        alias={7: 0},
     )
 
 
@@ -515,10 +530,14 @@
         return top, bottom
 
     window = taps - 1 + BLOCK
-    *sides, own_edges = rims(field_in, rim, groups)
+    *sides, own_edges, taps_near, reach = first_rims(
+        half_width, field_in, quadrature, rim, groups
+    )
     outer_sides = beside(sides[0:2])
     inner_sides = beside(sides[2:4])
-    bands, basis_edges = band_matrices(half_width, quadrature)
+    bands, basis_edges, field_near, cot_near = band_matrices(
+        reach, taps_near, field_in, cotangent
+    )
     picks = (0, len(outer) - 1)
     sent = edge_rows(own_edges, *outer_sides, picks, [])
     f_top, f_bottom = bands_beside(sent)
@@ -528,10 +547,10 @@
     filtered, keep, send = forward(
         ids,
         bands,
-        field_in,
+        field_near,
         f_top,
         f_bottom,
-        cotangent.reshape(rows * cols, outs),
+        cot_near.reshape(rows * cols, outs),
         groups,
         outer_sides + inner_sides,
         kernels,
@@ -548,10 +567,9 @@
     )
     sent = edge_rows(cot_edges, g_left, g_right, (0, rows - 1), [basis_edges])
     g_top, g_bottom = bands_beside(sent)
-    input_grad = backward_inner(bands, cotangent, mixing, g_left, g_right, window)
-    near_edges = jnp.concatenate([cotangent[:2], cotangent[rows - 2 :]], axis=0)
+    inner = backward_inner(bands, cot_near, g_left, g_right, window)
     input_grad = backward_edges(
-        bands, g_top, g_bottom, mixing, g_left, g_right, near_edges, input_grad, window
+        bands, g_top, g_bottom, mixing, g_left, g_right, cot_near, inner, window
     )
     return (
         field_out.reshape(rows, cols, outs),

time: 80.4 us -> 78.3 us (0.974)
  local copies, waits for them, and re-layouts: 4.77 us -> 0.05 us
  Pallas kernels: 21.1 us -> 23.6 us
  starting transfers between devices: 29.7 us -> 28.2 us
  waiting for transfers between devices: 23.3 us -> 24.5 us
    unnamed x12 -> x2, local copies, waits for them, and re-layouts: 4.7 us -> 0.01 us
    pallas_call x10, Pallas kernels: 21.1 us -> 23.6 us  [kernel_call(): pl.pallas_call(body, in_specs=specs, out_specs=place if single else [plac...]
    ppermute x2, starting transfers between devices: 3.42 us -> 2.05 us  [reduced_gradient(): other = lax.ppermute(pieces, 'lat', swap('lat', mask))]
    ppermute x3, waiting for transfers between devices: 7.6 us -> 6.39 us  [reduced_gradient(): other = lax.ppermute(wire[s], 'lon', ring('lon', s))]
    ppermute x3, waiting for transfers between devices: 6.56 us -> 7.74 us  [beside(): right = lax.ppermute(pair[1], 'lon', ring('lon', -1))]
  transfers between devices with their start and end apart: 17 -> 17, of which waited for: 7 -> 8; matrix products, arithmetic and copies ran while one was open for 0% -> 1% of each run, Pallas kernels for 17% -> 18%
where the time goes in v2:
time: 78.3 us; the launch traced here: 78 us
  starting transfers between devices  28.2 us (36%)
  waiting for transfers between devices  24.5 us (31%)
  Pallas kernels  23.6 us (30%)
  other arithmetic  0.91 us (1%)
  between operations  0.8 us (1%)
    pallas_call x10, Pallas kernels, kernel_call(): pl.pallas_call(body, in_specs=specs, out_specs=place if single else [plac...  23.6 us
    ppermute x2, waiting for transfers between devices, reduced_gradient(): other = lax.ppermute(send, 'lat', swap('lat', mask))  9.11 us
    ppermute x3, waiting for transfers between devices, beside(): right = lax.ppermute(pair[1], 'lon', ring('lon', -1))  7.74 us
    ppermute x3, starting transfers between devices, beside(): right = lax.ppermute(pair[1], 'lon', ring('lon', -1))  7.26 us
    ppermute x3, waiting for transfers between devices, reduced_gradient(): other = lax.ppermute(wire[s], 'lon', ring('lon', s))  6.39 us
    ppermute x3, starting transfers between devices, beside(): left = lax.ppermute(pair[0], 'lon', ring('lon', 1))  5.64 us
    ppermute x2, starting transfers between devices, reduced_gradient(): other = lax.ppermute(send, 'lat', swap('lat', mask))  4.68 us
    ppermute x2, starting transfers between devices, bands_beside(): top = lax.ppermute(pair[0], 'lat', line('lat', 1))  3.23 us
  transfers between devices with their start and end apart: 17, of which 8 were waited for; matrix products, arithmetic and copies ran while one was open for 1% of the time, Pallas kernels for 18%

profile of v2, /device:TPU:0, one launch (start us, length us, event | category | flops | bytes accessed | tf_op | source)
XLA Modules:
  0.0 78.0 jit_solution(3455613798397656355)
XLA Ops:
  0.6 2.0 %shard_map.76 = (bf16[4,64,256]{2,1,0:T(8,128)(2,1)S(1)}, bf16[4,64,256]{2,1,0:T(8,128)(2,1)S(1)}, bf16[4,64,256]{2,1,0:T(8,128)(2,1)S(1)}, bf16[4,64,256]{2,1,0...) custom-call(s32[8]{0:T(128)} %half_width.1, ...), custom_call_target="tpu_custom_call" | custom-call | tf_op jit(solution)/shard_map/pallas_call | solution.py:47
  2.7 3.1 %collective-permute-start = (bf16[4,64,256]{2,1,0:T(8,128)(2,1)S(1)}, bf16[4,64,256]{2,1,0:T(8,128)(2,1)S(1)}, u32[]{:S(2)}, u32[]{:S(2)}) collective-permute-start(bf16[4,64,256]{2,1,0:T(8,128)(2,1)S(1)} %get-tuple-element.29), channel_id=1, source_target_pairs={{0,1},{1,2},{2,3},{3,0},{4,5},{5,6},{6,7},{7,4},{8,9},{9,10},{10,1... | collective-permute-start | bytes 393224 | tf_op jit(solution)/shard_map/ppermute | solution.py:523
  5.8 2.1 %collective-permute-start.1 = (bf16[4,64,256]{2,1,0:T(8,128)(2,1)S(1)}, bf16[4,64,256]{2,1,0:T(8,128)(2,1)S(1)}, u32[]{:S(2)}, u32[]{:S(2)}) collective-permute-start(bf16[4,64,256]{2,1,0:T(8,128)(2,1)S(1)} %get-tuple-element.30), channel_id=1, source_target_pairs={{0,3},{1,0},{2,1},{3,2},{4,7},{5,4},{6,5},{7,6},{8,11},{9,8},{10,9... | collective-permute-start | bytes 393224 | tf_op jit(solution)/shard_map/ppermute | solution.py:524
  7.9 0.0 collective-permute-start.4
  7.9 3.8 %collective-permute-start.5 = (bf16[4,64,256]{2,1,0:T(8,128)(2,1)S(1)}, bf16[4,64,256]{2,1,0:T(8,128)(2,1)S(1)}, u32[]{:S(2)}, u32[]{:S(2)}) collective-permute-start(bf16[4,64,256]{2,1,0:T(8,128)(2,1)S(1)} %get-tuple-element.35), channel_id=1, source_target_pairs={{0,3},{1,0},{2,1},{3,2},{4,7},{5,4},{6,5},{7,6},{8,11},{9,8},{10,9... | collective-permute-start | bytes 393224 | tf_op jit(solution)/shard_map/ppermute | solution.py:524
  11.7 0.5 collective-permute-done.left.rest_0_
  12.2 2.9 %collective-permute-done.1.right.rest_1_ = bf16[4,64,256]{2,1,0:T(8,128)(2,1)S(1)} collective-permute-done((bf16[4,64,256]{2,1,0:T(8,128)(2,1)S(1)}, bf16[4,64,256]{2,1,0:T(8,128)(2,1)S(1)}, u32[]{:S(2)}, u32[]{:S(2)}) %collective-permute-start.1) | collective-permute-done | bytes 131104 | tf_op jit(solution)/shard_map/ppermute | solution.py:524
  15.1 1.3 %collective-permute-start.2 = (bf16[256,256]{1,0:T(8,128)(2,1)S(1)}, bf16[256,256]{1,0:T(8,128)(2,1)S(1)}, u32[]{:S(2)}, u32[]{:S(2)}) collective-permute-start(bf16[256,256]{1,0:T(8,128)(2,1)S(1)} %get-tuple-element.31), channel_id=1, source_target_pairs={{0,4},{4,8},{8,12},{1,5},{5,9},{9,13},{2,6},{6,10},{10,14},{3,7},{... | collective-permute-start | bytes 393224 | tf_op jit(solution)/shard_map/ppermute | solution.py:528
  16.4 1.3 %collective-permute-start.3 = (bf16[256,256]{1,0:T(8,128)(2,1)S(1)}, bf16[256,256]{1,0:T(8,128)(2,1)S(1)}, u32[]{:S(2)}, u32[]{:S(2)}) collective-permute-start(bf16[256,256]{1,0:T(8,128)(2,1)S(1)} %get-tuple-element.32), channel_id=1, source_target_pairs={{4,0},{8,4},{12,8},{5,1},{9,5},{13,9},{6,2},{10,6},{14,10},{7,3},{... | collective-permute-start | bytes 393224 | tf_op jit(solution)/shard_map/ppermute | solution.py:529
  17.7 2.7 %shard_map.77 = (bf16[8,256,512]{2,1,0:T(8,128)(2,1)S(1)}, bf16[2,8,256]{2,1,0:T(8,128)(2,1)S(1)}, bf16[8,128,256]{2,1,0:T(8,128)(2,1)S(1)}, bf16[8,128,256]{2,1,0:T(8,128)(2,1)S(1)}) custom-call(s32[8,128]{1,0:T(8,128)S(1)} %get-tuple-element.24.reach, f32[8,3,8,129]{3,2,1,0:T(8,128)S(1)} %get-tuple-element.25.quadrature, bf16[8,128,256]{2,1,0:T(8,128)(2,1)} %field.1, ...), custom_call_target="tpu_custom_call" | custom-call | tf_op jit(solution)/shard_map/pallas_call | solution.py:47
  20.4 0.7 pad_add_fusion.ids
  21.0 0.0 collective-permute-done.4.rest_2_
  21.1 0.0 collective-permute-done.5.rest_3_
  21.1 0.0 collective-permute-done.2.top
  21.1 0.5 collective-permute-done.3.bottom
  21.6 5.8 %shard_map.79 = (bf16[1024,2048]{1,0:T(8,128)(2,1)S(1)}, f32[2,4,2,64,256]{4,3,2,1,0:T(8,128)S(1)}, bf16[2,4,2,64,256]{4,3,2,1,0:T(8,128)(2,1)S(1)}) custom-call(s32[2]{0:T(128)} %pad_add_fusion.ids, bf16[8,256,512]{2,1,0:T(8,128)(2,1)S(1)} %get-tuple-element.26.bands, bf16[8,128,256]{2,1,0:T(8,128)(2,1)S(1)} %get-tuple-element.27.own, ...), custom_call_target="tpu_custom_call" | custom-call | tf_op jit(solution)/shard_map/pallas_call | solution.py:47
  27.4 3.6 %collective-permute-start.10 = (bf16[2,4,2,64,256]{4,3,2,1,0:T(8,128)(2,1)S(1)}, bf16[2,4,2,64,256]{4,3,2,1,0:T(8,128)(2,1)S(1)}, u32[]{:S(2)}, u32[]{:S(2)}) collective-permute-start(bf16[2,4,2,64,256]{4,3,2,1,0:T(8,128)(2,1)S(1)} %get-tuple-element.44), channel_id=1, source_target_pairs={{0,4},{4,0},{8,12},{12,8},{1,5},{5,1},{9,13},{13,9},{2,6},{6,2},{1... | collective-permute-start | bytes 1572872 | tf_op jit(solution)/shard_map/ppermute | solution.py:490
  31.0 1.5 %collective-permute-done.10 = bf16[2,4,2,64,256]{4,3,2,1,0:T(8,128)(2,1)S(1)} collective-permute-done((bf16[2,4,2,64,256]{4,3,2,1,0:T(8,128)(2,1)S(1)}, bf16[2,4,2,64,256]{4,3,2,1,0:T(8,128)(2,1)S(1)}, u32[]{:S(2)}, u32[]{:S(2)}) %collective-permute-start.10) | collective-permute-done | bytes 524320 | tf_op jit(solution)/shard_map/ppermute | solution.py:490
  32.5 0.0 copy-start
  32.5 0.1 convert_add_fusion
  32.7 1.1 %collective-permute-start.11 = (bf16[1,4,2,64,256]{4,3,2,1,0:T(8,128)(2,1)S(1)}, bf16[1,4,2,64,256]{4,3,2,1,0:T(8,128)(2,1)S(1)}, u32[]{:S(2)}, u32[]{:S(2)}) collective-permute-start(bf16[1,4,2,64,256]{4,3,2,1,0:T(8,128)(2,1)S(1)} %slice.51), channel_id=1, source_target_pairs={{0,8},{4,12},{8,0},{12,4},{1,9},{5,13},{9,1},{13,5},{2,10},{6,14},... | collective-permute-start | bytes 786440 | tf_op jit(solution)/shard_map/ppermute | solution.py:490
  33.8 7.6 %collective-permute-done.11 = bf16[1,4,2,64,256]{4,3,2,1,0:T(8,128)(2,1)S(1)} collective-permute-done((bf16[1,4,2,64,256]{4,3,2,1,0:T(8,128)(2,1)S(1)}, bf16[1,4,2,64,256]{4,3,2,1,0:T(8,128)(2,1)S(1)}, u32[]{:S(2)}, u32[]{:S(2)}) %collective-permute-start.11) | collective-permute-done | bytes 262176 | tf_op jit(solution)/shard_map/ppermute | solution.py:490
  41.4 0.1 fusion.5
  41.5 1.8 %collective-permute-start.14 = (bf16[2,64,256]{2,1,0:T(8,128)(2,1)S(1)}, bf16[2,64,256]{2,1,0:T(8,128)(2,1)S(1)}, u32[]{:S(2)}, u32[]{:S(2)}) collective-permute-start(bf16[2,64,256]{2,1,0:T(8,128)(2,1)S(1)} %get-tuple-element.48), channel_id=1, source_target_pairs={{0,3},{1,0},{2,1},{3,2},{4,7},{5,4},{6,5},{7,6},{8,11},{9,8},{10,9... | collective-permute-start | bytes 196616 | tf_op jit(solution)/shard_map/ppermute | solution.py:501
  43.2 0.3 collective-permute-start.13
  43.6 0.7 collective-permute-start.12
  44.2 1.2 %shard_map.81 = (bf16[8,64,256]{2,1,0:T(8,128)(2,1)S(1)}, bf16[8,64,256]{2,1,0:T(8,128)(2,1)S(1)}, bf16[2,128,256]{2,1,0:T(8,128)(2,1)S(1)}) custom-call(bf16[8,128,256]{2,1,0:T(8,128)(2,1)} %array.3), custom_call_target="tpu_custom_call" | custom-call | tf_op jit(solution)/shard_map/pallas_call | solution.py:47
  45.4 2.5 %collective-permute-start.6 = (bf16[8,64,256]{2,1,0:T(8,128)(2,1)S(1)}, bf16[8,64,256]{2,1,0:T(8,128)(2,1)S(1)}, u32[]{:S(2)}, u32[]{:S(2)}) collective-permute-start(bf16[8,64,256]{2,1,0:T(8,128)(2,1)S(1)} %get-tuple-element.38), channel_id=1, source_target_pairs={{0,1},{1,2},{2,3},{3,0},{4,5},{5,6},{6,7},{7,4},{8,9},{9,10},{10,1... | collective-permute-start | bytes 786440 | tf_op jit(solution)/shard_map/ppermute | solution.py:523
  47.9 1.3 %collective-permute-start.7 = (bf16[8,64,256]{2,1,0:T(8,128)(2,1)S(1)}, bf16[8,64,256]{2,1,0:T(8,128)(2,1)S(1)}, u32[]{:S(2)}, u32[]{:S(2)}) collective-permute-start(bf16[8,64,256]{2,1,0:T(8,128)(2,1)S(1)} %get-tuple-element.39), channel_id=1, source_target_pairs={{0,3},{1,0},{2,1},{3,2},{4,7},{5,4},{6,5},{7,6},{8,11},{9,8},{10,9... | collective-permute-start | bytes 786440 | tf_op jit(solution)/shard_map/ppermute | solution.py:524
  49.3 0.0 collective-permute-done.14
  49.3 6.4 %collective-permute-done.13 = bf16[2,64,256]{2,1,0:T(8,128)(2,1)S(1)} collective-permute-done((bf16[2,64,256]{2,1,0:T(8,128)(2,1)S(1)}, bf16[2,64,256]{2,1,0:T(8,128)(2,1)S(1)}, u32[]{:S(2)}, u32[]{:S(2)}) %collective-permute-start.13) | collective-permute-done | bytes 65568 | tf_op jit(solution)/shard_map/ppermute | solution.py:501
  55.7 0.0 collective-permute-done.12
  55.7 0.5 collective-permute-start.15
  56.3 0.2 collective-permute-done.6.left
  56.4 4.8 %collective-permute-done.7.right = bf16[8,64,256]{2,1,0:T(8,128)(2,1)S(1)} collective-permute-done((bf16[8,64,256]{2,1,0:T(8,128)(2,1)S(1)}, bf16[8,64,256]{2,1,0:T(8,128)(2,1)S(1)}, u32[]{:S(2)}, u32[]{:S(2)}) %collective-permute-start.7) | collective-permute-done | bytes 262176 | tf_op jit(solution)/shard_map/ppermute | solution.py:524
  61.3 1.9 %collective-permute-start.8 = (bf16[264,256]{1,0:T(8,128)(2,1)S(1)}, bf16[264,256]{1,0:T(8,128)(2,1)S(1)}, u32[]{:S(2)}, u32[]{:S(2)}) collective-permute-start(bf16[264,256]{1,0:T(8,128)(2,1)S(1)} %get-tuple-element.41), channel_id=1, source_target_pairs={{0,4},{4,8},{8,12},{1,5},{5,9},{9,13},{2,6},{6,10},{10,14},{3,7},{... | collective-permute-start | bytes 405512 | tf_op jit(solution)/shard_map/ppermute | solution.py:528
  63.2 1.3 %collective-permute-start.9 = (bf16[264,256]{1,0:T(8,128)(2,1)S(1)}, bf16[264,256]{1,0:T(8,128)(2,1)S(1)}, u32[]{:S(2)}, u32[]{:S(2)}) collective-permute-start(bf16[264,256]{1,0:T(8,128)(2,1)S(1)} %get-tuple-element.42), channel_id=1, source_target_pairs={{4,0},{8,4},{12,8},{5,1},{9,5},{13,9},{6,2},{10,6},{14,10},{7,3},{... | collective-permute-start | bytes 405512 | tf_op jit(solution)/shard_map/ppermute | solution.py:529
  64.5 0.0 collective-permute-done.15
  64.6 1.5 %collective-permute-start.16 = (bf16[2,2,64,256]{3,2,1,0:T(8,128)(2,1)S(1)}, bf16[2,2,64,256]{3,2,1,0:T(8,128)(2,1)S(1)}, u32[]{:S(2)}, u32[]{:S(2)}) collective-permute-start(bf16[2,2,64,256]{3,2,1,0:T(8,128)(2,1)S(1)} %pad_maximum_fusion.mine), channel_id=1, source_target_pairs={{0,4},{4,0},{8,12},{12,8},{1,5},{5,1},{9,13},{13,9},{2,6},{6,2},{1... | collective-permute-start | bytes 393224 | tf_op jit(solution)/shard_map/ppermute | solution.py:506
  66.1 0.0 copy-done
  66.1 2.0 %shard_map.80 = bf16[1024,256]{1,0:T(8,128)(2,1)} custom-call(bf16[1024,2048]{1,0:T(8,128)(2,1)S(1)} %get-tuple-element.36.filt, bf16[2048,256]{1,0:T(8,128)(2,1)S(1)} %bitcast.26), custom_call_target="tpu_custom_call" | custom-call | tf_op jit(solution)/shard_map/pallas_call | solution.py:47
  68.1 4.2 %shard_map.83.inner = bf16[8,768,256]{2,1,0:T(8,128)(2,1)S(1)} custom-call(bf16[8,256,512]{2,1,0:T(8,128)(2,1)S(1)} %get-tuple-element.26.bands, bf16[8,128,256]{2,1,0:T(8,128)(2,1)S(1)} %get-tuple-element.33.own, bf16[8,64,256]{2,1,0:T(8,128)(2,1)S(1)} %collective-permute-done.6.left, bf16[8,64,256]{2,1,0:T(8,128)(2,1)S(1)} %collective-permute-done.7.right), custom_call_target="tpu_custom_call" | custom-call | tf_op jit(solution)/shard_map/pallas_call | solution.py:47
  72.4 0.0 collective-permute-done.8.top
  72.4 0.0 collective-permute-done.9.bottom
  72.4 4.1 %shard_map.84 = bf16[8,128,256]{2,1,0:T(8,128)(2,1)} custom-call(bf16[8,256,512]{2,1,0:T(8,128)(2,1)S(1)} %get-tuple-element.26.bands, bf16[264,256]{1,0:T(8,128)(2,1)S(1)} %collective-permute-done.8.top, bf16[264,256]{1,0:T(8,128)(2,1)S(1)} %collective-permute-done.9.bottom, bf16[8,256,256]{2,1,0:T(8,128)(2,1)S(1)} %copy-done, ...), custom_call_target="tpu_custom_call" | custom-call | tf_op jit(solution)/shard_map/pallas_call | solution.py:47
  76.5 0.0 collective-permute-done.16.other
  76.5 1.5 %shard_map.85 = f32[2,256,256]{2,1,0:T(8,128)} custom-call(s32[2]{0:T(128)} %pad_add_fusion.ids, bf16[2,2,64,256]{3,2,1,0:T(8,128)(2,1)S(1)} %pad_maximum_fusion.mine, bf16[2,2,64,256]{3,2,1,0:T(8,128)(2,1)S(1)} %collective-permute-done.16.other), custom_call_target="tpu_custom_call" | custom-call | tf_op jit(solution)/shard_map/pallas_call | solution.py:47
  (6 shorter events, 0.1 us)
Async XLA Ops:
  2.7 9.5 %collective-permute-start = (bf16[4,64,256]{2,1,0:T(8,128)(2,1)S(1)}, bf16[4,64,256]{2,1,0:T(8,128)(2,1)S(1)}, u32[]{:S(2)}, u32[]{:S(2)}) collective-permute-start(bf16[4,64,256]{2,1,0:T(8,128)(2,1)S(1)} %get-tuple-element.29), channel_id=1, source_target_pairs={{0,1},{1,2},{2,3},{3,0},{4,5},{5,6},{6,7},{7,4},{8,9},{9,10},{10,1... | collective-permute-start | bytes 393224 | tf_op jit(solution)/shard_map/ppermute | solution.py:523
  5.8 9.3 %collective-permute-start.1 = (bf16[4,64,256]{2,1,0:T(8,128)(2,1)S(1)}, bf16[4,64,256]{2,1,0:T(8,128)(2,1)S(1)}, u32[]{:S(2)}, u32[]{:S(2)}) collective-permute-start(bf16[4,64,256]{2,1,0:T(8,128)(2,1)S(1)} %get-tuple-element.30), channel_id=1, source_target_pairs={{0,3},{1,0},{2,1},{3,2},{4,7},{5,4},{6,5},{7,6},{8,11},{9,8},{10,9... | collective-permute-start | bytes 393224 | tf_op jit(solution)/shard_map/ppermute | solution.py:524
  7.9 13.2 %collective-permute-start.4 = (bf16[4,64,256]{2,1,0:T(8,128)(2,1)S(1)}, bf16[4,64,256]{2,1,0:T(8,128)(2,1)S(1)}, u32[]{:S(2)}, u32[]{:S(2)}) collective-permute-start(bf16[4,64,256]{2,1,0:T(8,128)(2,1)S(1)} %get-tuple-element.34), channel_id=1, source_target_pairs={{0,1},{1,2},{2,3},{3,0},{4,5},{5,6},{6,7},{7,4},{8,9},{9,10},{10,1... | collective-permute-start | bytes 393224 | tf_op jit(solution)/shard_map/ppermute | solution.py:523
  7.9 13.2 %collective-permute-start.5 = (bf16[4,64,256]{2,1,0:T(8,128)(2,1)S(1)}, bf16[4,64,256]{2,1,0:T(8,128)(2,1)S(1)}, u32[]{:S(2)}, u32[]{:S(2)}) collective-permute-start(bf16[4,64,256]{2,1,0:T(8,128)(2,1)S(1)} %get-tuple-element.35), channel_id=1, source_target_pairs={{0,3},{1,0},{2,1},{3,2},{4,7},{5,4},{6,5},{7,6},{8,11},{9,8},{10,9... | collective-permute-start | bytes 393224 | tf_op jit(solution)/shard_map/ppermute | solution.py:524
  15.1 6.0 %collective-permute-start.2 = (bf16[256,256]{1,0:T(8,128)(2,1)S(1)}, bf16[256,256]{1,0:T(8,128)(2,1)S(1)}, u32[]{:S(2)}, u32[]{:S(2)}) collective-permute-start(bf16[256,256]{1,0:T(8,128)(2,1)S(1)} %get-tuple-element.31), channel_id=1, source_target_pairs={{0,4},{4,8},{8,12},{1,5},{5,9},{9,13},{2,6},{6,10},{10,14},{3,7},{... | collective-permute-start | bytes 393224 | tf_op jit(solution)/shard_map/ppermute | solution.py:528
  16.4 5.2 %collective-permute-start.3 = (bf16[256,256]{1,0:T(8,128)(2,1)S(1)}, bf16[256,256]{1,0:T(8,128)(2,1)S(1)}, u32[]{:S(2)}, u32[]{:S(2)}) collective-permute-start(bf16[256,256]{1,0:T(8,128)(2,1)S(1)} %get-tuple-element.32), channel_id=1, source_target_pairs={{4,0},{8,4},{12,8},{5,1},{9,5},{13,9},{6,2},{10,6},{14,10},{7,3},{... | collective-permute-start | bytes 393224 | tf_op jit(solution)/shard_map/ppermute | solution.py:529
  27.4 5.1 %collective-permute-start.10 = (bf16[2,4,2,64,256]{4,3,2,1,0:T(8,128)(2,1)S(1)}, bf16[2,4,2,64,256]{4,3,2,1,0:T(8,128)(2,1)S(1)}, u32[]{:S(2)}, u32[]{:S(2)}) collective-permute-start(bf16[2,4,2,64,256]{4,3,2,1,0:T(8,128)(2,1)S(1)} %get-tuple-element.44), channel_id=1, source_target_pairs={{0,4},{4,0},{8,12},{12,8},{1,5},{5,1},{9,13},{13,9},{2,6},{6,2},{1... | collective-permute-start | bytes 1572872 | tf_op jit(solution)/shard_map/ppermute | solution.py:490
  32.5 33.6 %copy-start = (bf16[8,256,256]{2,1,0:T(8,128)(2,1)S(1)}, bf16[8,256,256]{2,1,0:T(8,128)(2,1)}, u32[]{:S(2)}) copy-start(bf16[8,256,256]{2,1,0:T(8,128)(2,1)} %mixing.1) | copy-start | bytes 3145732
  32.7 8.7 %collective-permute-start.11 = (bf16[1,4,2,64,256]{4,3,2,1,0:T(8,128)(2,1)S(1)}, bf16[1,4,2,64,256]{4,3,2,1,0:T(8,128)(2,1)S(1)}, u32[]{:S(2)}, u32[]{:S(2)}) collective-permute-start(bf16[1,4,2,64,256]{4,3,2,1,0:T(8,128)(2,1)S(1)} %slice.51), channel_id=1, source_target_pairs={{0,8},{4,12},{8,0},{12,4},{1,9},{5,13},{9,1},{13,5},{2,10},{6,14},... | collective-permute-start | bytes 786440 | tf_op jit(solution)/shard_map/ppermute | solution.py:490
  41.5 7.8 %collective-permute-start.14 = (bf16[2,64,256]{2,1,0:T(8,128)(2,1)S(1)}, bf16[2,64,256]{2,1,0:T(8,128)(2,1)S(1)}, u32[]{:S(2)}, u32[]{:S(2)}) collective-permute-start(bf16[2,64,256]{2,1,0:T(8,128)(2,1)S(1)} %get-tuple-element.48), channel_id=1, source_target_pairs={{0,3},{1,0},{2,1},{3,2},{4,7},{5,4},{6,5},{7,6},{8,11},{9,8},{10,9... | collective-permute-start | bytes 196616 | tf_op jit(solution)/shard_map/ppermute | solution.py:501
  43.2 12.5 %collective-permute-start.13 = (bf16[2,64,256]{2,1,0:T(8,128)(2,1)S(1)}, bf16[2,64,256]{2,1,0:T(8,128)(2,1)S(1)}, u32[]{:S(2)}, u32[]{:S(2)}) collective-permute-start(bf16[2,64,256]{2,1,0:T(8,128)(2,1)S(1)} %get-tuple-element.49), channel_id=1, source_target_pairs={{0,2},{1,3},{2,0},{3,1},{4,6},{5,7},{6,4},{7,5},{8,10},{9,11},{10,... | collective-permute-start | bytes 196616 | tf_op jit(solution)/shard_map/ppermute | solution.py:501
  43.6 12.1 %collective-permute-start.12 = (bf16[2,64,256]{2,1,0:T(8,128)(2,1)S(1)}, bf16[2,64,256]{2,1,0:T(8,128)(2,1)S(1)}, u32[]{:S(2)}, u32[]{:S(2)}) collective-permute-start(bf16[2,64,256]{2,1,0:T(8,128)(2,1)S(1)} %get-tuple-element.47), channel_id=1, source_target_pairs={{0,1},{1,2},{2,3},{3,0},{4,5},{5,6},{6,7},{7,4},{8,9},{9,10},{10,1... | collective-permute-start | bytes 196616 | tf_op jit(solution)/shard_map/ppermute | solution.py:501
  45.4 11.0 %collective-permute-start.6 = (bf16[8,64,256]{2,1,0:T(8,128)(2,1)S(1)}, bf16[8,64,256]{2,1,0:T(8,128)(2,1)S(1)}, u32[]{:S(2)}, u32[]{:S(2)}) collective-permute-start(bf16[8,64,256]{2,1,0:T(8,128)(2,1)S(1)} %get-tuple-element.38), channel_id=1, source_target_pairs={{0,1},{1,2},{2,3},{3,0},{4,5},{5,6},{6,7},{7,4},{8,9},{9,10},{10,1... | collective-permute-start | bytes 786440 | tf_op jit(solution)/shard_map/ppermute | solution.py:523
  47.9 13.3 %collective-permute-start.7 = (bf16[8,64,256]{2,1,0:T(8,128)(2,1)S(1)}, bf16[8,64,256]{2,1,0:T(8,128)(2,1)S(1)}, u32[]{:S(2)}, u32[]{:S(2)}) collective-permute-start(bf16[8,64,256]{2,1,0:T(8,128)(2,1)S(1)} %get-tuple-element.39), channel_id=1, source_target_pairs={{0,3},{1,0},{2,1},{3,2},{4,7},{5,4},{6,5},{7,6},{8,11},{9,8},{10,9... | collective-permute-start | bytes 786440 | tf_op jit(solution)/shard_map/ppermute | solution.py:524
  55.7 8.8 %collective-permute-start.15 = (bf16[1,2,64,256]{3,2,1,0:T(8,128)(2,1)S(1)}, bf16[1,2,64,256]{3,2,1,0:T(8,128)(2,1)S(1)}, u32[]{:S(2)}, u32[]{:S(2)}) collective-permute-start(bf16[1,2,64,256]{3,2,1,0:T(8,128)(2,1)S(1)} %fusion.4), channel_id=1, source_target_pairs={{0,8},{4,12},{8,0},{12,4},{1,9},{5,13},{9,1},{13,5},{2,10},{6,14},... | collective-permute-start | bytes 196616 | tf_op jit(solution)/shard_map/ppermute | solution.py:506
  61.3 11.1 %collective-permute-start.8 = (bf16[264,256]{1,0:T(8,128)(2,1)S(1)}, bf16[264,256]{1,0:T(8,128)(2,1)S(1)}, u32[]{:S(2)}, u32[]{:S(2)}) collective-permute-start(bf16[264,256]{1,0:T(8,128)(2,1)S(1)} %get-tuple-element.41), channel_id=1, source_target_pairs={{0,4},{4,8},{8,12},{1,5},{5,9},{9,13},{2,6},{6,10},{10,14},{3,7},{... | collective-permute-start | bytes 405512 | tf_op jit(solution)/shard_map/ppermute | solution.py:528
  63.2 9.2 %collective-permute-start.9 = (bf16[264,256]{1,0:T(8,128)(2,1)S(1)}, bf16[264,256]{1,0:T(8,128)(2,1)S(1)}, u32[]{:S(2)}, u32[]{:S(2)}) collective-permute-start(bf16[264,256]{1,0:T(8,128)(2,1)S(1)} %get-tuple-element.42), channel_id=1, source_target_pairs={{4,0},{8,4},{12,8},{5,1},{9,5},{13,9},{6,2},{10,6},{14,10},{7,3},{... | collective-permute-start | bytes 405512 | tf_op jit(solution)/shard_map/ppermute | solution.py:529
  64.6 11.9 %collective-permute-start.16 = (bf16[2,2,64,256]{3,2,1,0:T(8,128)(2,1)S(1)}, bf16[2,2,64,256]{3,2,1,0:T(8,128)(2,1)S(1)}, u32[]{:S(2)}, u32[]{:S(2)}) collective-permute-start(bf16[2,2,64,256]{3,2,1,0:T(8,128)(2,1)S(1)} %pad_maximum_fusion.mine), channel_id=1, source_target_pairs={{0,4},{4,0},{8,12},{12,8},{1,5},{5,1},{9,13},{13,9},{2,6},{6,2},{1... | collective-permute-start | bytes 393224 | tf_op jit(solution)/shard_map/ppermute | solution.py:506

commit v3 on v2

--- a/solution.py
+++ b/solution.py
@@ -16,11 +16,6 @@
 def ring(axis, distance):
     count = lax.axis_size(axis)
     return [(i, (i + distance) % count) for i in range(count)]
-
-
-def line(axis, distance):
-    count = lax.axis_size(axis)
-    return [(i, i + distance) for i in range(count) if 0 <= i + distance < count]
 
 
 def swap(axis, mask):
@@ -159,12 +154,15 @@
         copy.wait()
 
 
-def first_kernel(groups, half_width, array, quadrature, *refs):
-    *outs, edges, taps_near, reach, sems = refs
+def second_kernel(groups, half_width, array, quadrature, *refs):
+    *outs, edges, taps_near, reach, widths, sems = refs
+    first = pltpu.make_async_copy(half_width, widths, sems.at[15])
+    first.start()
 
     def spread_reach():
+        first.wait()
         for row in range(reach.shape[0]):
-            reach[row : row + 1, :] = jnp.full((1, LANES), half_width[row], jnp.int32)
+            reach[row : row + 1, :] = jnp.full((1, LANES), widths[row], jnp.int32)
 
     copies = rim_copies(groups, array, outs, edges)
     run_copies(copies + [(quadrature, taps_near)], sems, spread_reach)
@@ -183,18 +181,17 @@
     return outs + [pltpu.VMEM((2, cols, chans), jnp.bfloat16)]
 
 
-def first_rims(half_width, array, quadrature, rim, groups):
+def second_rims(half_width, array, quadrature, rim, groups):
     outs = rim_shapes(array, rim, groups)
     outs.append(pltpu.VMEM(quadrature.shape, jnp.float32))
     outs.append(pltpu.VMEM((half_width.shape[0], LANES), jnp.int32))
     return kernel_call(
-        functools.partial(first_kernel, groups),
+        functools.partial(second_kernel, groups),
         [half_width, array, quadrature],
         outs,
-        [pltpu.SemaphoreType.DMA((16,))],
+        [pltpu.SMEM(half_width.shape, jnp.int32), pltpu.SemaphoreType.DMA((16,))],
         6,
-        scalars=1,
-        far=(1, 2),
+        far=(0, 1, 2),
     )
 
 
@@ -209,13 +206,20 @@
     )
 
 
+def even_band():
+    return lax.rem(lax.axis_index("lat"), 2) == 0
+
+
 def edges_kernel(picks, own, left, right, *rest):
-    *basis, bottom_row, top_row = rest
+    *basis, core_row, far_row = rest
     rim, cols = left.shape[1], own.shape[1]
-    for i, out in ((1, bottom_row), (0, top_row)):
-        out[0:rim] = left[picks[i]]
+    even = even_band()
+    for out, last in ((core_row, even), (far_row, jnp.logical_not(even))):
+        i = jnp.where(last, 1, 0)
+        pick = jnp.where(last, picks[1], picks[0])
+        out[0:rim] = left[pick]
         out[rim : rim + cols] = own[i]
-        out[rim + cols : 2 * rim + cols] = right[picks[i]]
+        out[rim + cols : 2 * rim + cols] = right[pick]
         if basis:
             out[2 * rim + cols :] = basis[0][1 - i]
 
@@ -229,12 +233,13 @@
     )
 
 
-def fill_extended(ext, own, top, bottom, groups, sides):
+def fill_extended(ext, own, core, far, groups, sides):
     rows, cols = own.shape[0], own.shape[1]
     rim = sides[0].shape[1]
     span = ext.shape[1]
-    ext[0] = top[0:span]
-    ext[rows + 1] = bottom[0:span]
+    even = even_band()
+    ext[jnp.where(even, rows + 1, 0)] = core[0:span]
+    ext[jnp.where(even, 0, rows + 1)] = far[0:span]
     ext[1 : rows + 1, rim : rim + cols, :] = own[...]
     for g, group in enumerate(groups):
         for i, row in enumerate(group):
@@ -246,32 +251,26 @@
     rows, height, total = bands.shape
     reach = ext.shape[1] - cols + BLOCK
     spare = total - 3 * reach
-
-    def one(row, carry):
-        for g in range(cols // BLOCK):
-            first = g * BLOCK
+    for row in range(rows):
+        for first in range(0, cols, BLOCK):
             pieces = [ext[row + r, first : first + reach, :] for r in range(3)]
             if spare:
                 pieces.append(ext[row, 0:spare, :])
             source = jnp.concatenate(pieces, axis=0)
             result = jnp.dot(bands[row], source, preferred_element_type=jnp.float32)
             result = result.astype(jnp.bfloat16)
-            start = pl.multiple_of(row * cols + first, BLOCK)
             for k in range(height // BLOCK):
-                write(start, k, result[k * BLOCK : (k + 1) * BLOCK])
-        return carry
-
-    lax.fori_loop(0, rows, one, 0)
-
-
-def forward_kernel(n_lat, groups, ids, bands, own, top, bottom, cot, *rest):
+                write(row * cols + first, k, result[k * BLOCK : (k + 1) * BLOCK])
+
+
+def forward_kernel(groups, bands, own, core, far, cot, *rest):
     *sides, filt, keep, send, ext, grad = rest
     _, cols, chans = own.shape
     kernels = grad.shape[0]
-    fill_extended(ext, own, top, bottom, groups, sides)
+    fill_extended(ext, own, core, far, groups, sides)
 
     def write(start, k, value):
-        filt[pl.ds(start, BLOCK), k * chans : (k + 1) * chans] = value
+        filt[start : start + BLOCK, k * chans : (k + 1) * chans] = value
 
     filter_rows(bands, ext, cols, write)
     for k in range(kernels):
@@ -281,28 +280,23 @@
             (((0,), (0,)), ((), ())),
             preferred_element_type=jnp.float32,
         )
-    lat, lon = ids[0], ids[1]
-    n_lon, share, piece = keep.shape[1], keep.shape[2], keep.shape[3]
-    bits = n_lat.bit_length() - 1
-    for m in range(n_lat):
-        slot = sum(((m >> b) & 1) << (bits - 1 - b) for b in range(bits))
-        start = pl.multiple_of((lat ^ slot) * piece, piece)
+    lat, lon = lax.axis_index("lat"), lax.axis_index("lon")
+    n_lon, share, piece = keep.shape[0], keep.shape[1], keep.shape[2]
+    for slot, out in ((0, keep), (1, send)):
+        start = pl.multiple_of((lax.rem(lat, 2) ^ slot) * piece, piece)
         for s in range(n_lon):
             first = lax.rem(lon + s, n_lon) * share
             value = grad[pl.ds(first, share), pl.ds(start, piece), :]
-            if m < n_lat // 2:
-                keep[m, s] = value
-            else:
-                send[m - n_lat // 2, s] = value.astype(send.dtype)
-
-
-def forward(ids, bands, own, top, bottom, cot, groups, sides, kernels, n_lat, n_lon):
+            out[s] = value.astype(out.dtype)
+
+
+def forward(bands, own, core, far, cot, groups, sides, kernels, n_lon):
     rows, cols, chans = own.shape
     rim = sides[0].shape[1]
-    parts = (n_lat // 2, n_lon, kernels // n_lon, chans // n_lat, chans)
-    return kernel_call(
-        functools.partial(forward_kernel, n_lat, groups),
-        [ids, bands, own, top, bottom, cot, *sides],
+    parts = (n_lon, kernels // n_lon, chans // 2, cot.shape[1])
+    return kernel_call(
+        functools.partial(forward_kernel, groups),
+        [bands, own, core, far, cot, *sides],
         [
             pltpu.VMEM((rows * cols, kernels * chans), jnp.bfloat16),
             pltpu.VMEM(parts, jnp.float32),
@@ -313,7 +307,6 @@
             pltpu.VMEM((kernels, chans, chans), jnp.float32),
         ],
         20,
-        scalars=1,
     )
 
 
@@ -363,28 +356,19 @@
     rows, cols, _ = own.shape
     flip = mirror(reverse.shape[1])
 
-    def turn(row, carry):
+    for row in range(rows):
         line = jnp.concatenate([left[row], own[row], right[row]], axis=0)
         reverse[row] = jnp.dot(flip, line, preferred_element_type=jnp.float32).astype(
             reverse.dtype
         )
-        return carry
-
-    lax.fori_loop(0, rows, turn, 0)
-
-    def one(step, carry):
-        row = step + 1
+    for row in range(1, rows - 1):
         band = adjoint_band(window, bands[row - 1], bands[row], bands[row + 1])
-        base = step * cols
-
-        def write(first, k, value):
-            filt[k, pl.ds(pl.multiple_of(base + first, BLOCK), BLOCK), :] = value
+
+        def write(first, k, value, base=(row - 1) * cols):
+            filt[k, base + first : base + first + BLOCK, :] = value
 
         lines = [reverse.at[row + 1], reverse.at[row], reverse.at[row - 1]]
         adjoint_row(band, lines, cols, write)
-        return carry
-
-    lax.fori_loop(0, rows - 2, one, 0)
 
 
 def backward_inner(bands, own, left, right, window):
@@ -401,20 +385,20 @@
 
 
 def backward_edges_kernel(
-    window, bands, top, bottom, mixing, left, right, own, inner, out, reverse, extra, filt
+    window, bands, core, far, mixing, left, right, own, inner, out, reverse, extra, filt
 ):
     rows, cols, _ = own.shape
     span = reverse.shape[1]
     flip = mirror(span)
-    lines = [top[0:span]]
-    for row in (0, 1, rows - 2, rows - 1):
-        lines.append(jnp.concatenate([left[row], own[row], right[row]], axis=0))
-    lines.append(bottom[0:span])
-    for i, line in enumerate(lines):
+    even = even_band()
+    lines = [(jnp.where(even, 5, 0), core[0:span]), (jnp.where(even, 0, 5), far[0:span])]
+    for i, row in enumerate((0, 1, rows - 2, rows - 1)):
+        lines.append((i + 1, jnp.concatenate([left[row], own[row], right[row]], axis=0)))
+    for i, line in lines:
         reverse[i] = jnp.dot(flip, line, preferred_element_type=jnp.float32).astype(reverse.dtype)
-    none = jnp.zeros((top.shape[0] - span, 2 * LANES), jnp.float32)
-    above = top[span:, :].astype(jnp.float32)
-    below = bottom[span:, :].astype(jnp.float32)
+    none = jnp.zeros((core.shape[0] - span, 2 * LANES), jnp.float32)
+    beside, across = core[span:, :].astype(jnp.float32), far[span:, :].astype(jnp.float32)
+    above, below = jnp.where(even, across, beside), jnp.where(even, beside, across)
     spread_bands(packed_taps([none, none, above], window, bands.shape[2]), extra, 0)
     spread_bands(packed_taps([below, none, none], window, bands.shape[2]), extra, 1)
     picks = (
@@ -443,13 +427,13 @@
             out[row] = part.astype(out.dtype)
 
 
-def backward_edges(bands, top, bottom, mixing, left, right, own, inner, window):
+def backward_edges(bands, core, far, mixing, left, right, own, inner, window):
     rows, cols, outs = own.shape
     span = cols + 2 * left.shape[1]
     kernels, chans, _ = mixing.shape
     return kernel_call(
         functools.partial(backward_edges_kernel, window),
-        [bands, top, bottom, mixing, left, right, own, inner],
+        [bands, core, far, mixing, left, right, own, inner],
         jax.ShapeDtypeStruct((rows, cols, chans), jnp.bfloat16),
         [
             pltpu.VMEM((6, span, outs), jnp.bfloat16),
@@ -460,53 +444,40 @@
     )
 
 
-def assemble_kernel(ids, mine, other, out):
-    half, _, piece, _ = mine.shape
-    count = 2 * half
-    bits = count.bit_length() - 1
-    for slot in range(count):
-        m = sum(((slot >> b) & 1) << (bits - 1 - b) for b in range(bits))
-        source = mine[m] if m < half else other[m - half]
-        start = pl.multiple_of((ids[0] ^ slot) * piece, piece)
-        out[:, pl.ds(start, piece), :] = source.astype(out.dtype)
-
-
-def assemble(ids, mine, other):
-    half, share, piece, chans = mine.shape
+def assemble_kernel(mine, other, out):
+    _, piece, _ = mine.shape
+    for slot, source in ((0, mine), (1, other)):
+        start = pl.multiple_of((lax.rem(lax.axis_index("lat"), 2) ^ slot) * piece, piece)
+        out[:, pl.ds(start, piece), :] = source[...].astype(out.dtype)
+
+
+def assemble(mine, other):
+    share, piece, chans = mine.shape
     return kernel_call(
         assemble_kernel,
-        [ids, mine, other],
-        jax.ShapeDtypeStruct((share, 2 * half * piece, chans), jnp.float32),
+        [mine, other],
+        jax.ShapeDtypeStruct((share, 2 * piece, chans), jnp.float32),
         [],
         4,
-        scalars=1,
-    )
-
-
-def reduced_gradient(ids, keep, send):
+    )
+
+
+def reduced_gradient(keep, send):
     n_lat, n_lon = lax.axis_size("lat"), lax.axis_size("lon")
-    mask = 1
-    while True:
-        other = lax.ppermute(send, "lat", swap("lat", mask))
-        total = keep + other.astype(jnp.float32)
-        mask *= 2
-        if mask >= n_lat:
-            break
-        half = total.shape[0] // 2
-        keep, send = total[:half], total[half:].astype(jnp.bfloat16)
-    total = total[0]
+    total = keep + lax.ppermute(send, "lat", swap("lat", 1)).astype(jnp.float32)
     wire = total.astype(jnp.bfloat16)
     piece = total[0]
     for s in range(1, n_lon):
         other = lax.ppermute(wire[s], "lon", ring("lon", s))
         piece = piece + other.astype(jnp.float32)
-    pieces = piece.astype(jnp.bfloat16)[None]
-    while mask > 1:
-        mask //= 2
-        other = lax.ppermute(pieces, "lat", swap("lat", mask))
-        if mask > 1:
-            pieces = jnp.concatenate([pieces, other], axis=0)
-    return assemble(ids, pieces, other)
+    mask = 2
+    while mask < n_lat:
+        mine = piece.astype(jnp.bfloat16)
+        other = lax.ppermute(mine, "lat", swap("lat", mask))
+        piece = mine.astype(jnp.float32) + other.astype(jnp.float32)
+        mask *= 2
+    mine = piece.astype(jnp.bfloat16)
+    return assemble(mine, lax.ppermute(mine, "lat", swap("lat", 1)))
 
 
 def on_device(field_in, quadrature, half_width, mixing, cotangent):
@@ -514,8 +485,7 @@
     kernels, _, outs = mixing.shape
     taps = quadrature.shape[-1]
     rim = (taps - 1) // 2
-    n_lat, n_lon = lax.axis_size("lat"), lax.axis_size("lon")
-    ids = jnp.stack([lax.axis_index("lat"), lax.axis_index("lon")]).astype(jnp.int32)
+    n_lon = lax.axis_size("lon")
     groups = split_rows(rows)
     outer = groups[0]
 
@@ -525,39 +495,38 @@
         return [left, right]
 
     def bands_beside(pair):
-        top = lax.ppermute(pair[0], "lat", line("lat", 1))
-        bottom = lax.ppermute(pair[1], "lat", line("lat", -1))
-        return top, bottom
+        across = [(i, i + 1) for i in range(1, lax.axis_size("lat") - 1, 2)]
+        far = lax.ppermute(pair[1], "lat", across + [(j, i) for i, j in across])
+        core = lax.ppermute(pair[0], "lat", swap("lat", 1))
+        return core, far
 
     window = taps - 1 + BLOCK
-    *sides, own_edges, taps_near, reach = first_rims(
-        half_width, field_in, quadrature, rim, groups
-    )
+    *sides, own_edges = rims(field_in, rim, groups)
     outer_sides = beside(sides[0:2])
     inner_sides = beside(sides[2:4])
+    *sides, cot_edges, taps_near, reach = second_rims(
+        half_width, cotangent, quadrature, rim, [range(rows)]
+    )
     bands, basis_edges, field_near, cot_near = band_matrices(
         reach, taps_near, field_in, cotangent
     )
     picks = (0, len(outer) - 1)
     sent = edge_rows(own_edges, *outer_sides, picks, [])
-    f_top, f_bottom = bands_beside(sent)
-    *sides, cot_edges = rims(cotangent, rim, [range(rows)])
+    f_core, f_far = bands_beside(sent)
     g_left, g_right = beside(sides)
 
     filtered, keep, send = forward(
-        ids,
         bands,
         field_near,
-        f_top,
-        f_bottom,
+        f_core,
+        f_far,
         cot_near.reshape(rows * cols, outs),
         groups,
         outer_sides + inner_sides,
         kernels,
-        n_lat,
         n_lon,
     )
-    weight_grad = reduced_gradient(ids, keep, send)
+    weight_grad = reduced_gradient(keep, send)
     field_out = kernel_call(
         mix_kernel,
         [filtered, mixing.reshape(kernels * chans, outs)],
@@ -566,10 +535,10 @@
         8,
     )
     sent = edge_rows(cot_edges, g_left, g_right, (0, rows - 1), [basis_edges])
-    g_top, g_bottom = bands_beside(sent)
+    g_core, g_far = bands_beside(sent)
     inner = backward_inner(bands, cot_near, g_left, g_right, window)
     input_grad = backward_edges(
-        bands, g_top, g_bottom, mixing, g_left, g_right, cot_near, inner, window
+        bands, g_core, g_far, mixing, g_left, g_right, cot_near, inner, window
     )
     return (
         field_out.reshape(rows, cols, outs),

time: 78.3 us -> 63.9 us (0.82)
  starting transfers between devices: 28.2 us -> 22.4 us
  Pallas kernels: 23.6 us -> 18 us
  waiting for transfers between devices: 24.5 us -> 21.7 us
    ppermute x3, waiting for transfers between devices: 6.39 us -> 13.5 us  [reduced_gradient(): other = lax.ppermute(wire[s], 'lon', ring('lon', s))]
    ppermute x8 -> x7, starting transfers between devices: 12.5 us -> 5.64 us  [the longest x1 3.16 us: reduced_gradient(): total = keep + lax.ppermute(send, 'lat', swap('lat', 1)).astype(jnp.float32)]
    pallas_call x10, Pallas kernels: 23.6 us -> 18 us  [kernel_call(): pl.pallas_call(body, in_specs=specs, out_specs=place if single else [plac...]
    ppermute x8 -> x7, waiting for transfers between devices: 9.67 us -> 4.12 us  [the longest x1 2.57 us: reduced_gradient(): other = lax.ppermute(mine, 'lat', swap('lat', mask))]
    ppermute x3, waiting for transfers between devices: 7.74 us -> 3.67 us  [beside(): right = lax.ppermute(pair[1], 'lon', ring('lon', -1))]
    ppermute x3, starting transfers between devices: 5.64 us -> 3.67 us  [beside(): left = lax.ppermute(pair[0], 'lon', ring('lon', 1))]
    ppermute x3, starting transfers between devices: 7.26 us -> 9.17 us  [beside(): right = lax.ppermute(pair[1], 'lon', ring('lon', -1))]
    ppermute x3, starting transfers between devices: 2.77 us -> 3.88 us  [reduced_gradient(): other = lax.ppermute(wire[s], 'lon', ring('lon', s))]
  transfers between devices with their start and end apart: 17 -> 16, of which waited for: 8 -> 8; matrix products, arithmetic and copies ran while one was open for 1% -> 0% of each run, Pallas kernels for 18% -> 19%
where the time goes in v3:
time: 63.9 us; the launch traced here: 63.2 us
  starting transfers between devices  22.4 us (35%)
  waiting for transfers between devices  21.7 us (34%)
  Pallas kernels  18 us (28%)
  between operations  0.81 us (1%)
    pallas_call x10, Pallas kernels, kernel_call(): pl.pallas_call(body, in_specs=specs, out_specs=place if single else [plac...  18 us
    ppermute x3, waiting for transfers between devices, reduced_gradient(): other = lax.ppermute(wire[s], 'lon', ring('lon', s))  13.5 us
    ppermute x3, starting transfers between devices, beside(): right = lax.ppermute(pair[1], 'lon', ring('lon', -1))  9.17 us
    ppermute x3, starting transfers between devices, reduced_gradient(): other = lax.ppermute(wire[s], 'lon', ring('lon', s))  3.88 us
    ppermute x3, starting transfers between devices, beside(): left = lax.ppermute(pair[0], 'lon', ring('lon', 1))  3.67 us
    ppermute x3, waiting for transfers between devices, beside(): right = lax.ppermute(pair[1], 'lon', ring('lon', -1))  3.67 us
    ppermute x1, starting transfers between devices, reduced_gradient(): total = keep + lax.ppermute(send, 'lat', swap('lat', 1)).astype(jnp.float32)  3.16 us
    ppermute x1, waiting for transfers between devices, reduced_gradient(): other = lax.ppermute(mine, 'lat', swap('lat', mask))  2.57 us
  transfers between devices with their start and end apart: 16, of which 8 were waited for; matrix products, arithmetic and copies ran while one was open for 0% of the time, Pallas kernels for 19%

profile of v3, /device:TPU:0, one launch (start us, length us, event | category | flops | bytes accessed | tf_op | source)
XLA Modules:
  0.0 63.2 jit_solution(8063914751885550842)
XLA Ops:
  0.6 1.3 %shard_map.78 = (bf16[4,64,256]{2,1,0:T(8,128)(2,1)S(1)}, bf16[4,64,256]{2,1,0:T(8,128)(2,1)S(1)}, bf16[4,64,256]{2,1,0:T(8,128)(2,1)S(1)}, bf16[4,64,256]{2,1,0:T(8,128)(2,1)S(1)}, bf16[2,128,256]{2,1,0:T(8,128)(2,1)S(1)}) custom-call(bf16[8,128,256]{2,1,0:T(8,128)(2,1)} %array.3), custom_call_target="tpu_custom_call" | custom-call | tf_op jit(solution)/shard_map/pallas_call | solution.py:42
  1.9 3.1 %collective-permute-start = (bf16[4,64,256]{2,1,0:T(8,128)(2,1)S(1)}, bf16[4,64,256]{2,1,0:T(8,128)(2,1)S(1)}, u32[]{:S(2)}, u32[]{:S(2)}) collective-permute-start(bf16[4,64,256]{2,1,0:T(8,128)(2,1)S(1)} %get-tuple-element.29), channel_id=1, source_target_pairs={{0,1},{1,2},{2,3},{3,0},{4,5},{5,6},{6,7},{7,4},{8,9},{9,10},{10,1... | collective-permute-start | bytes 393224 | tf_op jit(solution)/shard_map/ppermute | solution.py:493
  5.0 2.1 %collective-permute-start.1 = (bf16[4,64,256]{2,1,0:T(8,128)(2,1)S(1)}, bf16[4,64,256]{2,1,0:T(8,128)(2,1)S(1)}, u32[]{:S(2)}, u32[]{:S(2)}) collective-permute-start(bf16[4,64,256]{2,1,0:T(8,128)(2,1)S(1)} %get-tuple-element.30), channel_id=1, source_target_pairs={{0,3},{1,0},{2,1},{3,2},{4,7},{5,4},{6,5},{7,6},{8,11},{9,8},{10,9... | collective-permute-start | bytes 393224 | tf_op jit(solution)/shard_map/ppermute | solution.py:494
  7.1 0.0 collective-permute-start.4
  7.1 3.8 %collective-permute-start.5 = (bf16[4,64,256]{2,1,0:T(8,128)(2,1)S(1)}, bf16[4,64,256]{2,1,0:T(8,128)(2,1)S(1)}, u32[]{:S(2)}, u32[]{:S(2)}) collective-permute-start(bf16[4,64,256]{2,1,0:T(8,128)(2,1)S(1)} %get-tuple-element.35), channel_id=1, source_target_pairs={{0,3},{1,0},{2,1},{3,2},{4,7},{5,4},{6,5},{7,6},{8,11},{9,8},{10,9... | collective-permute-start | bytes 393224 | tf_op jit(solution)/shard_map/ppermute | solution.py:494
  10.9 0.5 collective-permute-done.left.rest_0_
  11.4 2.9 %collective-permute-done.1.right.rest_1_ = bf16[4,64,256]{2,1,0:T(8,128)(2,1)S(1)} collective-permute-done((bf16[4,64,256]{2,1,0:T(8,128)(2,1)S(1)}, bf16[4,64,256]{2,1,0:T(8,128)(2,1)S(1)}, u32[]{:S(2)}, u32[]{:S(2)}) %collective-permute-start.1) | collective-permute-done | bytes 131104 | tf_op jit(solution)/shard_map/ppermute | solution.py:494
  14.3 0.1 collective-permute-start.2
  14.4 0.7 %collective-permute-start.3 = (bf16[256,256]{1,0:T(8,128)(2,1)S(1)}, bf16[256,256]{1,0:T(8,128)(2,1)S(1)}, u32[]{:S(2)}, u32[]{:S(2)}) collective-permute-start(bf16[256,256]{1,0:T(8,128)(2,1)S(1)} %get-tuple-element.32), channel_id=1, source_target_pairs={{4,8},{8,4},{5,9},{9,5},{6,10},{10,6},{7,11},{11,7},{20,24},{24,20... | collective-permute-start | bytes 393224 | tf_op jit(solution)/shard_map/ppermute | solution.py:499
  15.1 1.3 %shard_map.76 = (bf16[8,64,256]{2,1,0:T(8,128)(2,1)S(1)}, bf16[8,64,256]{2,1,0:T(8,128)(2,1)S(1)}, bf16[2,128,256]{2,1,0:T(8,128)(2,1)S(1)}, f32[8,3,8,129]{3,2,1,0:T(8,128)S(1)}, s32[8,128]{1,0:T(8,128)S(1)}) custom-call(s32[8]{0:T(128)} %half_width.1, bf16[8,128,256]{2,1,0:T(8,128)(2,1)} %cot.1, f32[8,3,8,129]{3,2,1,0:T(8,128)} %quadrature.1), custom_call_target="tpu_custom_call" | custom-call | tf_op jit(solution)/shard_map/pallas_call | solution.py:42
  16.3 2.7 %shard_map.77 = (bf16[8,256,512]{2,1,0:T(8,128)(2,1)S(1)}, bf16[2,8,256]{2,1,0:T(8,128)(2,1)S(1)}, bf16[8,128,256]{2,1,0:T(8,128)(2,1)S(1)}, bf16[8,128,256]{2,1,0:T(8,128)(2,1)S(1)}) custom-call(s32[8,128]{1,0:T(8,128)S(1)} %get-tuple-element.24.reach, f32[8,3,8,129]{3,2,1,0:T(8,128)S(1)} %get-tuple-element.25.quadrature, bf16[8,128,256]{2,1,0:T(8,128)(2,1)} %array.3, ...), custom_call_target="tpu_custom_call" | custom-call | tf_op jit(solution)/shard_map/pallas_call | solution.py:42
  19.0 0.0 collective-permute-done.4.rest_2_
  19.0 0.0 collective-permute-done.5.rest_3_
  19.0 0.0 collective-permute-done.2.core
  19.1 0.0 collective-permute-done.3.far
  19.1 3.7 %shard_map.80 = (bf16[1024,2048]{1,0:T(8,128)(2,1)S(1)}, f32[4,2,128,256]{3,2,1,0:T(8,128)S(1)}, bf16[4,2,128,256]{3,2,1,0:T(8,128)(2,1)S(1)}) custom-call(bf16[8,256,512]{2,1,0:T(8,128)(2,1)S(1)} %get-tuple-element.26.bands, bf16[8,128,256]{2,1,0:T(8,128)(2,1)S(1)} %get-tuple-element.27.own, bf16[256,256]{1,0:T(8,128)(2,1)S(1)} %collective-permute-done.2.core, ...), custom_call_target="tpu_custom_call" | custom-call | tf_op jit(solution)/shard_map/pallas_call | solution.py:42
  22.8 0.0 copy-start
  22.8 3.2 %collective-permute-start.10 = (bf16[4,2,128,256]{3,2,1,0:T(8,128)(2,1)S(1)}, bf16[4,2,128,256]{3,2,1,0:T(8,128)(2,1)S(1)}, u32[]{:S(2)}, u32[]{:S(2)}) collective-permute-start(bf16[4,2,128,256]{3,2,1,0:T(8,128)(2,1)S(1)} %get-tuple-element.44), channel_id=1, source_target_pairs={{0,4},{4,0},{8,12},{12,8},{1,5},{5,1},{9,13},{13,9},{2,6},{6,2},{1... | collective-permute-start | bytes 1572872 | tf_op jit(solution)/shard_map/ppermute | solution.py:467
  26.0 1.5 %collective-permute-done.10 = bf16[4,2,128,256]{3,2,1,0:T(8,128)(2,1)S(1)} collective-permute-done((bf16[4,2,128,256]{3,2,1,0:T(8,128)(2,1)S(1)}, bf16[4,2,128,256]{3,2,1,0:T(8,128)(2,1)S(1)}, u32[]{:S(2)}, u32[]{:S(2)}) %collective-permute-start.10) | collective-permute-done | bytes 524320 | tf_op jit(solution)/shard_map/ppermute | solution.py:467
  27.5 0.2 fusion.4
  27.7 0.6 collective-permute-start.11
  28.3 3.3 %collective-permute-start.13 = (bf16[2,128,256]{2,1,0:T(8,128)(2,1)S(1)}, bf16[2,128,256]{2,1,0:T(8,128)(2,1)S(1)}, u32[]{:S(2)}, u32[]{:S(2)}) collective-permute-start(bf16[2,128,256]{2,1,0:T(8,128)(2,1)S(1)} %get-tuple-element.48), channel_id=1, source_target_pairs={{0,3},{1,0},{2,1},{3,2},{4,7},{5,4},{6,5},{7,6},{8,11},{9,8},{10,9... | collective-permute-start | bytes 393224 | tf_op jit(solution)/shard_map/ppermute | solution.py:471
  31.6 0.0 collective-permute-start.12
  31.6 0.6 collective-permute-start.6
  32.2 3.3 %collective-permute-start.7 = (bf16[8,64,256]{2,1,0:T(8,128)(2,1)S(1)}, bf16[8,64,256]{2,1,0:T(8,128)(2,1)S(1)}, u32[]{:S(2)}, u32[]{:S(2)}) collective-permute-start(bf16[8,64,256]{2,1,0:T(8,128)(2,1)S(1)} %get-tuple-element.39), channel_id=1, source_target_pairs={{0,3},{1,0},{2,1},{3,2},{4,7},{5,4},{6,5},{7,6},{8,11},{9,8},{10,9... | collective-permute-start | bytes 786440 | tf_op jit(solution)/shard_map/ppermute | solution.py:494
  35.4 0.6 collective-permute-done.11
  36.0 3.1 %collective-permute-done.13 = bf16[2,128,256]{2,1,0:T(8,128)(2,1)S(1)} collective-permute-done((bf16[2,128,256]{2,1,0:T(8,128)(2,1)S(1)}, bf16[2,128,256]{2,1,0:T(8,128)(2,1)S(1)}, u32[]{:S(2)}, u32[]{:S(2)}) %collective-permute-start.13) | collective-permute-done | bytes 131104 | tf_op jit(solution)/shard_map/ppermute | solution.py:471
  39.0 9.9 %collective-permute-done.12 = bf16[2,128,256]{2,1,0:T(8,128)(2,1)S(1)} collective-permute-done((bf16[2,128,256]{2,1,0:T(8,128)(2,1)S(1)}, bf16[2,128,256]{2,1,0:T(8,128)(2,1)S(1)}, u32[]{:S(2)}, u32[]{:S(2)}) %collective-permute-start.12) | collective-permute-done | bytes 131104 | tf_op jit(solution)/shard_map/ppermute | solution.py:471
  48.9 0.1 fusion.3
  49.0 0.9 %collective-permute-start.14 = (bf16[2,128,256]{2,1,0:T(8,128)(2,1)S(1)}, bf16[2,128,256]{2,1,0:T(8,128)(2,1)S(1)}, u32[]{:S(2)}, u32[]{:S(2)}) collective-permute-start(bf16[2,128,256]{2,1,0:T(8,128)(2,1)S(1)} %fusion.3), channel_id=1, source_target_pairs={{0,8},{4,12},{8,0},{12,4},{1,9},{5,13},{9,1},{13,5},{2,10},{6,14},... | collective-permute-start | bytes 393224 | tf_op jit(solution)/shard_map/ppermute | solution.py:476
  49.9 0.0 collective-permute-done.6.left
  49.9 0.8 %collective-permute-done.7.right = bf16[8,64,256]{2,1,0:T(8,128)(2,1)S(1)} collective-permute-done((bf16[8,64,256]{2,1,0:T(8,128)(2,1)S(1)}, bf16[8,64,256]{2,1,0:T(8,128)(2,1)S(1)}, u32[]{:S(2)}, u32[]{:S(2)}) %collective-permute-start.7) | collective-permute-done | bytes 262176 | tf_op jit(solution)/shard_map/ppermute | solution.py:494
  50.7 0.1 collective-permute-start.8
  50.8 0.7 %collective-permute-start.9 = (bf16[264,256]{1,0:T(8,128)(2,1)S(1)}, bf16[264,256]{1,0:T(8,128)(2,1)S(1)}, u32[]{:S(2)}, u32[]{:S(2)}) collective-permute-start(bf16[264,256]{1,0:T(8,128)(2,1)S(1)} %get-tuple-element.42), channel_id=1, source_target_pairs={{4,8},{8,4},{5,9},{9,5},{6,10},{10,6},{7,11},{11,7},{20,24},{24,20... | collective-permute-start | bytes 405512 | tf_op jit(solution)/shard_map/ppermute | solution.py:499
  51.5 2.6 %collective-permute-done.14 = bf16[2,128,256]{2,1,0:T(8,128)(2,1)S(1)} collective-permute-done((bf16[2,128,256]{2,1,0:T(8,128)(2,1)S(1)}, bf16[2,128,256]{2,1,0:T(8,128)(2,1)S(1)}, u32[]{:S(2)}, u32[]{:S(2)}) %collective-permute-start.14) | collective-permute-done | bytes 131104 | tf_op jit(solution)/shard_map/ppermute | solution.py:476
  54.1 0.1 collective-permute-start.15
  54.2 0.0 copy-done
  54.2 2.0 %shard_map.81 = bf16[1024,256]{1,0:T(8,128)(2,1)} custom-call(bf16[1024,2048]{1,0:T(8,128)(2,1)S(1)} %get-tuple-element.36.filt, bf16[2048,256]{1,0:T(8,128)(2,1)S(1)} %bitcast.20), custom_call_target="tpu_custom_call" | custom-call | tf_op jit(solution)/shard_map/pallas_call | solution.py:42
  56.2 2.1 %shard_map.83.inner = bf16[8,768,256]{2,1,0:T(8,128)(2,1)S(1)} custom-call(bf16[8,256,512]{2,1,0:T(8,128)(2,1)S(1)} %get-tuple-element.26.bands, bf16[8,128,256]{2,1,0:T(8,128)(2,1)S(1)} %get-tuple-element.33.own, bf16[8,64,256]{2,1,0:T(8,128)(2,1)S(1)} %collective-permute-done.6.left, bf16[8,64,256]{2,1,0:T(8,128)(2,1)S(1)} %collective-permute-done.7.right), custom_call_target="tpu_custom_call" | custom-call | tf_op jit(solution)/shard_map/pallas_call | solution.py:42
  58.3 0.0 collective-permute-done.8.core
  58.3 0.0 collective-permute-done.9.far
  58.3 4.1 %shard_map.84 = bf16[8,128,256]{2,1,0:T(8,128)(2,1)} custom-call(bf16[8,256,512]{2,1,0:T(8,128)(2,1)S(1)} %get-tuple-element.26.bands, bf16[264,256]{1,0:T(8,128)(2,1)S(1)} %collective-permute-done.8.core, bf16[264,256]{1,0:T(8,128)(2,1)S(1)} %collective-permute-done.9.far, bf16[8,256,256]{2,1,0:T(8,128)(2,1)S(1)} %copy-done, ...), custom_call_target="tpu_custom_call" | custom-call | tf_op jit(solution)/shard_map/pallas_call | solution.py:42
  62.4 0.0 collective-permute-done.15.other
  62.4 0.8 %shard_map.85 = f32[2,256,256]{2,1,0:T(8,128)} custom-call(bf16[2,128,256]{2,1,0:T(8,128)(2,1)S(1)} %add_convert_fusion.mine, bf16[2,128,256]{2,1,0:T(8,128)(2,1)S(1)} %collective-permute-done.15.other), custom_call_target="tpu_custom_call" | custom-call | tf_op jit(solution)/shard_map/pallas_call | solution.py:42
  (4 shorter events, 0.1 us)
Async XLA Ops:
  1.9 9.5 %collective-permute-start = (bf16[4,64,256]{2,1,0:T(8,128)(2,1)S(1)}, bf16[4,64,256]{2,1,0:T(8,128)(2,1)S(1)}, u32[]{:S(2)}, u32[]{:S(2)}) collective-permute-start(bf16[4,64,256]{2,1,0:T(8,128)(2,1)S(1)} %get-tuple-element.29), channel_id=1, source_target_pairs={{0,1},{1,2},{2,3},{3,0},{4,5},{5,6},{6,7},{7,4},{8,9},{9,10},{10,1... | collective-permute-start | bytes 393224 | tf_op jit(solution)/shard_map/ppermute | solution.py:493
  5.0 9.3 %collective-permute-start.1 = (bf16[4,64,256]{2,1,0:T(8,128)(2,1)S(1)}, bf16[4,64,256]{2,1,0:T(8,128)(2,1)S(1)}, u32[]{:S(2)}, u32[]{:S(2)}) collective-permute-start(bf16[4,64,256]{2,1,0:T(8,128)(2,1)S(1)} %get-tuple-element.30), channel_id=1, source_target_pairs={{0,3},{1,0},{2,1},{3,2},{4,7},{5,4},{6,5},{7,6},{8,11},{9,8},{10,9... | collective-permute-start | bytes 393224 | tf_op jit(solution)/shard_map/ppermute | solution.py:494
  7.1 11.9 %collective-permute-start.4 = (bf16[4,64,256]{2,1,0:T(8,128)(2,1)S(1)}, bf16[4,64,256]{2,1,0:T(8,128)(2,1)S(1)}, u32[]{:S(2)}, u32[]{:S(2)}) collective-permute-start(bf16[4,64,256]{2,1,0:T(8,128)(2,1)S(1)} %get-tuple-element.34), channel_id=1, source_target_pairs={{0,1},{1,2},{2,3},{3,0},{4,5},{5,6},{6,7},{7,4},{8,9},{9,10},{10,1... | collective-permute-start | bytes 393224 | tf_op jit(solution)/shard_map/ppermute | solution.py:493
  7.1 11.9 %collective-permute-start.5 = (bf16[4,64,256]{2,1,0:T(8,128)(2,1)S(1)}, bf16[4,64,256]{2,1,0:T(8,128)(2,1)S(1)}, u32[]{:S(2)}, u32[]{:S(2)}) collective-permute-start(bf16[4,64,256]{2,1,0:T(8,128)(2,1)S(1)} %get-tuple-element.35), channel_id=1, source_target_pairs={{0,3},{1,0},{2,1},{3,2},{4,7},{5,4},{6,5},{7,6},{8,11},{9,8},{10,9... | collective-permute-start | bytes 393224 | tf_op jit(solution)/shard_map/ppermute | solution.py:494
  14.3 4.7 %collective-permute-start.2 = (bf16[256,256]{1,0:T(8,128)(2,1)S(1)}, bf16[256,256]{1,0:T(8,128)(2,1)S(1)}, u32[]{:S(2)}, u32[]{:S(2)}) collective-permute-start(bf16[256,256]{1,0:T(8,128)(2,1)S(1)} %get-tuple-element.31), channel_id=1, source_target_pairs={{0,4},{4,0},{8,12},{12,8},{1,5},{5,1},{9,13},{13,9},{2,6},{6,2},{1... | collective-permute-start | bytes 393224 | tf_op jit(solution)/shard_map/ppermute | solution.py:500
  14.4 4.7 %collective-permute-start.3 = (bf16[256,256]{1,0:T(8,128)(2,1)S(1)}, bf16[256,256]{1,0:T(8,128)(2,1)S(1)}, u32[]{:S(2)}, u32[]{:S(2)}) collective-permute-start(bf16[256,256]{1,0:T(8,128)(2,1)S(1)} %get-tuple-element.32), channel_id=1, source_target_pairs={{4,8},{8,4},{5,9},{9,5},{6,10},{10,6},{7,11},{11,7},{20,24},{24,20... | collective-permute-start | bytes 393224 | tf_op jit(solution)/shard_map/ppermute | solution.py:499
  22.8 31.4 %copy-start = (bf16[8,256,256]{2,1,0:T(8,128)(2,1)S(1)}, bf16[8,256,256]{2,1,0:T(8,128)(2,1)}, u32[]{:S(2)}) copy-start(bf16[8,256,256]{2,1,0:T(8,128)(2,1)} %mixing.1) | copy-start | bytes 3145732
  22.8 4.7 %collective-permute-start.10 = (bf16[4,2,128,256]{3,2,1,0:T(8,128)(2,1)S(1)}, bf16[4,2,128,256]{3,2,1,0:T(8,128)(2,1)S(1)}, u32[]{:S(2)}, u32[]{:S(2)}) collective-permute-start(bf16[4,2,128,256]{3,2,1,0:T(8,128)(2,1)S(1)} %get-tuple-element.44), channel_id=1, source_target_pairs={{0,4},{4,0},{8,12},{12,8},{1,5},{5,1},{9,13},{13,9},{2,6},{6,2},{1... | collective-permute-start | bytes 1572872 | tf_op jit(solution)/shard_map/ppermute | solution.py:467
  27.7 8.3 %collective-permute-start.11 = (bf16[2,128,256]{2,1,0:T(8,128)(2,1)S(1)}, bf16[2,128,256]{2,1,0:T(8,128)(2,1)S(1)}, u32[]{:S(2)}, u32[]{:S(2)}) collective-permute-start(bf16[2,128,256]{2,1,0:T(8,128)(2,1)S(1)} %get-tuple-element.47), channel_id=1, source_target_pairs={{0,1},{1,2},{2,3},{3,0},{4,5},{5,6},{6,7},{7,4},{8,9},{9,10},{10,1... | collective-permute-start | bytes 393224 | tf_op jit(solution)/shard_map/ppermute | solution.py:471
  28.3 10.7 %collective-permute-start.13 = (bf16[2,128,256]{2,1,0:T(8,128)(2,1)S(1)}, bf16[2,128,256]{2,1,0:T(8,128)(2,1)S(1)}, u32[]{:S(2)}, u32[]{:S(2)}) collective-permute-start(bf16[2,128,256]{2,1,0:T(8,128)(2,1)S(1)} %get-tuple-element.48), channel_id=1, source_target_pairs={{0,3},{1,0},{2,1},{3,2},{4,7},{5,4},{6,5},{7,6},{8,11},{9,8},{10,9... | collective-permute-start | bytes 393224 | tf_op jit(solution)/shard_map/ppermute | solution.py:471
  31.6 17.3 %collective-permute-start.12 = (bf16[2,128,256]{2,1,0:T(8,128)(2,1)S(1)}, bf16[2,128,256]{2,1,0:T(8,128)(2,1)S(1)}, u32[]{:S(2)}, u32[]{:S(2)}) collective-permute-start(bf16[2,128,256]{2,1,0:T(8,128)(2,1)S(1)} %get-tuple-element.49), channel_id=1, source_target_pairs={{0,2},{1,3},{2,0},{3,1},{4,6},{5,7},{6,4},{7,5},{8,10},{9,11},{10,... | collective-permute-start | bytes 393224 | tf_op jit(solution)/shard_map/ppermute | solution.py:471
  31.6 18.3 %collective-permute-start.6 = (bf16[8,64,256]{2,1,0:T(8,128)(2,1)S(1)}, bf16[8,64,256]{2,1,0:T(8,128)(2,1)S(1)}, u32[]{:S(2)}, u32[]{:S(2)}) collective-permute-start(bf16[8,64,256]{2,1,0:T(8,128)(2,1)S(1)} %get-tuple-element.38), channel_id=1, source_target_pairs={{0,1},{1,2},{2,3},{3,0},{4,5},{5,6},{6,7},{7,4},{8,9},{9,10},{10,1... | collective-permute-start | bytes 786440 | tf_op jit(solution)/shard_map/ppermute | solution.py:493
  32.2 18.5 %collective-permute-start.7 = (bf16[8,64,256]{2,1,0:T(8,128)(2,1)S(1)}, bf16[8,64,256]{2,1,0:T(8,128)(2,1)S(1)}, u32[]{:S(2)}, u32[]{:S(2)}) collective-permute-start(bf16[8,64,256]{2,1,0:T(8,128)(2,1)S(1)} %get-tuple-element.39), channel_id=1, source_target_pairs={{0,3},{1,0},{2,1},{3,2},{4,7},{5,4},{6,5},{7,6},{8,11},{9,8},{10,9... | collective-permute-start | bytes 786440 | tf_op jit(solution)/shard_map/ppermute | solution.py:494
  49.0 5.0 %collective-permute-start.14 = (bf16[2,128,256]{2,1,0:T(8,128)(2,1)S(1)}, bf16[2,128,256]{2,1,0:T(8,128)(2,1)S(1)}, u32[]{:S(2)}, u32[]{:S(2)}) collective-permute-start(bf16[2,128,256]{2,1,0:T(8,128)(2,1)S(1)} %fusion.3), channel_id=1, source_target_pairs={{0,8},{4,12},{8,0},{12,4},{1,9},{5,13},{9,1},{13,5},{2,10},{6,14},... | collective-permute-start | bytes 393224 | tf_op jit(solution)/shard_map/ppermute | solution.py:476
  50.7 7.6 %collective-permute-start.8 = (bf16[264,256]{1,0:T(8,128)(2,1)S(1)}, bf16[264,256]{1,0:T(8,128)(2,1)S(1)}, u32[]{:S(2)}, u32[]{:S(2)}) collective-permute-start(bf16[264,256]{1,0:T(8,128)(2,1)S(1)} %get-tuple-element.41), channel_id=1, source_target_pairs={{0,4},{4,0},{8,12},{12,8},{1,5},{5,1},{9,13},{13,9},{2,6},{6,2},{1... | collective-permute-start | bytes 405512 | tf_op jit(solution)/shard_map/ppermute | solution.py:500
  50.8 7.5 %collective-permute-start.9 = (bf16[264,256]{1,0:T(8,128)(2,1)S(1)}, bf16[264,256]{1,0:T(8,128)(2,1)S(1)}, u32[]{:S(2)}, u32[]{:S(2)}) collective-permute-start(bf16[264,256]{1,0:T(8,128)(2,1)S(1)} %get-tuple-element.42), channel_id=1, source_target_pairs={{4,8},{8,4},{5,9},{9,5},{6,10},{10,6},{7,11},{11,7},{20,24},{24,20... | collective-permute-start | bytes 405512 | tf_op jit(solution)/shard_map/ppermute | solution.py:499
  54.1 8.3 %collective-permute-start.15 = (bf16[2,128,256]{2,1,0:T(8,128)(2,1)S(1)}, bf16[2,128,256]{2,1,0:T(8,128)(2,1)S(1)}, u32[]{:S(2)}, u32[]{:S(2)}) collective-permute-start(bf16[2,128,256]{2,1,0:T(8,128)(2,1)S(1)} %add_convert_fusion.mine), channel_id=1, source_target_pairs={{0,4},{4,0},{8,12},{12,8},{1,5},{5,1},{9,13},{13,9},{2,6},{6,2},{1... | collective-permute-start | bytes 393224 | tf_op jit(solution)/shard_map/ppermute | solution.py:480

commit v4 on v3

v4 whole, which is shorter than its diff:
```python
import functools

import jax
import jax.numpy as jnp
from jax import lax
from jax.experimental import pallas as pl
from jax.experimental.pallas import tpu as pltpu
from jax.sharding import PartitionSpec as P


BLOCK = 32
LANES = 128
DEPTH = 256


def swap(axis, mask):
    return [(i, i ^ mask) for i in range(lax.axis_size(axis))]


IN_VMEM = pl.BlockSpec(memory_space=pltpu.VMEM)
IN_SMEM = pl.BlockSpec(memory_space=pltpu.SMEM)
IN_HBM = pl.BlockSpec(memory_space=pltpu.HBM)


def near(array):
    return pltpu.with_memory_space_constraint(array, pltpu.VMEM)


def kernel_call(body, operands, outs, scratch, mib, scalars=0, far=(), far_out=False, alias=None):
    specs = [IN_SMEM] * scalars
    given = [pltpu.with_memory_space_constraint(x, pltpu.HBM) for x in operands[:scalars]]
    for i, operand in enumerate(operands[scalars:], scalars):
        specs.append(IN_HBM if i in far else IN_VMEM)
        given.append(pltpu.with_memory_space_constraint(operand, pltpu.HBM) if i in far else near(operand))
    single = not isinstance(outs, list)
    place = IN_HBM if far_out else IN_VMEM
    return pl.pallas_call(
        body,
        in_specs=specs,
        out_specs=place if single else [place] * len(outs),
        out_shape=outs,
        scratch_shapes=scratch,
        input_output_aliases=alias or {},
        compiler_params=pltpu.CompilerParams(vmem_limit_bytes=mib << 20),
    )(*given)


def packed_taps(pieces, window, total):
    kernels = pieces[0].shape[0]
    packed = None
    for r, piece in enumerate(pieces):
        wide = jnp.concatenate([piece, jnp.zeros((kernels, total - piece.shape[1]), piece.dtype)], 1)
        wide = pltpu.roll(wide, r * window, 1) if r else wide
        packed = wide if packed is None else packed + wide
    return packed


def spread_bands(packed, bands, row):
    kernels, total = packed.shape
    for k in range(kernels):
        rows = jnp.broadcast_to(packed[k : k + 1, :], (BLOCK, total))
        rolled = pltpu.roll(rows, 0, 1, stride=1, stride_axis=0)
        bands[row, k * BLOCK : (k + 1) * BLOCK, :] = rolled.astype(bands.dtype)


def bands_kernel(reach, quadrature, bands, edges):
    rows, three, kernels, taps = quadrature.shape
    window = taps - 1 + BLOCK
    middle = (taps - 1) // 2
    lane = lax.broadcasted_iota(jnp.int32, (kernels, LANES), 1)
    for row in range(rows):
        half = jnp.broadcast_to(reach[row : row + 1, :], (kernels, LANES))
        factor = 1.0 / jnp.sqrt(3.0 * (2.0 * half.astype(jnp.float32) + 1.0))
        head_inside = (jnp.abs(lane - middle) <= half).astype(jnp.float32)
        tail_inside = ((lane < taps - LANES) & (lane + LANES - middle <= half)).astype(jnp.float32)
        pieces = []
        for r in range(three):
            head = quadrature[row, r, :, 0:LANES] * factor * head_inside
            last = jnp.broadcast_to(quadrature[row, r, :, LANES:taps], (kernels, LANES))
            tail = last * factor * tail_inside
            piece = jnp.concatenate([head, tail], axis=1).astype(jnp.bfloat16)
            if row == rows - 1 and r == three - 1:
                edges[0] = piece
            if row == 0 and r == 0:
                edges[1] = piece
            pieces.append(piece.astype(jnp.float32))
        spread_bands(packed_taps(pieces, window, bands.shape[2]), bands, row)


def band_matrices(reach, quadrature):
    rows, three, kernels, taps = quadrature.shape
    total = -(-three * (taps - 1 + BLOCK) // DEPTH) * DEPTH
    return kernel_call(
        bands_kernel,
        [reach, quadrature],
        [
            pltpu.VMEM((rows, kernels * BLOCK, total), jnp.bfloat16),
            pltpu.VMEM((2, kernels, 2 * LANES), jnp.bfloat16),
        ],
        [],
        8,
    )


def split_rows(rows):
    part = 1
    outer = list(range(part)) + list(range(rows - part, rows))
    return outer, list(range(part, rows - part))


def even_sector():
    return lax.rem(lax.axis_index("lon"), 2) == 0


def rim_places(cols, rim):
    even = even_sector()
    first = pl.multiple_of(jnp.where(even, rim + cols, 0), rim)
    second = pl.multiple_of(jnp.where(even, 0, rim + cols), rim)
    return first, second


def rim_copies(groups, array, outs):
    cols = array.shape[1]
    rim = outs[0].shape[1]
    even = even_sector()
    starts = (jnp.where(even, cols - rim, 0), jnp.where(even, 0, cols - rim))
    copies = []
    for g, group in enumerate(groups):
        place = 0
        while place < len(group):
            size = 1
            while place + size < len(group) and group[place + size] == group[place] + size:
                size += 1
            source = array.at[pl.ds(group[place], size)]
            for side, first in enumerate(starts):
                target = outs[2 * g + side].at[pl.ds(place, size)]
                first = pl.multiple_of(first, rim)
                copies.append((source.at[:, pl.ds(first, rim), :], target))
            place += size
    return copies


def rims_kernel(groups, field, *refs):
    *sides, sems = refs
    copies = rim_copies(groups, field, sides)
    copies = [pltpu.make_async_copy(*c, sems.at[i]) for i, c in enumerate(copies)]
    for copy in copies:
        copy.start()
    for copy in copies:
        copy.wait()


def rims(field, rim, groups):
    chans = field.shape[2]
    outs = [
        pltpu.VMEM((len(group), rim, chans), jnp.bfloat16) for group in groups for _ in range(2)
    ]
    return kernel_call(
        functools.partial(rims_kernel, groups),
        [field],
        outs,
        [pltpu.SemaphoreType.DMA((16,))],
        4,
        far=(0,),
    )


def loads_kernel(field, cot, quadrature, half_width, *refs):
    *sides, field_near, cot_near, taps_near, reach, widths, sems = refs
    first = pltpu.make_async_copy(half_width, widths, sems.at[0])
    first.start()
    copies = rim_copies([range(cot.shape[0])], cot, sides)
    copies += [(quadrature, taps_near), (field, field_near), (cot, cot_near)]
    copies = [pltpu.make_async_copy(*c, sems.at[i + 1]) for i, c in enumerate(copies)]
    for copy in copies:
        copy.start()
    first.wait()
    for row in range(reach.shape[0]):
        reach[row : row + 1, :] = jnp.full((1, LANES), widths[row], jnp.int32)
    for copy in copies:
        copy.wait()


def loads(field, cot, quadrature, half_width, rim):
    rows, _, chans = field.shape
    outs = [pltpu.VMEM((rows, rim, chans), jnp.bfloat16)] * 2
    outs.append(pltpu.VMEM(field.shape, field.dtype))
    outs.append(pltpu.VMEM(cot.shape, cot.dtype))
    outs.append(pltpu.VMEM(quadrature.shape, jnp.float32))
    outs.append(pltpu.VMEM((rows, LANES), jnp.int32))
    return kernel_call(
        loads_kernel,
        [field, cot, quadrature, half_width],
        outs,
        [pltpu.SMEM(half_width.shape, jnp.int32), pltpu.SemaphoreType.DMA((8,))],
        8,
        far=(0, 1, 2, 3),
    )


def even_band():
    return lax.rem(lax.axis_index("lat"), 2) == 0


def edges_kernel(picks, own, paired, other, *rest):
    *basis, core_row, far_row = rest
    rim, cols = paired.shape[1], own.shape[1]
    even = even_band()
    first, second = rim_places(cols, rim)
    for out, last in ((core_row, even), (far_row, jnp.logical_not(even))):
        pick = jnp.where(last, picks[1], picks[0])
        out[pl.ds(first, rim)] = paired[pick]
        out[pl.ds(second, rim)] = other[pick]
        out[rim : rim + cols] = own[jnp.where(last, own.shape[0] - 1, 0)]
        if basis:
            out[2 * rim + cols :] = basis[0][jnp.where(last, 0, 1)]


def edge_rows(own, paired, other, picks, basis):
    _, cols, chans = own.shape
    span = cols + 2 * paired.shape[1] + (basis[0].shape[1] if basis else 0)
    outs = [pltpu.VMEM((span, chans), jnp.bfloat16)] * 2
    return kernel_call(
        functools.partial(edges_kernel, picks), [own, paired, other, *basis], outs, [], 4
    )


def fill_extended(ext, own, core, far, groups, sides):
    rows, cols = own.shape[0], own.shape[1]
    rim = sides[0].shape[1]
    span = ext.shape[1]
    even = even_band()
    ext[jnp.where(even, rows + 1, 0)] = core[0:span]
    ext[jnp.where(even, 0, rows + 1)] = far[0:span]
    ext[1 : rows + 1, rim : rim + cols, :] = own[...]
    first, second = rim_places(cols, rim)
    for g, group in enumerate(groups):
        for i, row in enumerate(group):
            ext[row + 1, pl.ds(first, rim), :] = sides[2 * g][i]
            ext[row + 1, pl.ds(second, rim), :] = sides[2 * g + 1][i]


def filter_rows(bands, ext, cols, write):
    rows, height, total = bands.shape
    reach = ext.shape[1] - cols + BLOCK
    spare = total - 3 * reach
    for row in range(rows):
        for first in range(0, cols, BLOCK):
            pieces = [ext[row + r, first : first + reach, :] for r in range(3)]
            if spare:
                pieces.append(ext[row, 0:spare, :])
            source = jnp.concatenate(pieces, axis=0)
            result = jnp.dot(bands[row], source, preferred_element_type=jnp.float32)
            result = result.astype(jnp.bfloat16)
            for k in range(height // BLOCK):
                write(row * cols + first, k, result[k * BLOCK : (k + 1) * BLOCK])


def band_place(n_lat):
    bits = n_lat.bit_length() - 1
    lat = lax.axis_index("lat")
    return sum(((lat >> b) & 1) << (bits - 1 - b) for b in range(bits))


def half_gradient(n_lat, filt, cot, out, grad, slot):
    kernels, half, _ = grad.shape
    n_lon, share, piece = out.shape[1], out.shape[2], out.shape[3]
    place, lon = band_place(n_lat), lax.axis_index("lon")
    group = n_lat // 2
    side = pl.multiple_of(((place // group) ^ slot) * half, half)
    for k in range(kernels):
        grad[k] = lax.dot_general(
            filt[:, pl.ds(side + 2 * half * k, half)],
            cot[...],
            (((0,), (0,)), ((), ())),
            preferred_element_type=jnp.float32,
        )
    for m in range(group):
        start = pl.multiple_of(((place ^ m) % group) * piece, piece)
        for s in range(n_lon):
            first = (lon ^ s) * share
            out[m, s] = grad[pl.ds(first, share), pl.ds(start, piece), :].astype(out.dtype)


def forward_kernel(n_lat, groups, bands, own, core, far, cot, *rest):
    *sides, filt, send, ext, grad = rest
    _, cols, chans = own.shape
    fill_extended(ext, own, core, far, groups, sides)

    def write(start, k, value):
        filt[start : start + BLOCK, k * chans : (k + 1) * chans] = value

    filter_rows(bands, ext, cols, write)
    half_gradient(n_lat, filt, cot, send, grad, 1)


def part_shape(kernels, chans, outs, n_lat, n_lon):
    return (n_lat // 2, n_lon, kernels // n_lon, chans // n_lat, outs)


def forward(bands, own, core, far, cot, groups, sides, kernels, n_lat, n_lon):
    rows, cols, chans = own.shape
    outs = cot.shape[1]
    rim = sides[0].shape[1]
    return kernel_call(
        functools.partial(forward_kernel, n_lat, groups),
        [bands, own, core, far, cot, *sides],
        [
            pltpu.VMEM((rows * cols, kernels * chans), jnp.bfloat16),
            pltpu.VMEM(part_shape(kernels, chans, outs, n_lat, n_lon), jnp.bfloat16),
        ],
        [
            pltpu.VMEM((rows + 2, cols + 2 * rim, chans), jnp.bfloat16),
            pltpu.VMEM((kernels, chans // 2, outs), jnp.float32),
        ],
        20,
    )


def kept_kernel(n_lat, filt, cot, keep, grad):
    half_gradient(n_lat, filt, cot, keep, grad, 0)


def kept(filt, cot, kernels, n_lat, n_lon):
    chans, outs = filt.shape[1] // kernels, cot.shape[1]
    return kernel_call(
        functools.partial(kept_kernel, n_lat),
        [filt, cot],
        pltpu.VMEM(part_shape(kernels, chans, outs, n_lat, n_lon), jnp.float32),
        [pltpu.VMEM((kernels, chans // 2, outs), jnp.float32)],
        12,
    )


def mix_kernel(filt, mixing, out):
    out[...] = jnp.dot(filt[...], mixing[...], preferred_element_type=jnp.float32).astype(out.dtype)


def mirror(size):
    across = lax.broadcasted_iota(jnp.int32, (size, size), 0)
    down = lax.broadcasted_iota(jnp.int32, (size, size), 1)
    return (across + down == size - 1).astype(jnp.float32).astype(jnp.bfloat16)


def adjoint_band(window, above, here, below):
    total = here.shape[1]
    sources = [below, here, above]
    lane = lax.broadcasted_iota(jnp.int32, (here.shape[0], LANES), 1)
    tiles = []
    for first in range(0, total, LANES):
        r = min(first // window, 2)
        tile = sources[r][:, first : first + LANES]
        cut = (r + 1) * window - first
        if r < 2 and cut < LANES:
            following = sources[r + 1][:, first : first + LANES]
            tile = jnp.where(lane < cut, tile, following)
        tiles.append(tile)
    return jnp.concatenate(tiles, axis=1)


def adjoint_row(band, reversed_rows, cols, write):
    span = reversed_rows[0].shape[0]
    reach = span - cols + BLOCK
    spare = band.shape[1] - 3 * reach
    for g in range(cols // BLOCK):
        first = g * BLOCK
        pieces = [source[first : first + reach, :] for source in reversed_rows]
        if spare:
            pieces.append(reversed_rows[0][0:spare, :])
        result = jnp.dot(
            band, jnp.concatenate(pieces, axis=0), preferred_element_type=jnp.float32
        ).astype(jnp.bfloat16)
        for k in range(result.shape[0] // BLOCK):
            write(first, k, result[k * BLOCK : (k + 1) * BLOCK])


def backward_inner_kernel(window, bands, own, paired, other, filt, reverse, lines):
    rows, cols, _ = own.shape
    rim = paired.shape[1]
    flip = mirror(reverse.shape[1])
    first, second = rim_places(cols, rim)
    for row in range(rows):
        lines[row, pl.ds(first, rim), :] = paired[row]
        lines[row, pl.ds(second, rim), :] = other[row]
        lines[row, rim : rim + cols, :] = own[row]
    for row in range(rows):
        reverse[row] = jnp.dot(flip, lines[row], preferred_element_type=jnp.float32).astype(
            reverse.dtype
        )
    for row in range(1, rows - 1):
        band = adjoint_band(window, bands[row - 1], bands[row], bands[row + 1])

        def write(first, k, value, base=(row - 1) * cols):
            filt[k, base + first : base + first + BLOCK, :] = value

        lines = [reverse.at[row + 1], reverse.at[row], reverse.at[row - 1]]
        adjoint_row(band, lines, cols, write)


def backward_inner(bands, own, paired, other, window):
    rows, cols, outs = own.shape
    span = cols + 2 * paired.shape[1]
    kernels = bands.shape[1] // BLOCK
    return kernel_call(
        functools.partial(backward_inner_kernel, window),
        [bands, own, paired, other],
        [
            pltpu.VMEM((kernels, (rows - 2) * cols, outs), jnp.bfloat16),
            pltpu.VMEM((rows, span, outs), jnp.bfloat16),
        ],
        [pltpu.VMEM((rows, span, outs), jnp.bfloat16)],
        12,
    )


def backward_edges_kernel(
    window, cols, bands, core, far, turned, filt, edge, extra
):
    rows, span, _ = turned.shape
    flip = mirror(span)
    even = even_band()
    for i, line in ((jnp.where(even, 1, 0), core), (jnp.where(even, 0, 1), far)):
        edge[i] = jnp.dot(flip, line[0:span], preferred_element_type=jnp.float32).astype(edge.dtype)
    none = jnp.zeros((core.shape[0] - span, 2 * LANES), jnp.float32)
    beside, across = core[span:, :].astype(jnp.float32), far[span:, :].astype(jnp.float32)
    above, below = jnp.where(even, across, beside), jnp.where(even, beside, across)
    spread_bands(packed_taps([none, none, above], window, bands.shape[2]), extra, 0)
    spread_bands(packed_taps([below, none, none], window, bands.shape[2]), extra, 1)
    last = rows - 1
    picks = (
        (extra[0], bands[0], bands[1], [turned.at[1], turned.at[0], edge.at[0]]),
        (bands[last - 1], bands[last], extra[1], [edge.at[1], turned.at[last], turned.at[last - 1]]),
    )
    for i, (above, here, below, lines) in enumerate(picks):
        band = adjoint_band(window, above, here, below)

        def write(first, k, value, base=i * cols):
            filt[k, base + first : base + first + BLOCK, :] = value

        adjoint_row(band, lines, cols, write)


def backward_edges(bands, core, far, turned, cols, window):
    _, span, outs = turned.shape
    kernels = bands.shape[1] // BLOCK
    return kernel_call(
        functools.partial(backward_edges_kernel, window, cols),
        [bands, core, far, turned],
        pltpu.VMEM((kernels, 2 * cols, outs), jnp.bfloat16),
        [
            pltpu.VMEM((2, span, outs), jnp.bfloat16),
            pltpu.VMEM((2,) + bands.shape[1:], jnp.bfloat16),
        ],
        8,
    )


def mixed_rows(source, mixing, cols, store):
    total = None
    for k in range(mixing.shape[0]):
        term = lax.dot_general(
            source[k], mixing[k], (((1,), (1,)), ((), ())), preferred_element_type=jnp.float32
        )
        total = term if total is None else total + term
    total = total.astype(jnp.bfloat16)
    back = mirror(cols)
    for i in range(total.shape[0] // cols):
        part = total[i * cols : (i + 1) * cols]
        store(i, jnp.dot(back, part, preferred_element_type=jnp.float32).astype(jnp.bfloat16))


def inner_mix_kernel(mixing, inner, out):
    def store(i, value):
        out[i] = value

    mixed_rows(inner, mixing, out.shape[1], store)


def inner_mix(mixing, inner, cols):
    _, chans, _ = mixing.shape
    shape = (inner.shape[1] // cols, cols, chans)
    return kernel_call(inner_mix_kernel, [mixing, inner], pltpu.VMEM(shape, jnp.bfloat16), [], 8)


def back_mix_kernel(mixing, inner, filt, out, stage, sems):
    rows, cols, _ = out.shape
    copies = [
        pltpu.make_async_copy(inner, out.at[pl.ds(1, rows - 2)], sems.at[0]),
        pltpu.make_async_copy(stage.at[0], out.at[0], sems.at[1]),
        pltpu.make_async_copy(stage.at[1], out.at[rows - 1], sems.at[2]),
    ]
    copies[0].start()

    def store(i, value):
        stage[i] = value

    mixed_rows(filt, mixing, cols, store)
    copies[1].start()
    copies[2].start()
    for copy in copies:
        copy.wait()


def back_mix(mixing, inner, filt, rows):
    _, chans, _ = mixing.shape
    cols = filt.shape[1] // 2
    return kernel_call(
        back_mix_kernel,
        [mixing, inner, filt],
        jax.ShapeDtypeStruct((rows, cols, chans), jnp.bfloat16),
        [pltpu.VMEM((2, cols, chans), jnp.bfloat16), pltpu.SemaphoreType.DMA((3,))],
        8,
        far_out=True,
    )


def assemble_kernel(mine, other, out):
    half, _, piece, _ = mine.shape
    place = band_place(2 * half)
    for m in range(2 * half):
        source = mine[m] if m < half else other[m - half]
        start = pl.multiple_of((place ^ m) * piece, piece)
        out[:, pl.ds(start, piece), :] = source.astype(out.dtype)


def assemble(mine, other):
    half, share, piece, chans = mine.shape
    return kernel_call(
        assemble_kernel,
        [mine, other],
        jax.ShapeDtypeStruct((share, 2 * half * piece, chans), jnp.float32),
        [],
        4,
    )


def reduced_gradient(keep, send):
    n_lat, n_lon = lax.axis_size("lat"), lax.axis_size("lon")
    mask = 1
    while True:
        other = lax.ppermute(send, "lat", swap("lat", mask))
        total = keep + other.astype(jnp.float32)
        mask *= 2
        if mask >= n_lat:
            break
        half = total.shape[0] // 2
        keep, send = total[:half], total[half:].astype(jnp.bfloat16)
    total = total[0]
    wire = total.astype(jnp.bfloat16)
    piece = total[0]
    for s in range(1, n_lon):
        other = lax.ppermute(wire[s], "lon", swap("lon", s))
        piece = piece + other.astype(jnp.float32)
    pieces = piece.astype(jnp.bfloat16)[None]
    while mask > 1:
        mask //= 2
        other = lax.ppermute(pieces, "lat", swap("lat", mask))
        if mask > 1:
            pieces = jnp.concatenate([pieces, other], axis=0)
    return assemble(pieces, other)


def on_device(field_in, quadrature, half_width, mixing, cotangent):
    rows, cols, chans = field_in.shape
    kernels, _, outs = mixing.shape
    taps = quadrature.shape[-1]
    rim = (taps - 1) // 2
    n_lat, n_lon = lax.axis_size("lat"), lax.axis_size("lon")
    groups = split_rows(rows)
    outer = groups[0]

    def beside(pair):
        count = lax.axis_size("lon")
        other = [(i, (i + 1) % count) for i in range(1, count, 2)]
        return [
            lax.ppermute(pair[0], "lon", swap("lon", 1)),
            lax.ppermute(pair[1], "lon", other + [(j, i) for i, j in other]),
        ]

    def bands_beside(pair):
        across = [(i, i + 1) for i in range(1, lax.axis_size("lat") - 1, 2)]
        far = lax.ppermute(pair[1], "lat", across + [(j, i) for i, j in across])
        core = lax.ppermute(pair[0], "lat", swap("lat", 1))
        return core, far

    window = taps - 1 + BLOCK
    sides = rims(field_in, rim, groups)
    outer_sides = beside(sides[0:2])
    inner_sides = beside(sides[2:4])
    *sides, field_near, cot_near, taps_near, reach = loads(
        field_in, cotangent, quadrature, half_width, rim
    )
    g_sides = beside(sides)
    bands, basis_edges = band_matrices(reach, taps_near)
    picks = (0, len(outer) - 1)
    sent = edge_rows(field_near, *outer_sides, picks, [])
    f_core, f_far = bands_beside(sent)

    flat_cot = cot_near.reshape(rows * cols, outs)
    filtered, send = forward(
        bands,
        field_near,
        f_core,
        f_far,
        flat_cot,
        groups,
        outer_sides + inner_sides,
        kernels,
        n_lat,
        n_lon,
    )
    keep = kept(filtered, flat_cot, kernels, n_lat, n_lon)
    weight_grad = reduced_gradient(keep, send)
    field_out = kernel_call(
        mix_kernel,
        [filtered, mixing.reshape(kernels * chans, outs)],
        jax.ShapeDtypeStruct((rows * cols, outs), jnp.bfloat16),
        [],
        8,
    )
    sent = edge_rows(cot_near, *g_sides, (0, rows - 1), [basis_edges])
    g_core, g_far = bands_beside(sent)
    inner, turned = backward_inner(bands, cot_near, *g_sides, window)
    edge = backward_edges(bands, g_core, g_far, turned, cols, window)
    input_grad = back_mix(mixing, inner_mix(mixing, inner, cols), edge, rows)
    return (
        field_out.reshape(rows, cols, outs),
        input_grad,
        weight_grad,
    )


def solution(mesh):
    return jax.shard_map(
        on_device,
        mesh=mesh,
        in_specs=(
            P(("ens", "lat"), "lon", None),
            P("lat", None, None, None),
            P("lat"),
            P(),
            P(("ens", "lat"), "lon", None),
        ),
        out_specs=(
            P(("ens", "lat"), "lon", None),
            P(("ens", "lat"), "lon", None),
            P("lon", "ens", None),
        ),
        check_vma=False,
    )
```

time: 63.9 us -> 64.9 us (1.016)
  waiting for transfers between devices: 21.7 us -> 24.3 us
  Pallas kernels: 18 us -> 17.1 us
    ppermute x12 -> x13, waiting for transfers between devices: 21.7 us -> 24.2 us  [the longest x3 11.1 us: beside(): lax.ppermute(pair[1], 'lon', other + [(j, i) for i, j in other])]
    pallas_call x10 -> x13, Pallas kernels: 18 us -> 17.1 us  [kernel_call(): pl.pallas_call(body, in_specs=specs, out_specs=place if single else [plac...]
    ppermute x12 -> x13, starting transfers between devices: 20.9 us -> 20.7 us  [the longest x3 5.73 us: beside(): lax.ppermute(pair[1], 'lon', other + [(j, i) for i, j in other])]
  transfers between devices with their start and end apart: 16 -> 17, of which waited for: 8 -> 8; matrix products, arithmetic and copies ran while one was open for 0% -> 0% of each run, Pallas kernels for 19% -> 18%
where the time goes in v4:
time: 64.9 us; the launch traced here: 64.8 us
  waiting for transfers between devices  24.3 us (37%)
  starting transfers between devices  22.2 us (34%)
  Pallas kernels  17.1 us (26%)
  between operations  0.86 us (1%)
    pallas_call x13, Pallas kernels, kernel_call(): pl.pallas_call(body, in_specs=specs, out_specs=place if single else [plac...  17.1 us
    ppermute x3, waiting for transfers between devices, beside(): lax.ppermute(pair[1], 'lon', other + [(j, i) for i, j in other])  11.1 us
    ppermute x2, waiting for transfers between devices, reduced_gradient(): other = lax.ppermute(send, 'lat', swap('lat', mask))  7.78 us
    ppermute x3, starting transfers between devices, beside(): lax.ppermute(pair[1], 'lon', other + [(j, i) for i, j in other])  5.73 us
    ppermute x3, starting transfers between devices, beside(): lax.ppermute(pair[0], 'lon', swap('lon', 1))  5.28 us
    ppermute x2, starting transfers between devices, reduced_gradient(): other = lax.ppermute(pieces, 'lat', swap('lat', mask))  4.52 us
    ppermute x3, starting transfers between devices, reduced_gradient(): other = lax.ppermute(wire[s], 'lon', swap('lon', s))  3.55 us
    ppermute x3, waiting for transfers between devices, beside(): lax.ppermute(pair[0], 'lon', swap('lon', 1))  2.93 us
  transfers between devices with their start and end apart: 17, of which 8 were waited for; matrix products, arithmetic and copies ran while one was open for 0% of the time, Pallas kernels for 18%

profile of v4, /device:TPU:0, one launch (start us, length us, event | category | flops | bytes accessed | tf_op | source)
XLA Modules:
  0.0 64.8 jit_solution(2703353735609159554)
XLA Ops:
  0.6 1.3 %shard_map.78 = (bf16[2,64,256]{2,1,0:T(8,128)(2,1)S(1)}, bf16[2,64,256]{2,1,0:T(8,128)(2,1)S(1)}, bf16[6,64,256]{2,1,0:T(8,128)(2,1)S(1)}, bf16[6,64,256]{2,1,0:T(8,128)(2,1)S(1)}) custom-call(bf16[8,128,256]{2,1,0:T(8,128)(2,1)} %field.3), custom_call_target="tpu_custom_call" | custom-call | tf_op jit(solution)/shard_map/pallas_call | solution.py:37
  1.9 3.1 %collective-permute-start = (bf16[2,64,256]{2,1,0:T(8,128)(2,1)S(1)}, bf16[2,64,256]{2,1,0:T(8,128)(2,1)S(1)}, u32[]{:S(2)}, u32[]{:S(2)}) collective-permute-start(bf16[2,64,256]{2,1,0:T(8,128)(2,1)S(1)} %get-tuple-element.27), channel_id=1, source_target_pairs={{0,1},{1,0},{2,3},{3,2},{4,5},{5,4},{6,7},{7,6},{8,9},{9,8},{10,11... | collective-permute-start | bytes 196616 | tf_op jit(solution)/shard_map/ppermute | solution.py:576
  5.0 2.5 %collective-permute-start.1 = (bf16[2,64,256]{2,1,0:T(8,128)(2,1)S(1)}, bf16[2,64,256]{2,1,0:T(8,128)(2,1)S(1)}, u32[]{:S(2)}, u32[]{:S(2)}) collective-permute-start(bf16[2,64,256]{2,1,0:T(8,128)(2,1)S(1)} %get-tuple-element.28), channel_id=1, source_target_pairs={{1,2},{3,0},{2,1},{0,3},{5,6},{7,4},{6,5},{4,7},{9,10},{11,8},{10,... | collective-permute-start | bytes 196616 | tf_op jit(solution)/shard_map/ppermute | solution.py:577
  7.5 0.7 %collective-permute-start.4 = (bf16[6,64,256]{2,1,0:T(8,128)(2,1)S(1)}, bf16[6,64,256]{2,1,0:T(8,128)(2,1)S(1)}, u32[]{:S(2)}, u32[]{:S(2)}) collective-permute-start(bf16[6,64,256]{2,1,0:T(8,128)(2,1)S(1)} %get-tuple-element.32), channel_id=1, source_target_pairs={{0,1},{1,0},{2,3},{3,2},{4,5},{5,4},{6,7},{7,6},{8,9},{9,8},{10,11... | collective-permute-start | bytes 589832 | tf_op jit(solution)/shard_map/ppermute | solution.py:576
  8.2 0.9 %collective-permute-start.5 = (bf16[6,64,256]{2,1,0:T(8,128)(2,1)S(1)}, bf16[6,64,256]{2,1,0:T(8,128)(2,1)S(1)}, u32[]{:S(2)}, u32[]{:S(2)}) collective-permute-start(bf16[6,64,256]{2,1,0:T(8,128)(2,1)S(1)} %get-tuple-element.33), channel_id=1, source_target_pairs={{1,2},{3,0},{2,1},{0,3},{5,6},{7,4},{6,5},{4,7},{9,10},{11,8},{10,... | collective-permute-start | bytes 589832 | tf_op jit(solution)/shard_map/ppermute | solution.py:577
  9.1 1.5 %shard_map.76 = (bf16[8,64,256]{2,1,0:T(8,128)(2,1)S(1)}, bf16[8,64,256]{2,1,0:T(8,128)(2,1)S(1)}, bf16[8,128,256]{2,1,0:T(8,128)(2,1)S(1)}, bf16[8,128,256]{2,1...) custom-call(bf16[8,128,256]{2,1,0:T(8,128)(2,1)} %field.3, bf16[8,128,256]{2,1,0:T(8,128)(2,1)} %cot.1, ...), custom_call_target="tpu_custom_call" | custom-call | tf_op jit(solution)/shard_map/pallas_call | solution.py:37
  10.6 0.0 collective-permute-done.paired.rest_0_
  10.6 1.3 %collective-permute-done.1.other.rest_1_ = bf16[2,64,256]{2,1,0:T(8,128)(2,1)S(1)} collective-permute-done((bf16[2,64,256]{2,1,0:T(8,128)(2,1)S(1)}, bf16[2,64,256]{2,1,0:T(8,128)(2,1)S(1)}, u32[]{:S(2)}, u32[]{:S(2)}) %collective-permute-start.1) | collective-permute-done | bytes 65568 | tf_op jit(solution)/shard_map/ppermute | solution.py:577
  11.9 0.1 collective-permute-start.2
  11.9 0.7 %collective-permute-start.3 = (bf16[256,256]{1,0:T(8,128)(2,1)S(1)}, bf16[256,256]{1,0:T(8,128)(2,1)S(1)}, u32[]{:S(2)}, u32[]{:S(2)}) collective-permute-start(bf16[256,256]{1,0:T(8,128)(2,1)S(1)} %get-tuple-element.30), channel_id=1, source_target_pairs={{4,8},{8,4},{5,9},{9,5},{6,10},{10,6},{7,11},{11,7},{20,24},{24,20... | collective-permute-start | bytes 393224 | tf_op jit(solution)/shard_map/ppermute | solution.py:582
  12.6 1.6 %shard_map.77 = (bf16[8,256,512]{2,1,0:T(8,128)(2,1)S(1)}, bf16[2,8,256]{2,1,0:T(8,128)(2,1)S(1)}) custom-call(s32[8,128]{1,0:T(8,128)S(1)} %get-tuple-element.23.reach, f32[8,3,8,129]{3,2,1,0:T(8,128)S(1)} %get-tuple-element.24.quadrature), custom_call_target="tpu_custom_call" | custom-call | tf_op jit(solution)/shard_map/pallas_call | solution.py:37
  14.2 0.0 collective-permute-done.2.core
  14.2 0.0 collective-permute-done.3.far
  14.3 0.7 %collective-permute-done.4.rest_2_ = bf16[6,64,256]{2,1,0:T(8,128)(2,1)S(1)} collective-permute-done((bf16[6,64,256]{2,1,0:T(8,128)(2,1)S(1)}, bf16[6,64,256]{2,1,0:T(8,128)(2,1)S(1)}, u32[]{:S(2)}, u32[]{:S(2)}) %collective-permute-start.4) | collective-permute-done | bytes 196640 | tf_op jit(solution)/shard_map/ppermute | solution.py:576
  15.0 4.6 %collective-permute-done.5.rest_3_ = bf16[6,64,256]{2,1,0:T(8,128)(2,1)S(1)} collective-permute-done((bf16[6,64,256]{2,1,0:T(8,128)(2,1)S(1)}, bf16[6,64,256]{2,1,0:T(8,128)(2,1)S(1)}, u32[]{:S(2)}, u32[]{:S(2)}) %collective-permute-start.5) | collective-permute-done | bytes 196640 | tf_op jit(solution)/shard_map/ppermute | solution.py:577
  19.6 3.3 %shard_map.80 = (bf16[1024,2048]{1,0:T(8,128)(2,1)S(1)}, bf16[2,4,2,64,256]{4,3,2,1,0:T(8,128)(2,1)S(1)}) custom-call(bf16[8,256,512]{2,1,0:T(8,128)(2,1)S(1)} %get-tuple-element.25.bands, bf16[8,128,256]{2,1,0:T(8,128)(2,1)S(1)} %get-tuple-element.26.own, bf16[256,256]{1,0:T(8,128)(2,1)S(1)} %collective-permute-done.2.core, ...), custom_call_target="tpu_custom_call" | custom-call | tf_op jit(solution)/shard_map/pallas_call | solution.py:37
  22.9 0.1 collective-permute-start.10
  23.0 0.9 %shard_map.87 = f32[2,4,2,64,256]{4,3,2,1,0:T(8,128)S(1)} custom-call(bf16[1024,2048]{1,0:T(8,128)(2,1)S(1)} %get-tuple-element.34.filt, bf16[1024,256]{1,0:T(8,128)(2,1)S(1)} %bitcast.25), custom_call_target="tpu_custom_call" | custom-call | tf_op jit(solution)/shard_map/pallas_call | solution.py:37
  23.9 0.0 copy-start
  23.9 1.0 %collective-permute-done.10 = bf16[2,4,2,64,256]{4,3,2,1,0:T(8,128)(2,1)S(1)} collective-permute-done((bf16[2,4,2,64,256]{4,3,2,1,0:T(8,128)(2,1)S(1)}, bf16[2,4,2,64,256]{4,3,2,1,0:T(8,128)(2,1)S(1)}, u32[]{:S(2)}, u32[]{:S(2)}) %collective-permute-start.10) | collective-permute-done | bytes 524320 | tf_op jit(solution)/shard_map/ppermute | solution.py:541
  24.9 0.1 convert_add_fusion
  25.1 1.6 %collective-permute-start.11 = (bf16[1,4,2,64,256]{4,3,2,1,0:T(8,128)(2,1)S(1)}, bf16[1,4,2,64,256]{4,3,2,1,0:T(8,128)(2,1)S(1)}, u32[]{:S(2)}, u32[]{:S(2)}) collective-permute-start(bf16[1,4,2,64,256]{4,3,2,1,0:T(8,128)(2,1)S(1)} %slice.51), channel_id=1, source_target_pairs={{0,8},{4,12},{8,0},{12,4},{1,9},{5,13},{9,1},{13,5},{2,10},{6,14},... | collective-permute-start | bytes 786440 | tf_op jit(solution)/shard_map/ppermute | solution.py:541
  26.6 6.8 %collective-permute-done.11 = bf16[1,4,2,64,256]{4,3,2,1,0:T(8,128)(2,1)S(1)} collective-permute-done((bf16[1,4,2,64,256]{4,3,2,1,0:T(8,128)(2,1)S(1)}, bf16[1,4,2,64,256]{4,3,2,1,0:T(8,128)(2,1)S(1)}, u32[]{:S(2)}, u32[]{:S(2)}) %collective-permute-start.11) | collective-permute-done | bytes 262176 | tf_op jit(solution)/shard_map/ppermute | solution.py:541
  33.5 0.1 fusion.5
  33.6 0.7 %collective-permute-start.12 = (bf16[2,64,256]{2,1,0:T(8,128)(2,1)S(1)}, bf16[2,64,256]{2,1,0:T(8,128)(2,1)S(1)}, u32[]{:S(2)}, u32[]{:S(2)}) collective-permute-start(bf16[2,64,256]{2,1,0:T(8,128)(2,1)S(1)} %get-tuple-element.45), channel_id=1, source_target_pairs={{0,1},{1,0},{2,3},{3,2},{4,5},{5,4},{6,7},{7,6},{8,9},{9,8},{10,11... | collective-permute-start | bytes 196616 | tf_op jit(solution)/shard_map/ppermute | solution.py:552
  34.2 2.4 %collective-permute-start.14 = (bf16[2,64,256]{2,1,0:T(8,128)(2,1)S(1)}, bf16[2,64,256]{2,1,0:T(8,128)(2,1)S(1)}, u32[]{:S(2)}, u32[]{:S(2)}) collective-permute-start(bf16[2,64,256]{2,1,0:T(8,128)(2,1)S(1)} %get-tuple-element.46), channel_id=1, source_target_pairs={{0,3},{1,2},{2,1},{3,0},{4,7},{5,6},{6,5},{7,4},{8,11},{9,10},{10,... | collective-permute-start | bytes 196616 | tf_op jit(solution)/shard_map/ppermute | solution.py:552
  36.6 0.5 collective-permute-start.13
  37.1 1.5 %collective-permute-start.6 = (bf16[8,64,256]{2,1,0:T(8,128)(2,1)S(1)}, bf16[8,64,256]{2,1,0:T(8,128)(2,1)S(1)}, u32[]{:S(2)}, u32[]{:S(2)}) collective-permute-start(bf16[8,64,256]{2,1,0:T(8,128)(2,1)S(1)} %get-tuple-element.35), channel_id=1, source_target_pairs={{0,1},{1,0},{2,3},{3,2},{4,5},{5,4},{6,7},{7,6},{8,9},{9,8},{10,11... | collective-permute-start | bytes 786440 | tf_op jit(solution)/shard_map/ppermute | solution.py:576
  38.6 2.4 %collective-permute-start.7 = (bf16[8,64,256]{2,1,0:T(8,128)(2,1)S(1)}, bf16[8,64,256]{2,1,0:T(8,128)(2,1)S(1)}, u32[]{:S(2)}, u32[]{:S(2)}) collective-permute-start(bf16[8,64,256]{2,1,0:T(8,128)(2,1)S(1)} %get-tuple-element.36), channel_id=1, source_target_pairs={{1,2},{3,0},{2,1},{0,3},{5,6},{7,4},{6,5},{4,7},{9,10},{11,8},{10,... | collective-permute-start | bytes 786440 | tf_op jit(solution)/shard_map/ppermute | solution.py:577
  41.0 0.0 collective-permute-done.12
  41.0 0.0 collective-permute-done.14
  41.0 2.5 %collective-permute-done.13 = bf16[2,64,256]{2,1,0:T(8,128)(2,1)S(1)} collective-permute-done((bf16[2,64,256]{2,1,0:T(8,128)(2,1)S(1)}, bf16[2,64,256]{2,1,0:T(8,128)(2,1)S(1)}, u32[]{:S(2)}, u32[]{:S(2)}) %collective-permute-start.13) | collective-permute-done | bytes 65568 | tf_op jit(solution)/shard_map/ppermute | solution.py:552
  43.5 1.6 %collective-permute-start.15 = (bf16[1,2,64,256]{3,2,1,0:T(8,128)(2,1)S(1)}, bf16[1,2,64,256]{3,2,1,0:T(8,128)(2,1)S(1)}, u32[]{:S(2)}, u32[]{:S(2)}) collective-permute-start(bf16[1,2,64,256]{3,2,1,0:T(8,128)(2,1)S(1)} %fusion.4), channel_id=1, source_target_pairs={{0,8},{4,12},{8,0},{12,4},{1,9},{5,13},{9,1},{13,5},{2,10},{6,14},... | collective-permute-start | bytes 196616 | tf_op jit(solution)/shard_map/ppermute | solution.py:557
  45.1 2.2 %collective-permute-done.6.paired = bf16[8,64,256]{2,1,0:T(8,128)(2,1)S(1)} collective-permute-done((bf16[8,64,256]{2,1,0:T(8,128)(2,1)S(1)}, bf16[8,64,256]{2,1,0:T(8,128)(2,1)S(1)}, u32[]{:S(2)}, u32[]{:S(2)}) %collective-permute-start.6) | collective-permute-done | bytes 262176 | tf_op jit(solution)/shard_map/ppermute | solution.py:576
  47.3 5.2 %collective-permute-done.7.other = bf16[8,64,256]{2,1,0:T(8,128)(2,1)S(1)} collective-permute-done((bf16[8,64,256]{2,1,0:T(8,128)(2,1)S(1)}, bf16[8,64,256]{2,1,0:T(8,128)(2,1)S(1)}, u32[]{:S(2)}, u32[]{:S(2)}) %collective-permute-start.7) | collective-permute-done | bytes 262176 | tf_op jit(solution)/shard_map/ppermute | solution.py:577
  52.5 0.1 collective-permute-start.8
  52.6 0.7 %collective-permute-start.9 = (bf16[264,256]{1,0:T(8,128)(2,1)S(1)}, bf16[264,256]{1,0:T(8,128)(2,1)S(1)}, u32[]{:S(2)}, u32[]{:S(2)}) collective-permute-start(bf16[264,256]{1,0:T(8,128)(2,1)S(1)} %get-tuple-element.40), channel_id=1, source_target_pairs={{4,8},{8,4},{5,9},{9,5},{6,10},{10,6},{7,11},{11,7},{20,24},{24,20... | collective-permute-start | bytes 405512 | tf_op jit(solution)/shard_map/ppermute | solution.py:582
  53.2 0.0 collective-permute-done.15
  53.3 2.9 %collective-permute-start.16 = (bf16[2,2,64,256]{3,2,1,0:T(8,128)(2,1)S(1)}, bf16[2,2,64,256]{3,2,1,0:T(8,128)(2,1)S(1)}, u32[]{:S(2)}, u32[]{:S(2)}) collective-permute-start(bf16[2,2,64,256]{3,2,1,0:T(8,128)(2,1)S(1)} %pad_maximum_fusion.mine), channel_id=1, source_target_pairs={{0,4},{4,0},{8,12},{12,8},{1,5},{5,1},{9,13},{13,9},{2,6},{6,2},{1... | collective-permute-start | bytes 393224 | tf_op jit(solution)/shard_map/ppermute | solution.py:557
  56.2 2.0 %shard_map.81 = bf16[1024,256]{1,0:T(8,128)(2,1)} custom-call(bf16[1024,2048]{1,0:T(8,128)(2,1)S(1)} %get-tuple-element.34.filt, bf16[2048,256]{1,0:T(8,128)(2,1)S(1)} %bitcast.23), custom_call_target="tpu_custom_call" | custom-call | tf_op jit(solution)/shard_map/pallas_call | solution.py:37
  58.3 2.1 %shard_map.82 = (bf16[8,768,256]{2,1,0:T(8,128)(2,1)S(1)}, bf16[8,256,256]{2,1,0:T(8,128)(2,1)S(1)}) custom-call(bf16[8,256,512]{2,1,0:T(8,128)(2,1)S(1)} %get-tuple-element.25.bands, bf16[8,128,256]{2,1,0:T(8,128)(2,1)S(1)} %get-tuple-element.31.own, bf16[8,64,256]{2,1,0:T(8,128)(2,1)S(1)} %collective-permute-done.6.paired, ...), custom_call_target="tpu_custom_call" | custom-call | tf_op jit(solution)/shard_map/pallas_call | solution.py:37
  60.4 1.3 %shard_map.83.inner = bf16[6,128,256]{2,1,0:T(8,128)(2,1)S(1)} custom-call(bf16[8,256,256]{2,1,0:T(8,128)(2,1)S(1)} %copy-done, bf16[8,768,256]{2,1,0:T(8,128)(2,1)S(1)} %get-tuple-element.37.inner), custom_call_target="tpu_custom_call" | custom-call | tf_op jit(solution)/shard_map/pallas_call | solution.py:37
  61.6 0.0 collective-permute-done.8.core
  61.7 0.0 collective-permute-done.9.far
  61.7 0.9 %shard_map.85.filt = bf16[8,256,256]{2,1,0:T(8,128)(2,1)S(1)} custom-call(bf16[8,256,512]{2,1,0:T(8,128)(2,1)S(1)} %get-tuple-element.25.bands, bf16[264,256]{1,0:T(8,128)(2,1)S(1)} %collective-permute-done.8.core, bf16[264,256]{1,0:T(8,128)(2,1)S(1)} %collective-permute-done.9.far, bf16[8,256,256]{2,1,0:T(8,128)(2,1)S(1)} %get-tuple-element.41.turned), custom_call_target="tpu_custom_call" | custom-call | tf_op jit(solution)/shard_map/pallas_call | solution.py:37
  62.5 1.4 %shard_map.86 = bf16[8,128,256]{2,1,0:T(8,128)(2,1)} custom-call(bf16[8,256,256]{2,1,0:T(8,128)(2,1)S(1)} %copy-done, bf16[6,128,256]{2,1,0:T(8,128)(2,1)S(1)} %shard_map.83.inner, bf16[8,256,256]{2,1,0:T(8,128)(2,1)S(1)} %shard_map.85.filt), custom_call_target="tpu_custom_call" | custom-call | tf_op jit(solution)/shard_map/pallas_call | solution.py:37
  63.9 0.0 collective-permute-done.16.other
  63.9 0.8 %shard_map.88 = f32[2,256,256]{2,1,0:T(8,128)} custom-call(bf16[2,2,64,256]{3,2,1,0:T(8,128)(2,1)S(1)} %pad_maximum_fusion.mine, bf16[2,2,64,256]{3,2,1,0:T(8,128)(2,1)S(1)} %collective-permute-done.16.other), custom_call_target="tpu_custom_call" | custom-call | tf_op jit(solution)/shard_map/pallas_call | solution.py:37
  (7 shorter events, 0.1 us)
Async XLA Ops:
  1.9 8.7 %collective-permute-start = (bf16[2,64,256]{2,1,0:T(8,128)(2,1)S(1)}, bf16[2,64,256]{2,1,0:T(8,128)(2,1)S(1)}, u32[]{:S(2)}, u32[]{:S(2)}) collective-permute-start(bf16[2,64,256]{2,1,0:T(8,128)(2,1)S(1)} %get-tuple-element.27), channel_id=1, source_target_pairs={{0,1},{1,0},{2,3},{3,2},{4,5},{5,4},{6,7},{7,6},{8,9},{9,8},{10,11... | collective-permute-start | bytes 196616 | tf_op jit(solution)/shard_map/ppermute | solution.py:576
  5.0 6.8 %collective-permute-start.1 = (bf16[2,64,256]{2,1,0:T(8,128)(2,1)S(1)}, bf16[2,64,256]{2,1,0:T(8,128)(2,1)S(1)}, u32[]{:S(2)}, u32[]{:S(2)}) collective-permute-start(bf16[2,64,256]{2,1,0:T(8,128)(2,1)S(1)} %get-tuple-element.28), channel_id=1, source_target_pairs={{1,2},{3,0},{2,1},{0,3},{5,6},{7,4},{6,5},{4,7},{9,10},{11,8},{10,... | collective-permute-start | bytes 196616 | tf_op jit(solution)/shard_map/ppermute | solution.py:577
  7.5 7.5 %collective-permute-start.4 = (bf16[6,64,256]{2,1,0:T(8,128)(2,1)S(1)}, bf16[6,64,256]{2,1,0:T(8,128)(2,1)S(1)}, u32[]{:S(2)}, u32[]{:S(2)}) collective-permute-start(bf16[6,64,256]{2,1,0:T(8,128)(2,1)S(1)} %get-tuple-element.32), channel_id=1, source_target_pairs={{0,1},{1,0},{2,3},{3,2},{4,5},{5,4},{6,7},{7,6},{8,9},{9,8},{10,11... | collective-permute-start | bytes 589832 | tf_op jit(solution)/shard_map/ppermute | solution.py:576
  8.2 11.4 %collective-permute-start.5 = (bf16[6,64,256]{2,1,0:T(8,128)(2,1)S(1)}, bf16[6,64,256]{2,1,0:T(8,128)(2,1)S(1)}, u32[]{:S(2)}, u32[]{:S(2)}) collective-permute-start(bf16[6,64,256]{2,1,0:T(8,128)(2,1)S(1)} %get-tuple-element.33), channel_id=1, source_target_pairs={{1,2},{3,0},{2,1},{0,3},{5,6},{7,4},{6,5},{4,7},{9,10},{11,8},{10,... | collective-permute-start | bytes 589832 | tf_op jit(solution)/shard_map/ppermute | solution.py:577
  11.9 2.4 %collective-permute-start.2 = (bf16[256,256]{1,0:T(8,128)(2,1)S(1)}, bf16[256,256]{1,0:T(8,128)(2,1)S(1)}, u32[]{:S(2)}, u32[]{:S(2)}) collective-permute-start(bf16[256,256]{1,0:T(8,128)(2,1)S(1)} %get-tuple-element.29), channel_id=1, source_target_pairs={{0,4},{4,0},{8,12},{12,8},{1,5},{5,1},{9,13},{13,9},{2,6},{6,2},{1... | collective-permute-start | bytes 393224 | tf_op jit(solution)/shard_map/ppermute | solution.py:583
  11.9 2.3 %collective-permute-start.3 = (bf16[256,256]{1,0:T(8,128)(2,1)S(1)}, bf16[256,256]{1,0:T(8,128)(2,1)S(1)}, u32[]{:S(2)}, u32[]{:S(2)}) collective-permute-start(bf16[256,256]{1,0:T(8,128)(2,1)S(1)} %get-tuple-element.30), channel_id=1, source_target_pairs={{4,8},{8,4},{5,9},{9,5},{6,10},{10,6},{7,11},{11,7},{20,24},{24,20... | collective-permute-start | bytes 393224 | tf_op jit(solution)/shard_map/ppermute | solution.py:582
  22.9 2.0 %collective-permute-start.10 = (bf16[2,4,2,64,256]{4,3,2,1,0:T(8,128)(2,1)S(1)}, bf16[2,4,2,64,256]{4,3,2,1,0:T(8,128)(2,1)S(1)}, u32[]{:S(2)}, u32[]{:S(2)}) collective-permute-start(bf16[2,4,2,64,256]{4,3,2,1,0:T(8,128)(2,1)S(1)} %get-tuple-element.42), channel_id=1, source_target_pairs={{0,4},{4,0},{8,12},{12,8},{1,5},{5,1},{9,13},{13,9},{2,6},{6,2},{1... | collective-permute-start | bytes 1572872 | tf_op jit(solution)/shard_map/ppermute | solution.py:541
  23.9 32.3 %copy-start = (bf16[8,256,256]{2,1,0:T(8,128)(2,1)S(1)}, bf16[8,256,256]{2,1,0:T(8,128)(2,1)}, u32[]{:S(2)}) copy-start(bf16[8,256,256]{2,1,0:T(8,128)(2,1)} %mixing.3) | copy-start | bytes 3145732
  25.1 8.4 %collective-permute-start.11 = (bf16[1,4,2,64,256]{4,3,2,1,0:T(8,128)(2,1)S(1)}, bf16[1,4,2,64,256]{4,3,2,1,0:T(8,128)(2,1)S(1)}, u32[]{:S(2)}, u32[]{:S(2)}) collective-permute-start(bf16[1,4,2,64,256]{4,3,2,1,0:T(8,128)(2,1)S(1)} %slice.51), channel_id=1, source_target_pairs={{0,8},{4,12},{8,0},{12,4},{1,9},{5,13},{9,1},{13,5},{2,10},{6,14},... | collective-permute-start | bytes 786440 | tf_op jit(solution)/shard_map/ppermute | solution.py:541
  33.6 7.4 %collective-permute-start.12 = (bf16[2,64,256]{2,1,0:T(8,128)(2,1)S(1)}, bf16[2,64,256]{2,1,0:T(8,128)(2,1)S(1)}, u32[]{:S(2)}, u32[]{:S(2)}) collective-permute-start(bf16[2,64,256]{2,1,0:T(8,128)(2,1)S(1)} %get-tuple-element.45), channel_id=1, source_target_pairs={{0,1},{1,0},{2,3},{3,2},{4,5},{5,4},{6,7},{7,6},{8,9},{9,8},{10,11... | collective-permute-start | bytes 196616 | tf_op jit(solution)/shard_map/ppermute | solution.py:552
  34.2 6.7 %collective-permute-start.14 = (bf16[2,64,256]{2,1,0:T(8,128)(2,1)S(1)}, bf16[2,64,256]{2,1,0:T(8,128)(2,1)S(1)}, u32[]{:S(2)}, u32[]{:S(2)}) collective-permute-start(bf16[2,64,256]{2,1,0:T(8,128)(2,1)S(1)} %get-tuple-element.46), channel_id=1, source_target_pairs={{0,3},{1,2},{2,1},{3,0},{4,7},{5,6},{6,5},{7,4},{8,11},{9,10},{10,... | collective-permute-start | bytes 196616 | tf_op jit(solution)/shard_map/ppermute | solution.py:552
  36.6 6.9 %collective-permute-start.13 = (bf16[2,64,256]{2,1,0:T(8,128)(2,1)S(1)}, bf16[2,64,256]{2,1,0:T(8,128)(2,1)S(1)}, u32[]{:S(2)}, u32[]{:S(2)}) collective-permute-start(bf16[2,64,256]{2,1,0:T(8,128)(2,1)S(1)} %get-tuple-element.47), channel_id=1, source_target_pairs={{0,2},{1,3},{2,0},{3,1},{4,6},{5,7},{6,4},{7,5},{8,10},{9,11},{10,... | collective-permute-start | bytes 196616 | tf_op jit(solution)/shard_map/ppermute | solution.py:552
  37.1 10.2 %collective-permute-start.6 = (bf16[8,64,256]{2,1,0:T(8,128)(2,1)S(1)}, bf16[8,64,256]{2,1,0:T(8,128)(2,1)S(1)}, u32[]{:S(2)}, u32[]{:S(2)}) collective-permute-start(bf16[8,64,256]{2,1,0:T(8,128)(2,1)S(1)} %get-tuple-element.35), channel_id=1, source_target_pairs={{0,1},{1,0},{2,3},{3,2},{4,5},{5,4},{6,7},{7,6},{8,9},{9,8},{10,11... | collective-permute-start | bytes 786440 | tf_op jit(solution)/shard_map/ppermute | solution.py:576
  38.6 13.8 %collective-permute-start.7 = (bf16[8,64,256]{2,1,0:T(8,128)(2,1)S(1)}, bf16[8,64,256]{2,1,0:T(8,128)(2,1)S(1)}, u32[]{:S(2)}, u32[]{:S(2)}) collective-permute-start(bf16[8,64,256]{2,1,0:T(8,128)(2,1)S(1)} %get-tuple-element.36), channel_id=1, source_target_pairs={{1,2},{3,0},{2,1},{0,3},{5,6},{7,4},{6,5},{4,7},{9,10},{11,8},{10,... | collective-permute-start | bytes 786440 | tf_op jit(solution)/shard_map/ppermute | solution.py:577
  43.5 9.8 %collective-permute-start.15 = (bf16[1,2,64,256]{3,2,1,0:T(8,128)(2,1)S(1)}, bf16[1,2,64,256]{3,2,1,0:T(8,128)(2,1)S(1)}, u32[]{:S(2)}, u32[]{:S(2)}) collective-permute-start(bf16[1,2,64,256]{3,2,1,0:T(8,128)(2,1)S(1)} %fusion.4), channel_id=1, source_target_pairs={{0,8},{4,12},{8,0},{12,4},{1,9},{5,13},{9,1},{13,5},{2,10},{6,14},... | collective-permute-start | bytes 196616 | tf_op jit(solution)/shard_map/ppermute | solution.py:557
  52.5 9.2 %collective-permute-start.8 = (bf16[264,256]{1,0:T(8,128)(2,1)S(1)}, bf16[264,256]{1,0:T(8,128)(2,1)S(1)}, u32[]{:S(2)}, u32[]{:S(2)}) collective-permute-start(bf16[264,256]{1,0:T(8,128)(2,1)S(1)} %get-tuple-element.39), channel_id=1, source_target_pairs={{0,4},{4,0},{8,12},{12,8},{1,5},{5,1},{9,13},{13,9},{2,6},{6,2},{1... | collective-permute-start | bytes 405512 | tf_op jit(solution)/shard_map/ppermute | solution.py:583
  52.6 9.1 %collective-permute-start.9 = (bf16[264,256]{1,0:T(8,128)(2,1)S(1)}, bf16[264,256]{1,0:T(8,128)(2,1)S(1)}, u32[]{:S(2)}, u32[]{:S(2)}) collective-permute-start(bf16[264,256]{1,0:T(8,128)(2,1)S(1)} %get-tuple-element.40), channel_id=1, source_target_pairs={{4,8},{8,4},{5,9},{9,5},{6,10},{10,6},{7,11},{11,7},{20,24},{24,20... | collective-permute-start | bytes 405512 | tf_op jit(solution)/shard_map/ppermute | solution.py:582
  53.3 10.6 %collective-permute-start.16 = (bf16[2,2,64,256]{3,2,1,0:T(8,128)(2,1)S(1)}, bf16[2,2,64,256]{3,2,1,0:T(8,128)(2,1)S(1)}, u32[]{:S(2)}, u32[]{:S(2)}) collective-permute-start(bf16[2,2,64,256]{3,2,1,0:T(8,128)(2,1)S(1)} %pad_maximum_fusion.mine), channel_id=1, source_target_pairs={{0,4},{4,0},{8,12},{12,8},{1,5},{5,1},{9,13},{13,9},{2,6},{6,2},{1... | collective-permute-start | bytes 393224 | tf_op jit(solution)/shard_map/ppermute | solution.py:557

commit v5 on v4

--- a/solution.py
+++ b/solution.py
@@ -455,60 +455,71 @@
     )
 
 
-def mixed_rows(source, mixing, cols, store):
+def mixed_rows(source, mixing, first, count, cols, store):
     total = None
     for k in range(mixing.shape[0]):
         term = lax.dot_general(
-            source[k], mixing[k], (((1,), (1,)), ((), ())), preferred_element_type=jnp.float32
+            source[k, first * cols : (first + count) * cols, :],
+            mixing[k],
+            (((1,), (1,)), ((), ())),
+            preferred_element_type=jnp.float32,
         )
         total = term if total is None else total + term
     total = total.astype(jnp.bfloat16)
     back = mirror(cols)
-    for i in range(total.shape[0] // cols):
+    for i in range(count):
         part = total[i * cols : (i + 1) * cols]
         store(i, jnp.dot(back, part, preferred_element_type=jnp.float32).astype(jnp.bfloat16))
 
 
-def inner_mix_kernel(mixing, inner, out):
+def inner_mix_kernel(first, mixing, inner, out):
     def store(i, value):
         out[i] = value
 
-    mixed_rows(inner, mixing, out.shape[1], store)
-
-
-def inner_mix(mixing, inner, cols):
-    _, chans, _ = mixing.shape
-    shape = (inner.shape[1] // cols, cols, chans)
-    return kernel_call(inner_mix_kernel, [mixing, inner], pltpu.VMEM(shape, jnp.bfloat16), [], 8)
-
-
-def back_mix_kernel(mixing, inner, filt, out, stage, sems):
+    mixed_rows(inner, mixing, first, out.shape[0], out.shape[1], store)
+
+
+def inner_mix(mixing, inner, first, count, cols):
+    shape = (count, cols, mixing.shape[1])
+    return kernel_call(
+        functools.partial(inner_mix_kernel, first),
+        [mixing, inner],
+        pltpu.VMEM(shape, jnp.bfloat16),
+        [],
+        8,
+    )
+
+
+def back_mix_kernel(mixing, upper, lower, filt, out, stage, sems):
     rows, cols, _ = out.shape
+    split = 1 + upper.shape[0]
     copies = [
-        pltpu.make_async_copy(inner, out.at[pl.ds(1, rows - 2)], sems.at[0]),
-        pltpu.make_async_copy(stage.at[0], out.at[0], sems.at[1]),
-        pltpu.make_async_copy(stage.at[1], out.at[rows - 1], sems.at[2]),
+        pltpu.make_async_copy(upper, out.at[pl.ds(1, upper.shape[0])], sems.at[0]),
+        pltpu.make_async_copy(lower, out.at[pl.ds(split, lower.shape[0])], sems.at[1]),
+        pltpu.make_async_copy(stage.at[0], out.at[0], sems.at[2]),
+        pltpu.make_async_copy(stage.at[1], out.at[rows - 1], sems.at[3]),
     ]
     copies[0].start()
+    copies[1].start()
 
     def store(i, value):
         stage[i] = value
 
-    mixed_rows(filt, mixing, cols, store)
-    copies[1].start()
+    mixed_rows(filt, mixing, 0, 2, cols, store)
     copies[2].start()
+    copies[3].start()
     for copy in copies:
         copy.wait()
 
 
-def back_mix(mixing, inner, filt, rows):
+def back_mix(mixing, upper, lower, filt, rows):
     _, chans, _ = mixing.shape
     cols = filt.shape[1] // 2
     return kernel_call(
         back_mix_kernel,
-        [mixing, inner, filt],
+        [mixing, upper, lower, filt],
         jax.ShapeDtypeStruct((rows, cols, chans), jnp.bfloat16),
-        [pltpu.VMEM((2, cols, chans), jnp.bfloat16), pltpu.SemaphoreType.DMA((3,))],
+        [pltpu.VMEM((2, cols, chans), jnp.bfloat16), pltpu.SemaphoreType.DMA((4,))],
         8,
         far_out=True,
     )
@@ -622,7 +633,10 @@
     g_core, g_far = bands_beside(sent)
     inner, turned = backward_inner(bands, cot_near, *g_sides, window)
     edge = backward_edges(bands, g_core, g_far, turned, cols, window)
-    input_grad = back_mix(mixing, inner_mix(mixing, inner, cols), edge, rows)
+    half = (rows - 2) // 2
+    upper = inner_mix(mixing, inner, 0, half, cols)
+    lower = inner_mix(mixing, inner, half, rows - 2 - half, cols)
+    input_grad = back_mix(mixing, upper, lower, edge, rows)
     return (
         field_out.reshape(rows, cols, outs),
         input_grad,

time: 64.9 us -> 65.4 us (level)
    pallas_call x13 -> x14, Pallas kernels: 17.1 us -> 17.6 us  [kernel_call(): pl.pallas_call(body, in_specs=specs, out_specs=place if single else [plac...]
  transfers between devices with their start and end apart: 17 -> 17, of which waited for: 8 -> 8; matrix products, arithmetic and copies ran while one was open for 0% -> 0% of each run, Pallas kernels for 18% -> 19%
where the time goes in v5:
time: 65.4 us; the launch traced here: 65.2 us
  waiting for transfers between devices  24.3 us (37%)
  starting transfers between devices  22.2 us (34%)
  Pallas kernels  17.6 us (27%)
  between operations  0.87 us (1%)
    pallas_call x14, Pallas kernels, kernel_call(): pl.pallas_call(body, in_specs=specs, out_specs=place if single else [plac...  17.6 us
    ppermute x3, waiting for transfers between devices, beside(): lax.ppermute(pair[1], 'lon', other + [(j, i) for i, j in other])  11.1 us
    ppermute x2, waiting for transfers between devices, reduced_gradient(): other = lax.ppermute(send, 'lat', swap('lat', mask))  7.78 us
    ppermute x3, starting transfers between devices, beside(): lax.ppermute(pair[1], 'lon', other + [(j, i) for i, j in other])  5.73 us
    ppermute x3, starting transfers between devices, beside(): lax.ppermute(pair[0], 'lon', swap('lon', 1))  5.28 us
    ppermute x2, starting transfers between devices, reduced_gradient(): other = lax.ppermute(pieces, 'lat', swap('lat', mask))  4.52 us
    ppermute x3, starting transfers between devices, reduced_gradient(): other = lax.ppermute(wire[s], 'lon', swap('lon', s))  3.55 us
    ppermute x3, waiting for transfers between devices, beside(): lax.ppermute(pair[0], 'lon', swap('lon', 1))  2.93 us
  transfers between devices with their start and end apart: 17, of which 8 were waited for; matrix products, arithmetic and copies ran while one was open for 0% of the time, Pallas kernels for 19%

profile of v5, /device:TPU:0, one launch (start us, length us, event | category | flops | bytes accessed | tf_op | source)
XLA Modules:
  0.0 65.2 jit_solution(18232519397911466232)
XLA Ops:
  0.6 1.3 %shard_map.78 = (bf16[2,64,256]{2,1,0:T(8,128)(2,1)S(1)}, bf16[2,64,256]{2,1,0:T(8,128)(2,1)S(1)}, bf16[6,64,256]{2,1,0:T(8,128)(2,1)S(1)}, bf16[6,64,256]{2,1,0:T(8,128)(2,1)S(1)}) custom-call(bf16[8,128,256]{2,1,0:T(8,128)(2,1)} %field.3), custom_call_target="tpu_custom_call" | custom-call | tf_op jit(solution)/shard_map/pallas_call | solution.py:37
  1.9 3.1 %collective-permute-start = (bf16[2,64,256]{2,1,0:T(8,128)(2,1)S(1)}, bf16[2,64,256]{2,1,0:T(8,128)(2,1)S(1)}, u32[]{:S(2)}, u32[]{:S(2)}) collective-permute-start(bf16[2,64,256]{2,1,0:T(8,128)(2,1)S(1)} %get-tuple-element.27), channel_id=1, source_target_pairs={{0,1},{1,0},{2,3},{3,2},{4,5},{5,4},{6,7},{7,6},{8,9},{9,8},{10,11... | collective-permute-start | bytes 196616 | tf_op jit(solution)/shard_map/ppermute | solution.py:587
  5.0 2.5 %collective-permute-start.1 = (bf16[2,64,256]{2,1,0:T(8,128)(2,1)S(1)}, bf16[2,64,256]{2,1,0:T(8,128)(2,1)S(1)}, u32[]{:S(2)}, u32[]{:S(2)}) collective-permute-start(bf16[2,64,256]{2,1,0:T(8,128)(2,1)S(1)} %get-tuple-element.28), channel_id=1, source_target_pairs={{1,2},{3,0},{2,1},{0,3},{5,6},{7,4},{6,5},{4,7},{9,10},{11,8},{10,... | collective-permute-start | bytes 196616 | tf_op jit(solution)/shard_map/ppermute | solution.py:588
  7.5 0.7 %collective-permute-start.4 = (bf16[6,64,256]{2,1,0:T(8,128)(2,1)S(1)}, bf16[6,64,256]{2,1,0:T(8,128)(2,1)S(1)}, u32[]{:S(2)}, u32[]{:S(2)}) collective-permute-start(bf16[6,64,256]{2,1,0:T(8,128)(2,1)S(1)} %get-tuple-element.32), channel_id=1, source_target_pairs={{0,1},{1,0},{2,3},{3,2},{4,5},{5,4},{6,7},{7,6},{8,9},{9,8},{10,11... | collective-permute-start | bytes 589832 | tf_op jit(solution)/shard_map/ppermute | solution.py:587
  8.2 0.9 %collective-permute-start.5 = (bf16[6,64,256]{2,1,0:T(8,128)(2,1)S(1)}, bf16[6,64,256]{2,1,0:T(8,128)(2,1)S(1)}, u32[]{:S(2)}, u32[]{:S(2)}) collective-permute-start(bf16[6,64,256]{2,1,0:T(8,128)(2,1)S(1)} %get-tuple-element.33), channel_id=1, source_target_pairs={{1,2},{3,0},{2,1},{0,3},{5,6},{7,4},{6,5},{4,7},{9,10},{11,8},{10,... | collective-permute-start | bytes 589832 | tf_op jit(solution)/shard_map/ppermute | solution.py:588
  9.1 1.5 %shard_map.76 = (bf16[8,64,256]{2,1,0:T(8,128)(2,1)S(1)}, bf16[8,64,256]{2,1,0:T(8,128)(2,1)S(1)}, bf16[8,128,256]{2,1,0:T(8,128)(2,1)S(1)}, bf16[8,128,256]{2,1...) custom-call(bf16[8,128,256]{2,1,0:T(8,128)(2,1)} %field.3, bf16[8,128,256]{2,1,0:T(8,128)(2,1)} %cot.1, ...), custom_call_target="tpu_custom_call" | custom-call | tf_op jit(solution)/shard_map/pallas_call | solution.py:37
  10.6 0.0 collective-permute-done.paired.rest_0_
  10.6 1.3 %collective-permute-done.1.other.rest_1_ = bf16[2,64,256]{2,1,0:T(8,128)(2,1)S(1)} collective-permute-done((bf16[2,64,256]{2,1,0:T(8,128)(2,1)S(1)}, bf16[2,64,256]{2,1,0:T(8,128)(2,1)S(1)}, u32[]{:S(2)}, u32[]{:S(2)}) %collective-permute-start.1) | collective-permute-done | bytes 65568 | tf_op jit(solution)/shard_map/ppermute | solution.py:588
  11.9 0.1 collective-permute-start.2
  11.9 0.7 %collective-permute-start.3 = (bf16[256,256]{1,0:T(8,128)(2,1)S(1)}, bf16[256,256]{1,0:T(8,128)(2,1)S(1)}, u32[]{:S(2)}, u32[]{:S(2)}) collective-permute-start(bf16[256,256]{1,0:T(8,128)(2,1)S(1)} %get-tuple-element.30), channel_id=1, source_target_pairs={{4,8},{8,4},{5,9},{9,5},{6,10},{10,6},{7,11},{11,7},{20,24},{24,20... | collective-permute-start | bytes 393224 | tf_op jit(solution)/shard_map/ppermute | solution.py:593
  12.6 1.6 %shard_map.77 = (bf16[8,256,512]{2,1,0:T(8,128)(2,1)S(1)}, bf16[2,8,256]{2,1,0:T(8,128)(2,1)S(1)}) custom-call(s32[8,128]{1,0:T(8,128)S(1)} %get-tuple-element.23.reach, f32[8,3,8,129]{3,2,1,0:T(8,128)S(1)} %get-tuple-element.24.quadrature), custom_call_target="tpu_custom_call" | custom-call | tf_op jit(solution)/shard_map/pallas_call | solution.py:37
  14.2 0.0 collective-permute-done.2.core
  14.2 0.0 collective-permute-done.3.far
  14.3 0.7 %collective-permute-done.4.rest_2_ = bf16[6,64,256]{2,1,0:T(8,128)(2,1)S(1)} collective-permute-done((bf16[6,64,256]{2,1,0:T(8,128)(2,1)S(1)}, bf16[6,64,256]{2,1,0:T(8,128)(2,1)S(1)}, u32[]{:S(2)}, u32[]{:S(2)}) %collective-permute-start.4) | collective-permute-done | bytes 196640 | tf_op jit(solution)/shard_map/ppermute | solution.py:587
  15.0 4.6 %collective-permute-done.5.rest_3_ = bf16[6,64,256]{2,1,0:T(8,128)(2,1)S(1)} collective-permute-done((bf16[6,64,256]{2,1,0:T(8,128)(2,1)S(1)}, bf16[6,64,256]{2,1,0:T(8,128)(2,1)S(1)}, u32[]{:S(2)}, u32[]{:S(2)}) %collective-permute-start.5) | collective-permute-done | bytes 196640 | tf_op jit(solution)/shard_map/ppermute | solution.py:588
  19.6 3.3 %shard_map.80 = (bf16[1024,2048]{1,0:T(8,128)(2,1)S(1)}, bf16[2,4,2,64,256]{4,3,2,1,0:T(8,128)(2,1)S(1)}) custom-call(bf16[8,256,512]{2,1,0:T(8,128)(2,1)S(1)} %get-tuple-element.25.bands, bf16[8,128,256]{2,1,0:T(8,128)(2,1)S(1)} %get-tuple-element.26.own, bf16[256,256]{1,0:T(8,128)(2,1)S(1)} %collective-permute-done.2.core, ...), custom_call_target="tpu_custom_call" | custom-call | tf_op jit(solution)/shard_map/pallas_call | solution.py:37
  22.9 0.1 collective-permute-start.10
  23.0 0.9 %shard_map.88 = f32[2,4,2,64,256]{4,3,2,1,0:T(8,128)S(1)} custom-call(bf16[1024,2048]{1,0:T(8,128)(2,1)S(1)} %get-tuple-element.34.filt, bf16[1024,256]{1,0:T(8,128)(2,1)S(1)} %bitcast.25), custom_call_target="tpu_custom_call" | custom-call | tf_op jit(solution)/shard_map/pallas_call | solution.py:37
  23.9 0.0 copy-start
  23.9 1.0 %collective-permute-done.10 = bf16[2,4,2,64,256]{4,3,2,1,0:T(8,128)(2,1)S(1)} collective-permute-done((bf16[2,4,2,64,256]{4,3,2,1,0:T(8,128)(2,1)S(1)}, bf16[2,4,2,64,256]{4,3,2,1,0:T(8,128)(2,1)S(1)}, u32[]{:S(2)}, u32[]{:S(2)}) %collective-permute-start.10) | collective-permute-done | bytes 524320 | tf_op jit(solution)/shard_map/ppermute | solution.py:552
  24.9 0.1 convert_add_fusion
  25.1 1.6 %collective-permute-start.11 = (bf16[1,4,2,64,256]{4,3,2,1,0:T(8,128)(2,1)S(1)}, bf16[1,4,2,64,256]{4,3,2,1,0:T(8,128)(2,1)S(1)}, u32[]{:S(2)}, u32[]{:S(2)}) collective-permute-start(bf16[1,4,2,64,256]{4,3,2,1,0:T(8,128)(2,1)S(1)} %slice.51), channel_id=1, source_target_pairs={{0,8},{4,12},{8,0},{12,4},{1,9},{5,13},{9,1},{13,5},{2,10},{6,14},... | collective-permute-start | bytes 786440 | tf_op jit(solution)/shard_map/ppermute | solution.py:552
  26.6 6.8 %collective-permute-done.11 = bf16[1,4,2,64,256]{4,3,2,1,0:T(8,128)(2,1)S(1)} collective-permute-done((bf16[1,4,2,64,256]{4,3,2,1,0:T(8,128)(2,1)S(1)}, bf16[1,4,2,64,256]{4,3,2,1,0:T(8,128)(2,1)S(1)}, u32[]{:S(2)}, u32[]{:S(2)}) %collective-permute-start.11) | collective-permute-done | bytes 262176 | tf_op jit(solution)/shard_map/ppermute | solution.py:552
  33.5 0.1 fusion.5
  33.6 0.7 collective-permute-start.12
  34.2 2.4 %collective-permute-start.14 = (bf16[2,64,256]{2,1,0:T(8,128)(2,1)S(1)}, bf16[2,64,256]{2,1,0:T(8,128)(2,1)S(1)}, u32[]{:S(2)}, u32[]{:S(2)}) collective-permute-start(bf16[2,64,256]{2,1,0:T(8,128)(2,1)S(1)} %get-tuple-element.46), channel_id=1, source_target_pairs={{0,3},{1,2},{2,1},{3,0},{4,7},{5,6},{6,5},{7,4},{8,11},{9,10},{10,... | collective-permute-start | bytes 196616 | tf_op jit(solution)/shard_map/ppermute | solution.py:563
  36.6 0.5 collective-permute-start.13
  37.1 1.5 %collective-permute-start.6 = (bf16[8,64,256]{2,1,0:T(8,128)(2,1)S(1)}, bf16[8,64,256]{2,1,0:T(8,128)(2,1)S(1)}, u32[]{:S(2)}, u32[]{:S(2)}) collective-permute-start(bf16[8,64,256]{2,1,0:T(8,128)(2,1)S(1)} %get-tuple-element.35), channel_id=1, source_target_pairs={{0,1},{1,0},{2,3},{3,2},{4,5},{5,4},{6,7},{7,6},{8,9},{9,8},{10,11... | collective-permute-start | bytes 786440 | tf_op jit(solution)/shard_map/ppermute | solution.py:587
  38.6 2.4 %collective-permute-start.7 = (bf16[8,64,256]{2,1,0:T(8,128)(2,1)S(1)}, bf16[8,64,256]{2,1,0:T(8,128)(2,1)S(1)}, u32[]{:S(2)}, u32[]{:S(2)}) collective-permute-start(bf16[8,64,256]{2,1,0:T(8,128)(2,1)S(1)} %get-tuple-element.36), channel_id=1, source_target_pairs={{1,2},{3,0},{2,1},{0,3},{5,6},{7,4},{6,5},{4,7},{9,10},{11,8},{10,... | collective-permute-start | bytes 786440 | tf_op jit(solution)/shard_map/ppermute | solution.py:588
  41.0 0.0 collective-permute-done.12
  41.0 0.0 collective-permute-done.14
  41.0 2.5 %collective-permute-done.13 = bf16[2,64,256]{2,1,0:T(8,128)(2,1)S(1)} collective-permute-done((bf16[2,64,256]{2,1,0:T(8,128)(2,1)S(1)}, bf16[2,64,256]{2,1,0:T(8,128)(2,1)S(1)}, u32[]{:S(2)}, u32[]{:S(2)}) %collective-permute-start.13) | collective-permute-done | bytes 65568 | tf_op jit(solution)/shard_map/ppermute | solution.py:563
  43.5 1.6 %collective-permute-start.15 = (bf16[1,2,64,256]{3,2,1,0:T(8,128)(2,1)S(1)}, bf16[1,2,64,256]{3,2,1,0:T(8,128)(2,1)S(1)}, u32[]{:S(2)}, u32[]{:S(2)}) collective-permute-start(bf16[1,2,64,256]{3,2,1,0:T(8,128)(2,1)S(1)} %fusion.4), channel_id=1, source_target_pairs={{0,8},{4,12},{8,0},{12,4},{1,9},{5,13},{9,1},{13,5},{2,10},{6,14},... | collective-permute-start | bytes 196616 | tf_op jit(solution)/shard_map/ppermute | solution.py:568
  45.1 2.2 %collective-permute-done.6.paired = bf16[8,64,256]{2,1,0:T(8,128)(2,1)S(1)} collective-permute-done((bf16[8,64,256]{2,1,0:T(8,128)(2,1)S(1)}, bf16[8,64,256]{2,1,0:T(8,128)(2,1)S(1)}, u32[]{:S(2)}, u32[]{:S(2)}) %collective-permute-start.6) | collective-permute-done | bytes 262176 | tf_op jit(solution)/shard_map/ppermute | solution.py:587
  47.3 5.2 %collective-permute-done.7.other = bf16[8,64,256]{2,1,0:T(8,128)(2,1)S(1)} collective-permute-done((bf16[8,64,256]{2,1,0:T(8,128)(2,1)S(1)}, bf16[8,64,256]{2,1,0:T(8,128)(2,1)S(1)}, u32[]{:S(2)}, u32[]{:S(2)}) %collective-permute-start.7) | collective-permute-done | bytes 262176 | tf_op jit(solution)/shard_map/ppermute | solution.py:588
  52.5 0.1 collective-permute-start.8
  52.6 0.7 %collective-permute-start.9 = (bf16[264,256]{1,0:T(8,128)(2,1)S(1)}, bf16[264,256]{1,0:T(8,128)(2,1)S(1)}, u32[]{:S(2)}, u32[]{:S(2)}) collective-permute-start(bf16[264,256]{1,0:T(8,128)(2,1)S(1)} %get-tuple-element.40), channel_id=1, source_target_pairs={{4,8},{8,4},{5,9},{9,5},{6,10},{10,6},{7,11},{11,7},{20,24},{24,20... | collective-permute-start | bytes 405512 | tf_op jit(solution)/shard_map/ppermute | solution.py:593
  53.2 0.0 collective-permute-done.15
  53.3 2.9 %collective-permute-start.16 = (bf16[2,2,64,256]{3,2,1,0:T(8,128)(2,1)S(1)}, bf16[2,2,64,256]{3,2,1,0:T(8,128)(2,1)S(1)}, u32[]{:S(2)}, u32[]{:S(2)}) collective-permute-start(bf16[2,2,64,256]{3,2,1,0:T(8,128)(2,1)S(1)} %pad_maximum_fusion.mine), channel_id=1, source_target_pairs={{0,4},{4,0},{8,12},{12,8},{1,5},{5,1},{9,13},{13,9},{2,6},{6,2},{1... | collective-permute-start | bytes 393224 | tf_op jit(solution)/shard_map/ppermute | solution.py:568
  56.2 2.0 %shard_map.81 = bf16[1024,256]{1,0:T(8,128)(2,1)} custom-call(bf16[1024,2048]{1,0:T(8,128)(2,1)S(1)} %get-tuple-element.34.filt, bf16[2048,256]{1,0:T(8,128)(2,1)S(1)} %bitcast.23), custom_call_target="tpu_custom_call" | custom-call | tf_op jit(solution)/shard_map/pallas_call | solution.py:37
  58.3 2.1 %shard_map.82 = (bf16[8,768,256]{2,1,0:T(8,128)(2,1)S(1)}, bf16[8,256,256]{2,1,0:T(8,128)(2,1)S(1)}) custom-call(bf16[8,256,512]{2,1,0:T(8,128)(2,1)S(1)} %get-tuple-element.25.bands, bf16[8,128,256]{2,1,0:T(8,128)(2,1)S(1)} %get-tuple-element.31.own, bf16[8,64,256]{2,1,0:T(8,128)(2,1)S(1)} %collective-permute-done.6.paired, ...), custom_call_target="tpu_custom_call" | custom-call | tf_op jit(solution)/shard_map/pallas_call | solution.py:37
  60.4 0.9 %shard_map.84.lower = bf16[3,128,256]{2,1,0:T(8,128)(2,1)S(1)} custom-call(bf16[8,256,256]{2,1,0:T(8,128)(2,1)S(1)} %copy-done, bf16[8,768,256]{2,1,0:T(8,128)(2,1)S(1)} %get-tuple-element.37.inner), custom_call_target="tpu_custom_call" | custom-call | tf_op jit(solution)/shard_map/pallas_call | solution.py:37
  61.2 0.9 %shard_map.83.upper = bf16[3,128,256]{2,1,0:T(8,128)(2,1)S(1)} custom-call(bf16[8,256,256]{2,1,0:T(8,128)(2,1)S(1)} %copy-done, bf16[8,768,256]{2,1,0:T(8,128)(2,1)S(1)} %get-tuple-element.37.inner), custom_call_target="tpu_custom_call" | custom-call | tf_op jit(solution)/shard_map/pallas_call | solution.py:37
  62.1 0.0 collective-permute-done.9.far
  62.1 0.9 %shard_map.86.filt = bf16[8,256,256]{2,1,0:T(8,128)(2,1)S(1)} custom-call(bf16[8,256,512]{2,1,0:T(8,128)(2,1)S(1)} %get-tuple-element.25.bands, bf16[264,256]{1,0:T(8,128)(2,1)S(1)} %collective-permute-done.8.core, bf16[264,256]{1,0:T(8,128)(2,1)S(1)} %collective-permute-done.9.far, bf16[8,256,256]{2,1,0:T(8,128)(2,1)S(1)} %get-tuple-element.41.turned), custom_call_target="tpu_custom_call" | custom-call | tf_op jit(solution)/shard_map/pallas_call | solution.py:37
  63.0 1.4 %shard_map.87 = bf16[8,128,256]{2,1,0:T(8,128)(2,1)} custom-call(bf16[8,256,256]{2,1,0:T(8,128)(2,1)S(1)} %copy-done, bf16[3,128,256]{2,1,0:T(8,128)(2,1)S(1)} %shard_map.83.upper, bf16[3,128,256]{2,1,0:T(8,128)(2,1)S(1)} %shard_map.84.lower, bf16[8,256,256]{2,1,0:T(8,128)(2,1)S(1)} %shard_map.86.filt), custom_call_target="tpu_custom_call" | custom-call | tf_op jit(solution)/shard_map/pallas_call | solution.py:37
  64.4 0.0 collective-permute-done.16.other
  64.4 0.8 %shard_map.89 = f32[2,256,256]{2,1,0:T(8,128)} custom-call(bf16[2,2,64,256]{3,2,1,0:T(8,128)(2,1)S(1)} %pad_maximum_fusion.mine, bf16[2,2,64,256]{3,2,1,0:T(8,128)(2,1)S(1)} %collective-permute-done.16.other), custom_call_target="tpu_custom_call" | custom-call | tf_op jit(solution)/shard_map/pallas_call | solution.py:37
  (8 shorter events, 0.1 us)
Async XLA Ops:
  1.9 8.7 %collective-permute-start = (bf16[2,64,256]{2,1,0:T(8,128)(2,1)S(1)}, bf16[2,64,256]{2,1,0:T(8,128)(2,1)S(1)}, u32[]{:S(2)}, u32[]{:S(2)}) collective-permute-start(bf16[2,64,256]{2,1,0:T(8,128)(2,1)S(1)} %get-tuple-element.27), channel_id=1, source_target_pairs={{0,1},{1,0},{2,3},{3,2},{4,5},{5,4},{6,7},{7,6},{8,9},{9,8},{10,11... | collective-permute-start | bytes 196616 | tf_op jit(solution)/shard_map/ppermute | solution.py:587
  5.0 6.8 %collective-permute-start.1 = (bf16[2,64,256]{2,1,0:T(8,128)(2,1)S(1)}, bf16[2,64,256]{2,1,0:T(8,128)(2,1)S(1)}, u32[]{:S(2)}, u32[]{:S(2)}) collective-permute-start(bf16[2,64,256]{2,1,0:T(8,128)(2,1)S(1)} %get-tuple-element.28), channel_id=1, source_target_pairs={{1,2},{3,0},{2,1},{0,3},{5,6},{7,4},{6,5},{4,7},{9,10},{11,8},{10,... | collective-permute-start | bytes 196616 | tf_op jit(solution)/shard_map/ppermute | solution.py:588
  7.5 7.5 %collective-permute-start.4 = (bf16[6,64,256]{2,1,0:T(8,128)(2,1)S(1)}, bf16[6,64,256]{2,1,0:T(8,128)(2,1)S(1)}, u32[]{:S(2)}, u32[]{:S(2)}) collective-permute-start(bf16[6,64,256]{2,1,0:T(8,128)(2,1)S(1)} %get-tuple-element.32), channel_id=1, source_target_pairs={{0,1},{1,0},{2,3},{3,2},{4,5},{5,4},{6,7},{7,6},{8,9},{9,8},{10,11... | collective-permute-start | bytes 589832 | tf_op jit(solution)/shard_map/ppermute | solution.py:587
  8.2 11.4 %collective-permute-start.5 = (bf16[6,64,256]{2,1,0:T(8,128)(2,1)S(1)}, bf16[6,64,256]{2,1,0:T(8,128)(2,1)S(1)}, u32[]{:S(2)}, u32[]{:S(2)}) collective-permute-start(bf16[6,64,256]{2,1,0:T(8,128)(2,1)S(1)} %get-tuple-element.33), channel_id=1, source_target_pairs={{1,2},{3,0},{2,1},{0,3},{5,6},{7,4},{6,5},{4,7},{9,10},{11,8},{10,... | collective-permute-start | bytes 589832 | tf_op jit(solution)/shard_map/ppermute | solution.py:588
  11.9 2.4 %collective-permute-start.2 = (bf16[256,256]{1,0:T(8,128)(2,1)S(1)}, bf16[256,256]{1,0:T(8,128)(2,1)S(1)}, u32[]{:S(2)}, u32[]{:S(2)}) collective-permute-start(bf16[256,256]{1,0:T(8,128)(2,1)S(1)} %get-tuple-element.29), channel_id=1, source_target_pairs={{0,4},{4,0},{8,12},{12,8},{1,5},{5,1},{9,13},{13,9},{2,6},{6,2},{1... | collective-permute-start | bytes 393224 | tf_op jit(solution)/shard_map/ppermute | solution.py:594
  11.9 2.3 %collective-permute-start.3 = (bf16[256,256]{1,0:T(8,128)(2,1)S(1)}, bf16[256,256]{1,0:T(8,128)(2,1)S(1)}, u32[]{:S(2)}, u32[]{:S(2)}) collective-permute-start(bf16[256,256]{1,0:T(8,128)(2,1)S(1)} %get-tuple-element.30), channel_id=1, source_target_pairs={{4,8},{8,4},{5,9},{9,5},{6,10},{10,6},{7,11},{11,7},{20,24},{24,20... | collective-permute-start | bytes 393224 | tf_op jit(solution)/shard_map/ppermute | solution.py:593
  22.9 2.0 %collective-permute-start.10 = (bf16[2,4,2,64,256]{4,3,2,1,0:T(8,128)(2,1)S(1)}, bf16[2,4,2,64,256]{4,3,2,1,0:T(8,128)(2,1)S(1)}, u32[]{:S(2)}, u32[]{:S(2)}) collective-permute-start(bf16[2,4,2,64,256]{4,3,2,1,0:T(8,128)(2,1)S(1)} %get-tuple-element.42), channel_id=1, source_target_pairs={{0,4},{4,0},{8,12},{12,8},{1,5},{5,1},{9,13},{13,9},{2,6},{6,2},{1... | collective-permute-start | bytes 1572872 | tf_op jit(solution)/shard_map/ppermute | solution.py:552
  23.9 32.3 %copy-start = (bf16[8,256,256]{2,1,0:T(8,128)(2,1)S(1)}, bf16[8,256,256]{2,1,0:T(8,128)(2,1)}, u32[]{:S(2)}) copy-start(bf16[8,256,256]{2,1,0:T(8,128)(2,1)} %mixing.5) | copy-start | bytes 3145732
  25.1 8.4 %collective-permute-start.11 = (bf16[1,4,2,64,256]{4,3,2,1,0:T(8,128)(2,1)S(1)}, bf16[1,4,2,64,256]{4,3,2,1,0:T(8,128)(2,1)S(1)}, u32[]{:S(2)}, u32[]{:S(2)}) collective-permute-start(bf16[1,4,2,64,256]{4,3,2,1,0:T(8,128)(2,1)S(1)} %slice.51), channel_id=1, source_target_pairs={{0,8},{4,12},{8,0},{12,4},{1,9},{5,13},{9,1},{13,5},{2,10},{6,14},... | collective-permute-start | bytes 786440 | tf_op jit(solution)/shard_map/ppermute | solution.py:552
  33.6 7.4 %collective-permute-start.12 = (bf16[2,64,256]{2,1,0:T(8,128)(2,1)S(1)}, bf16[2,64,256]{2,1,0:T(8,128)(2,1)S(1)}, u32[]{:S(2)}, u32[]{:S(2)}) collective-permute-start(bf16[2,64,256]{2,1,0:T(8,128)(2,1)S(1)} %get-tuple-element.45), channel_id=1, source_target_pairs={{0,1},{1,0},{2,3},{3,2},{4,5},{5,4},{6,7},{7,6},{8,9},{9,8},{10,11... | collective-permute-start | bytes 196616 | tf_op jit(solution)/shard_map/ppermute | solution.py:563
  34.2 6.7 %collective-permute-start.14 = (bf16[2,64,256]{2,1,0:T(8,128)(2,1)S(1)}, bf16[2,64,256]{2,1,0:T(8,128)(2,1)S(1)}, u32[]{:S(2)}, u32[]{:S(2)}) collective-permute-start(bf16[2,64,256]{2,1,0:T(8,128)(2,1)S(1)} %get-tuple-element.46), channel_id=1, source_target_pairs={{0,3},{1,2},{2,1},{3,0},{4,7},{5,6},{6,5},{7,4},{8,11},{9,10},{10,... | collective-permute-start | bytes 196616 | tf_op jit(solution)/shard_map/ppermute | solution.py:563
  36.6 6.9 %collective-permute-start.13 = (bf16[2,64,256]{2,1,0:T(8,128)(2,1)S(1)}, bf16[2,64,256]{2,1,0:T(8,128)(2,1)S(1)}, u32[]{:S(2)}, u32[]{:S(2)}) collective-permute-start(bf16[2,64,256]{2,1,0:T(8,128)(2,1)S(1)} %get-tuple-element.47), channel_id=1, source_target_pairs={{0,2},{1,3},{2,0},{3,1},{4,6},{5,7},{6,4},{7,5},{8,10},{9,11},{10,... | collective-permute-start | bytes 196616 | tf_op jit(solution)/shard_map/ppermute | solution.py:563
  37.1 10.2 %collective-permute-start.6 = (bf16[8,64,256]{2,1,0:T(8,128)(2,1)S(1)}, bf16[8,64,256]{2,1,0:T(8,128)(2,1)S(1)}, u32[]{:S(2)}, u32[]{:S(2)}) collective-permute-start(bf16[8,64,256]{2,1,0:T(8,128)(2,1)S(1)} %get-tuple-element.35), channel_id=1, source_target_pairs={{0,1},{1,0},{2,3},{3,2},{4,5},{5,4},{6,7},{7,6},{8,9},{9,8},{10,11... | collective-permute-start | bytes 786440 | tf_op jit(solution)/shard_map/ppermute | solution.py:587
  38.6 13.8 %collective-permute-start.7 = (bf16[8,64,256]{2,1,0:T(8,128)(2,1)S(1)}, bf16[8,64,256]{2,1,0:T(8,128)(2,1)S(1)}, u32[]{:S(2)}, u32[]{:S(2)}) collective-permute-start(bf16[8,64,256]{2,1,0:T(8,128)(2,1)S(1)} %get-tuple-element.36), channel_id=1, source_target_pairs={{1,2},{3,0},{2,1},{0,3},{5,6},{7,4},{6,5},{4,7},{9,10},{11,8},{10,... | collective-permute-start | bytes 786440 | tf_op jit(solution)/shard_map/ppermute | solution.py:588
  43.5 9.8 %collective-permute-start.15 = (bf16[1,2,64,256]{3,2,1,0:T(8,128)(2,1)S(1)}, bf16[1,2,64,256]{3,2,1,0:T(8,128)(2,1)S(1)}, u32[]{:S(2)}, u32[]{:S(2)}) collective-permute-start(bf16[1,2,64,256]{3,2,1,0:T(8,128)(2,1)S(1)} %fusion.4), channel_id=1, source_target_pairs={{0,8},{4,12},{8,0},{12,4},{1,9},{5,13},{9,1},{13,5},{2,10},{6,14},... | collective-permute-start | bytes 196616 | tf_op jit(solution)/shard_map/ppermute | solution.py:568
  52.5 9.6 %collective-permute-start.8 = (bf16[264,256]{1,0:T(8,128)(2,1)S(1)}, bf16[264,256]{1,0:T(8,128)(2,1)S(1)}, u32[]{:S(2)}, u32[]{:S(2)}) collective-permute-start(bf16[264,256]{1,0:T(8,128)(2,1)S(1)} %get-tuple-element.39), channel_id=1, source_target_pairs={{0,4},{4,0},{8,12},{12,8},{1,5},{5,1},{9,13},{13,9},{2,6},{6,2},{1... | collective-permute-start | bytes 405512 | tf_op jit(solution)/shard_map/ppermute | solution.py:594
  52.6 9.5 %collective-permute-start.9 = (bf16[264,256]{1,0:T(8,128)(2,1)S(1)}, bf16[264,256]{1,0:T(8,128)(2,1)S(1)}, u32[]{:S(2)}, u32[]{:S(2)}) collective-permute-start(bf16[264,256]{1,0:T(8,128)(2,1)S(1)} %get-tuple-element.40), channel_id=1, source_target_pairs={{4,8},{8,4},{5,9},{9,5},{6,10},{10,6},{7,11},{11,7},{20,24},{24,20... | collective-permute-start | bytes 405512 | tf_op jit(solution)/shard_map/ppermute | solution.py:593
  53.3 11.1 %collective-permute-start.16 = (bf16[2,2,64,256]{3,2,1,0:T(8,128)(2,1)S(1)}, bf16[2,2,64,256]{3,2,1,0:T(8,128)(2,1)S(1)}, u32[]{:S(2)}, u32[]{:S(2)}) collective-permute-start(bf16[2,2,64,256]{3,2,1,0:T(8,128)(2,1)S(1)} %pad_maximum_fusion.mine), channel_id=1, source_target_pairs={{0,4},{4,0},{8,12},{12,8},{1,5},{5,1},{9,13},{13,9},{2,6},{6,2},{1... | collective-permute-start | bytes 393224 | tf_op jit(solution)/shard_map/ppermute | solution.py:568

commit v6 on v5

--- a/solution.py
+++ b/solution.py
@@ -262,9 +262,9 @@
     return sum(((lat >> b) & 1) << (bits - 1 - b) for b in range(bits))
 
 
-def half_gradient(n_lat, filt, cot, out, grad, slot):
+def half_gradient(n_lat, filt, cot, outs_of, grad, slot):
     kernels, half, _ = grad.shape
-    n_lon, share, piece = out.shape[1], out.shape[2], out.shape[3]
+    n_lon, share, piece = outs_of[0].shape[1:4]
     place, lon = band_place(n_lat), lax.axis_index("lon")
     group = n_lat // 2
     side = pl.multiple_of(((place // group) ^ slot) * half, half)
@@ -277,13 +277,15 @@
         )
     for m in range(group):
         start = pl.multiple_of(((place ^ m) % group) * piece, piece)
+        out, slot_of = outs_of[2 * m // group], m % (group // 2)
         for s in range(n_lon):
             first = (lon ^ s) * share
-            out[m, s] = grad[pl.ds(first, share), pl.ds(start, piece), :].astype(out.dtype)
+            value = grad[pl.ds(first, share), pl.ds(start, piece), :]
+            out[slot_of, s] = value.astype(out.dtype)
 
 
 def forward_kernel(n_lat, groups, bands, own, core, far, cot, *rest):
-    *sides, filt, send, ext, grad = rest
+    *sides, filt, send_low, send_high, ext, grad = rest
     _, cols, chans = own.shape
     fill_extended(ext, own, core, far, groups, sides)
 
@@ -291,11 +293,11 @@
         filt[start : start + BLOCK, k * chans : (k + 1) * chans] = value
 
     filter_rows(bands, ext, cols, write)
-    half_gradient(n_lat, filt, cot, send, grad, 1)
+    half_gradient(n_lat, filt, cot, (send_low, send_high), grad, 1)
 
 
 def part_shape(kernels, chans, outs, n_lat, n_lon):
-    return (n_lat // 2, n_lon, kernels // n_lon, chans // n_lat, outs)
+    return (n_lat // 4, n_lon, kernels // n_lon, chans // n_lat, outs)
 
 
 def forward(bands, own, core, far, cot, groups, sides, kernels, n_lat, n_lon):
@@ -307,6 +309,7 @@
         [bands, own, core, far, cot, *sides],
         [
             pltpu.VMEM((rows * cols, kernels * chans), jnp.bfloat16),
+            pltpu.VMEM(part_shape(kernels, chans, outs, n_lat, n_lon), jnp.bfloat16),
             pltpu.VMEM(part_shape(kernels, chans, outs, n_lat, n_lon), jnp.bfloat16),
         ],
         [
@@ -317,8 +320,8 @@
     )
 
 
-def kept_kernel(n_lat, filt, cot, keep, grad):
-    half_gradient(n_lat, filt, cot, keep, grad, 0)
+def kept_kernel(n_lat, filt, cot, keep_low, keep_high, grad):
+    half_gradient(n_lat, filt, cot, (keep_low, keep_high), grad, 0)
 
 
 def kept(filt, cot, kernels, n_lat, n_lon):
@@ -326,7 +329,7 @@
     return kernel_call(
         functools.partial(kept_kernel, n_lat),
         [filt, cot],
-        pltpu.VMEM(part_shape(kernels, chans, outs, n_lat, n_lon), jnp.float32),
+        [pltpu.VMEM(part_shape(kernels, chans, outs, n_lat, n_lon), jnp.float32)] * 2,
         [pltpu.VMEM((kernels, chans // 2, outs), jnp.float32)],
         12,
     )
@@ -547,7 +550,11 @@
 
 def reduced_gradient(keep, send):
     n_lat, n_lon = lax.axis_size("lat"), lax.axis_size("lon")
-    mask = 1
+    high = lax.ppermute(send[1], "lat", swap("lat", 1))
+    low = lax.ppermute(send[0], "lat", swap("lat", 1))
+    send = (keep[1] + high.astype(jnp.float32)).astype(jnp.bfloat16)
+    keep = keep[0] + low.astype(jnp.float32)
+    mask = 2
     while True:
         other = lax.ppermute(send, "lat", swap("lat", mask))
         total = keep + other.astype(jnp.float32)
@@ -608,7 +615,7 @@
     f_core, f_far = bands_beside(sent)
 
     flat_cot = cot_near.reshape(rows * cols, outs)
-    filtered, send = forward(
+    filtered, *send = forward(
         bands,
         field_near,
         f_core,

time: 65.4 us -> 64.9 us (level)
  waiting for transfers between devices: 24.3 us -> 23.4 us
    ppermute x2 -> x1, waiting for transfers between devices: 7.78 us -> 6.82 us  [reduced_gradient(): other = lax.ppermute(send, 'lat', swap('lat', mask))]
    ppermute x2 -> x1, starting transfers between devices: 1.66 us -> 1.59 us  [reduced_gradient(): other = lax.ppermute(send, 'lat', swap('lat', mask))]
  transfers between devices with their start and end apart: 17 -> 18, of which waited for: 8 -> 8; matrix products, arithmetic and copies ran while one was open for 0% -> 0% of each run, Pallas kernels for 19% -> 19%
where the time goes in v6:
time: 64.9 us; the launch traced here: 64.8 us
  waiting for transfers between devices  23.4 us (36%)
  starting transfers between devices  22.7 us (35%)
  Pallas kernels  17.6 us (27%)
  between operations  0.86 us (1%)
    pallas_call x14, Pallas kernels, kernel_call(): pl.pallas_call(body, in_specs=specs, out_specs=place if single else [plac...  17.6 us
    ppermute x3, waiting for transfers between devices, beside(): lax.ppermute(pair[1], 'lon', other + [(j, i) for i, j in other])  11.1 us
    ppermute x1, waiting for transfers between devices, reduced_gradient(): other = lax.ppermute(send, 'lat', swap('lat', mask))  6.82 us
    ppermute x3, starting transfers between devices, beside(): lax.ppermute(pair[1], 'lon', other + [(j, i) for i, j in other])  5.73 us
    ppermute x3, starting transfers between devices, beside(): lax.ppermute(pair[0], 'lon', swap('lon', 1))  5.28 us
    ppermute x2, starting transfers between devices, reduced_gradient(): other = lax.ppermute(pieces, 'lat', swap('lat', mask))  4.52 us
    ppermute x3, starting transfers between devices, reduced_gradient(): other = lax.ppermute(wire[s], 'lon', swap('lon', s))  3.55 us
    ppermute x3, waiting for transfers between devices, beside(): lax.ppermute(pair[0], 'lon', swap('lon', 1))  2.93 us
  transfers between devices with their start and end apart: 18, of which 8 were waited for; matrix products, arithmetic and copies ran while one was open for 0% of the time, Pallas kernels for 19%

profile of v6, /device:TPU:0, one launch (start us, length us, event | category | flops | bytes accessed | tf_op | source)
XLA Modules:
  0.0 64.8 jit_solution(14191424489853888816)
XLA Ops:
  0.6 1.3 %shard_map.78 = (bf16[2,64,256]{2,1,0:T(8,128)(2,1)S(1)}, bf16[2,64,256]{2,1,0:T(8,128)(2,1)S(1)}, bf16[6,64,256]{2,1,0:T(8,128)(2,1)S(1)}, bf16[6,64,256]{2,1,0:T(8,128)(2,1)S(1)}) custom-call(bf16[8,128,256]{2,1,0:T(8,128)(2,1)} %field.3), custom_call_target="tpu_custom_call" | custom-call | tf_op jit(solution)/shard_map/pallas_call | solution.py:37
  1.9 3.1 %collective-permute-start = (bf16[2,64,256]{2,1,0:T(8,128)(2,1)S(1)}, bf16[2,64,256]{2,1,0:T(8,128)(2,1)S(1)}, u32[]{:S(2)}, u32[]{:S(2)}) collective-permute-start(bf16[2,64,256]{2,1,0:T(8,128)(2,1)S(1)} %get-tuple-element.30), channel_id=1, source_target_pairs={{0,1},{1,0},{2,3},{3,2},{4,5},{5,4},{6,7},{7,6},{8,9},{9,8},{10,11... | collective-permute-start | bytes 196616 | tf_op jit(solution)/shard_map/ppermute | solution.py:594
  5.0 2.5 %collective-permute-start.1 = (bf16[2,64,256]{2,1,0:T(8,128)(2,1)S(1)}, bf16[2,64,256]{2,1,0:T(8,128)(2,1)S(1)}, u32[]{:S(2)}, u32[]{:S(2)}) collective-permute-start(bf16[2,64,256]{2,1,0:T(8,128)(2,1)S(1)} %get-tuple-element.31), channel_id=1, source_target_pairs={{1,2},{3,0},{2,1},{0,3},{5,6},{7,4},{6,5},{4,7},{9,10},{11,8},{10,... | collective-permute-start | bytes 196616 | tf_op jit(solution)/shard_map/ppermute | solution.py:595
  7.5 0.7 %collective-permute-start.4 = (bf16[6,64,256]{2,1,0:T(8,128)(2,1)S(1)}, bf16[6,64,256]{2,1,0:T(8,128)(2,1)S(1)}, u32[]{:S(2)}, u32[]{:S(2)}) collective-permute-start(bf16[6,64,256]{2,1,0:T(8,128)(2,1)S(1)} %get-tuple-element.35), channel_id=1, source_target_pairs={{0,1},{1,0},{2,3},{3,2},{4,5},{5,4},{6,7},{7,6},{8,9},{9,8},{10,11... | collective-permute-start | bytes 589832 | tf_op jit(solution)/shard_map/ppermute | solution.py:594
  8.2 0.9 %collective-permute-start.5 = (bf16[6,64,256]{2,1,0:T(8,128)(2,1)S(1)}, bf16[6,64,256]{2,1,0:T(8,128)(2,1)S(1)}, u32[]{:S(2)}, u32[]{:S(2)}) collective-permute-start(bf16[6,64,256]{2,1,0:T(8,128)(2,1)S(1)} %get-tuple-element.36), channel_id=1, source_target_pairs={{1,2},{3,0},{2,1},{0,3},{5,6},{7,4},{6,5},{4,7},{9,10},{11,8},{10,... | collective-permute-start | bytes 589832 | tf_op jit(solution)/shard_map/ppermute | solution.py:595
  9.1 1.5 %shard_map.76 = (bf16[8,64,256]{2,1,0:T(8,128)(2,1)S(1)}, bf16[8,64,256]{2,1,0:T(8,128)(2,1)S(1)}, bf16[8,128,256]{2,1,0:T(8,128)(2,1)S(1)}, bf16[8,128,256]{2,1...) custom-call(bf16[8,128,256]{2,1,0:T(8,128)(2,1)} %field.3, bf16[8,128,256]{2,1,0:T(8,128)(2,1)} %cot.1, ...), custom_call_target="tpu_custom_call" | custom-call | tf_op jit(solution)/shard_map/pallas_call | solution.py:37
  10.6 0.0 collective-permute-done.paired.rest_0_
  10.6 1.3 %collective-permute-done.1.other.rest_1_ = bf16[2,64,256]{2,1,0:T(8,128)(2,1)S(1)} collective-permute-done((bf16[2,64,256]{2,1,0:T(8,128)(2,1)S(1)}, bf16[2,64,256]{2,1,0:T(8,128)(2,1)S(1)}, u32[]{:S(2)}, u32[]{:S(2)}) %collective-permute-start.1) | collective-permute-done | bytes 65568 | tf_op jit(solution)/shard_map/ppermute | solution.py:595
  11.9 0.1 collective-permute-start.2
  11.9 0.7 %collective-permute-start.3 = (bf16[256,256]{1,0:T(8,128)(2,1)S(1)}, bf16[256,256]{1,0:T(8,128)(2,1)S(1)}, u32[]{:S(2)}, u32[]{:S(2)}) collective-permute-start(bf16[256,256]{1,0:T(8,128)(2,1)S(1)} %get-tuple-element.33), channel_id=1, source_target_pairs={{4,8},{8,4},{5,9},{9,5},{6,10},{10,6},{7,11},{11,7},{20,24},{24,20... | collective-permute-start | bytes 393224 | tf_op jit(solution)/shard_map/ppermute | solution.py:600
  12.6 1.6 %shard_map.77 = (bf16[8,256,512]{2,1,0:T(8,128)(2,1)S(1)}, bf16[2,8,256]{2,1,0:T(8,128)(2,1)S(1)}) custom-call(s32[8,128]{1,0:T(8,128)S(1)} %get-tuple-element.26.reach, f32[8,3,8,129]{3,2,1,0:T(8,128)S(1)} %get-tuple-element.27.quadrature), custom_call_target="tpu_custom_call" | custom-call | tf_op jit(solution)/shard_map/pallas_call | solution.py:37
  14.2 0.0 collective-permute-done.2.core
  14.2 0.0 collective-permute-done.3.far
  14.3 0.7 %collective-permute-done.4.rest_2_ = bf16[6,64,256]{2,1,0:T(8,128)(2,1)S(1)} collective-permute-done((bf16[6,64,256]{2,1,0:T(8,128)(2,1)S(1)}, bf16[6,64,256]{2,1,0:T(8,128)(2,1)S(1)}, u32[]{:S(2)}, u32[]{:S(2)}) %collective-permute-start.4) | collective-permute-done | bytes 196640 | tf_op jit(solution)/shard_map/ppermute | solution.py:594
  15.0 4.6 %collective-permute-done.5.rest_3_ = bf16[6,64,256]{2,1,0:T(8,128)(2,1)S(1)} collective-permute-done((bf16[6,64,256]{2,1,0:T(8,128)(2,1)S(1)}, bf16[6,64,256]{2,1,0:T(8,128)(2,1)S(1)}, u32[]{:S(2)}, u32[]{:S(2)}) %collective-permute-start.5) | collective-permute-done | bytes 196640 | tf_op jit(solution)/shard_map/ppermute | solution.py:595
  19.6 3.3 %shard_map.80 = (bf16[1024,2048]{1,0:T(8,128)(2,1)S(1)}, bf16[1,4,2,64,256]{4,3,2,1,0:T(8,128)(2,1)S(1)}, bf16[1,4,2,64,256]{4,3,2,1,0:T(8,128)(2,1)S(1)}) custom-call(bf16[8,256,512]{2,1,0:T(8,128)(2,1)S(1)} %get-tuple-element.28.bands, bf16[8,128,256]{2,1,0:T(8,128)(2,1)S(1)} %get-tuple-element.29.own, bf16[256,256]{1,0:T(8,128)(2,1)S(1)} %collective-permute-done.2.core, ...), custom_call_target="tpu_custom_call" | custom-call | tf_op jit(solution)/shard_map/pallas_call | solution.py:37
  22.9 0.1 collective-permute-start.11
  23.0 0.5 collective-permute-start.10
  23.5 0.9 %shard_map.88 = (f32[1,4,2,64,256]{4,3,2,1,0:T(8,128)S(1)}, f32[1,4,2,64,256]{4,3,2,1,0:T(8,128)S(1)}) custom-call(bf16[1024,2048]{1,0:T(8,128)(2,1)S(1)} %get-tuple-element.37.filt, bf16[1024,256]{1,0:T(8,128)(2,1)S(1)} %bitcast.25), custom_call_target="tpu_custom_call" | custom-call | tf_op jit(solution)/shard_map/pallas_call | solution.py:37
  24.4 0.0 copy-start
  24.4 0.1 collective-permute-done.11
  24.5 0.1 add_convert_fusion
  24.6 1.6 %collective-permute-start.12 = (bf16[1,4,2,64,256]{4,3,2,1,0:T(8,128)(2,1)S(1)}, bf16[1,4,2,64,256]{4,3,2,1,0:T(8,128)(2,1)S(1)}, u32[]{:S(2)}, u32[]{:S(2)}) collective-permute-start(bf16[1,4,2,64,256]{4,3,2,1,0:T(8,128)(2,1)S(1)} %add_convert_fusion), channel_id=1, source_target_pairs={{0,8},{4,12},{8,0},{12,4},{1,9},{5,13},{9,1},{13,5},{2,10},{6,14},... | collective-permute-start | bytes 786440 | tf_op jit(solution)/shard_map/ppermute | solution.py:559
  26.2 0.0 collective-permute-done.10
  26.2 6.8 %collective-permute-done.12 = bf16[1,4,2,64,256]{4,3,2,1,0:T(8,128)(2,1)S(1)} collective-permute-done((bf16[1,4,2,64,256]{4,3,2,1,0:T(8,128)(2,1)S(1)}, bf16[1,4,2,64,256]{4,3,2,1,0:T(8,128)(2,1)S(1)}, u32[]{:S(2)}, u32[]{:S(2)}) %collective-permute-start.12) | collective-permute-done | bytes 262176 | tf_op jit(solution)/shard_map/ppermute | solution.py:559
  33.0 0.1 fusion.5
  33.1 0.7 %collective-permute-start.13 = (bf16[2,64,256]{2,1,0:T(8,128)(2,1)S(1)}, bf16[2,64,256]{2,1,0:T(8,128)(2,1)S(1)}, u32[]{:S(2)}, u32[]{:S(2)}) collective-permute-start(bf16[2,64,256]{2,1,0:T(8,128)(2,1)S(1)} %get-tuple-element.51), channel_id=1, source_target_pairs={{0,1},{1,0},{2,3},{3,2},{4,5},{5,4},{6,7},{7,6},{8,9},{9,8},{10,11... | collective-permute-start | bytes 196616 | tf_op jit(solution)/shard_map/ppermute | solution.py:570
  33.8 2.4 %collective-permute-start.15 = (bf16[2,64,256]{2,1,0:T(8,128)(2,1)S(1)}, bf16[2,64,256]{2,1,0:T(8,128)(2,1)S(1)}, u32[]{:S(2)}, u32[]{:S(2)}) collective-permute-start(bf16[2,64,256]{2,1,0:T(8,128)(2,1)S(1)} %get-tuple-element.52), channel_id=1, source_target_pairs={{0,3},{1,2},{2,1},{3,0},{4,7},{5,6},{6,5},{7,4},{8,11},{9,10},{10,... | collective-permute-start | bytes 196616 | tf_op jit(solution)/shard_map/ppermute | solution.py:570
  36.1 0.5 collective-permute-start.14
  36.7 1.5 %collective-permute-start.6 = (bf16[8,64,256]{2,1,0:T(8,128)(2,1)S(1)}, bf16[8,64,256]{2,1,0:T(8,128)(2,1)S(1)}, u32[]{:S(2)}, u32[]{:S(2)}) collective-permute-start(bf16[8,64,256]{2,1,0:T(8,128)(2,1)S(1)} %get-tuple-element.38), channel_id=1, source_target_pairs={{0,1},{1,0},{2,3},{3,2},{4,5},{5,4},{6,7},{7,6},{8,9},{9,8},{10,11... | collective-permute-start | bytes 786440 | tf_op jit(solution)/shard_map/ppermute | solution.py:594
  38.2 2.4 %collective-permute-start.7 = (bf16[8,64,256]{2,1,0:T(8,128)(2,1)S(1)}, bf16[8,64,256]{2,1,0:T(8,128)(2,1)S(1)}, u32[]{:S(2)}, u32[]{:S(2)}) collective-permute-start(bf16[8,64,256]{2,1,0:T(8,128)(2,1)S(1)} %get-tuple-element.39), channel_id=1, source_target_pairs={{1,2},{3,0},{2,1},{0,3},{5,6},{7,4},{6,5},{4,7},{9,10},{11,8},{10,... | collective-permute-start | bytes 786440 | tf_op jit(solution)/shard_map/ppermute | solution.py:595
  40.5 2.5 %collective-permute-done.14 = bf16[2,64,256]{2,1,0:T(8,128)(2,1)S(1)} collective-permute-done((bf16[2,64,256]{2,1,0:T(8,128)(2,1)S(1)}, bf16[2,64,256]{2,1,0:T(8,128)(2,1)S(1)}, u32[]{:S(2)}, u32[]{:S(2)}) %collective-permute-start.14) | collective-permute-done | bytes 65568 | tf_op jit(solution)/shard_map/ppermute | solution.py:570
  43.0 1.6 %collective-permute-start.16 = (bf16[1,2,64,256]{3,2,1,0:T(8,128)(2,1)S(1)}, bf16[1,2,64,256]{3,2,1,0:T(8,128)(2,1)S(1)}, u32[]{:S(2)}, u32[]{:S(2)}) collective-permute-start(bf16[1,2,64,256]{3,2,1,0:T(8,128)(2,1)S(1)} %fusion.4), channel_id=1, source_target_pairs={{0,8},{4,12},{8,0},{12,4},{1,9},{5,13},{9,1},{13,5},{2,10},{6,14},... | collective-permute-start | bytes 196616 | tf_op jit(solution)/shard_map/ppermute | solution.py:575
  44.6 2.2 %collective-permute-done.6.paired = bf16[8,64,256]{2,1,0:T(8,128)(2,1)S(1)} collective-permute-done((bf16[8,64,256]{2,1,0:T(8,128)(2,1)S(1)}, bf16[8,64,256]{2,1,0:T(8,128)(2,1)S(1)}, u32[]{:S(2)}, u32[]{:S(2)}) %collective-permute-start.6) | collective-permute-done | bytes 262176 | tf_op jit(solution)/shard_map/ppermute | solution.py:594
  46.8 5.2 %collective-permute-done.7.other = bf16[8,64,256]{2,1,0:T(8,128)(2,1)S(1)} collective-permute-done((bf16[8,64,256]{2,1,0:T(8,128)(2,1)S(1)}, bf16[8,64,256]{2,1,0:T(8,128)(2,1)S(1)}, u32[]{:S(2)}, u32[]{:S(2)}) %collective-permute-start.7) | collective-permute-done | bytes 262176 | tf_op jit(solution)/shard_map/ppermute | solution.py:595
  52.0 0.1 collective-permute-start.8
  52.1 0.7 %collective-permute-start.9 = (bf16[264,256]{1,0:T(8,128)(2,1)S(1)}, bf16[264,256]{1,0:T(8,128)(2,1)S(1)}, u32[]{:S(2)}, u32[]{:S(2)}) collective-permute-start(bf16[264,256]{1,0:T(8,128)(2,1)S(1)} %get-tuple-element.43), channel_id=1, source_target_pairs={{4,8},{8,4},{5,9},{9,5},{6,10},{10,6},{7,11},{11,7},{20,24},{24,20... | collective-permute-start | bytes 405512 | tf_op jit(solution)/shard_map/ppermute | solution.py:600
  52.8 2.9 %collective-permute-start.17 = (bf16[2,2,64,256]{3,2,1,0:T(8,128)(2,1)S(1)}, bf16[2,2,64,256]{3,2,1,0:T(8,128)(2,1)S(1)}, u32[]{:S(2)}, u32[]{:S(2)}) collective-permute-start(bf16[2,2,64,256]{3,2,1,0:T(8,128)(2,1)S(1)} %pad_maximum_fusion.mine), channel_id=1, source_target_pairs={{0,4},{4,0},{8,12},{12,8},{1,5},{5,1},{9,13},{13,9},{2,6},{6,2},{1... | collective-permute-start | bytes 393224 | tf_op jit(solution)/shard_map/ppermute | solution.py:575
  55.8 2.0 %shard_map.81 = bf16[1024,256]{1,0:T(8,128)(2,1)} custom-call(bf16[1024,2048]{1,0:T(8,128)(2,1)S(1)} %get-tuple-element.37.filt, bf16[2048,256]{1,0:T(8,128)(2,1)S(1)} %bitcast.23), custom_call_target="tpu_custom_call" | custom-call | tf_op jit(solution)/shard_map/pallas_call | solution.py:37
  57.8 2.1 %shard_map.82 = (bf16[8,768,256]{2,1,0:T(8,128)(2,1)S(1)}, bf16[8,256,256]{2,1,0:T(8,128)(2,1)S(1)}) custom-call(bf16[8,256,512]{2,1,0:T(8,128)(2,1)S(1)} %get-tuple-element.28.bands, bf16[8,128,256]{2,1,0:T(8,128)(2,1)S(1)} %get-tuple-element.34.own, bf16[8,64,256]{2,1,0:T(8,128)(2,1)S(1)} %collective-permute-done.6.paired, ...), custom_call_target="tpu_custom_call" | custom-call | tf_op jit(solution)/shard_map/pallas_call | solution.py:37
  59.9 0.9 %shard_map.84.lower = bf16[3,128,256]{2,1,0:T(8,128)(2,1)S(1)} custom-call(bf16[8,256,256]{2,1,0:T(8,128)(2,1)S(1)} %copy-done, bf16[8,768,256]{2,1,0:T(8,128)(2,1)S(1)} %get-tuple-element.40.inner), custom_call_target="tpu_custom_call" | custom-call | tf_op jit(solution)/shard_map/pallas_call | solution.py:37
  60.8 0.9 %shard_map.83.upper = bf16[3,128,256]{2,1,0:T(8,128)(2,1)S(1)} custom-call(bf16[8,256,256]{2,1,0:T(8,128)(2,1)S(1)} %copy-done, bf16[8,768,256]{2,1,0:T(8,128)(2,1)S(1)} %get-tuple-element.40.inner), custom_call_target="tpu_custom_call" | custom-call | tf_op jit(solution)/shard_map/pallas_call | solution.py:37
  61.6 0.0 collective-permute-done.8.core
  61.6 0.0 collective-permute-done.9.far
  61.7 0.9 %shard_map.86.filt = bf16[8,256,256]{2,1,0:T(8,128)(2,1)S(1)} custom-call(bf16[8,256,512]{2,1,0:T(8,128)(2,1)S(1)} %get-tuple-element.28.bands, bf16[264,256]{1,0:T(8,128)(2,1)S(1)} %collective-permute-done.8.core, bf16[264,256]{1,0:T(8,128)(2,1)S(1)} %collective-permute-done.9.far, bf16[8,256,256]{2,1,0:T(8,128)(2,1)S(1)} %get-tuple-element.44.turned), custom_call_target="tpu_custom_call" | custom-call | tf_op jit(solution)/shard_map/pallas_call | solution.py:37
  62.5 1.4 %shard_map.87 = bf16[8,128,256]{2,1,0:T(8,128)(2,1)} custom-call(bf16[8,256,256]{2,1,0:T(8,128)(2,1)S(1)} %copy-done, bf16[3,128,256]{2,1,0:T(8,128)(2,1)S(1)} %shard_map.83.upper, bf16[3,128,256]{2,1,0:T(8,128)(2,1)S(1)} %shard_map.84.lower, bf16[8,256,256]{2,1,0:T(8,128)(2,1)S(1)} %shard_map.86.filt), custom_call_target="tpu_custom_call" | custom-call | tf_op jit(solution)/shard_map/pallas_call | solution.py:37
  63.9 0.0 collective-permute-done.17.other
  63.9 0.8 %shard_map.89 = f32[2,256,256]{2,1,0:T(8,128)} custom-call(bf16[2,2,64,256]{3,2,1,0:T(8,128)(2,1)S(1)} %pad_maximum_fusion.mine, bf16[2,2,64,256]{3,2,1,0:T(8,128)(2,1)S(1)} %collective-permute-done.17.other), custom_call_target="tpu_custom_call" | custom-call | tf_op jit(solution)/shard_map/pallas_call | solution.py:37
  (9 shorter events, 0.1 us)
Async XLA Ops:
  1.9 8.7 %collective-permute-start = (bf16[2,64,256]{2,1,0:T(8,128)(2,1)S(1)}, bf16[2,64,256]{2,1,0:T(8,128)(2,1)S(1)}, u32[]{:S(2)}, u32[]{:S(2)}) collective-permute-start(bf16[2,64,256]{2,1,0:T(8,128)(2,1)S(1)} %get-tuple-element.30), channel_id=1, source_target_pairs={{0,1},{1,0},{2,3},{3,2},{4,5},{5,4},{6,7},{7,6},{8,9},{9,8},{10,11... | collective-permute-start | bytes 196616 | tf_op jit(solution)/shard_map/ppermute | solution.py:594
  5.0 6.8 %collective-permute-start.1 = (bf16[2,64,256]{2,1,0:T(8,128)(2,1)S(1)}, bf16[2,64,256]{2,1,0:T(8,128)(2,1)S(1)}, u32[]{:S(2)}, u32[]{:S(2)}) collective-permute-start(bf16[2,64,256]{2,1,0:T(8,128)(2,1)S(1)} %get-tuple-element.31), channel_id=1, source_target_pairs={{1,2},{3,0},{2,1},{0,3},{5,6},{7,4},{6,5},{4,7},{9,10},{11,8},{10,... | collective-permute-start | bytes 196616 | tf_op jit(solution)/shard_map/ppermute | solution.py:595
  7.5 7.5 %collective-permute-start.4 = (bf16[6,64,256]{2,1,0:T(8,128)(2,1)S(1)}, bf16[6,64,256]{2,1,0:T(8,128)(2,1)S(1)}, u32[]{:S(2)}, u32[]{:S(2)}) collective-permute-start(bf16[6,64,256]{2,1,0:T(8,128)(2,1)S(1)} %get-tuple-element.35), channel_id=1, source_target_pairs={{0,1},{1,0},{2,3},{3,2},{4,5},{5,4},{6,7},{7,6},{8,9},{9,8},{10,11... | collective-permute-start | bytes 589832 | tf_op jit(solution)/shard_map/ppermute | solution.py:594
  8.2 11.4 %collective-permute-start.5 = (bf16[6,64,256]{2,1,0:T(8,128)(2,1)S(1)}, bf16[6,64,256]{2,1,0:T(8,128)(2,1)S(1)}, u32[]{:S(2)}, u32[]{:S(2)}) collective-permute-start(bf16[6,64,256]{2,1,0:T(8,128)(2,1)S(1)} %get-tuple-element.36), channel_id=1, source_target_pairs={{1,2},{3,0},{2,1},{0,3},{5,6},{7,4},{6,5},{4,7},{9,10},{11,8},{10,... | collective-permute-start | bytes 589832 | tf_op jit(solution)/shard_map/ppermute | solution.py:595
  11.9 2.4 %collective-permute-start.2 = (bf16[256,256]{1,0:T(8,128)(2,1)S(1)}, bf16[256,256]{1,0:T(8,128)(2,1)S(1)}, u32[]{:S(2)}, u32[]{:S(2)}) collective-permute-start(bf16[256,256]{1,0:T(8,128)(2,1)S(1)} %get-tuple-element.32), channel_id=1, source_target_pairs={{0,4},{4,0},{8,12},{12,8},{1,5},{5,1},{9,13},{13,9},{2,6},{6,2},{1... | collective-permute-start | bytes 393224 | tf_op jit(solution)/shard_map/ppermute | solution.py:601
  11.9 2.3 %collective-permute-start.3 = (bf16[256,256]{1,0:T(8,128)(2,1)S(1)}, bf16[256,256]{1,0:T(8,128)(2,1)S(1)}, u32[]{:S(2)}, u32[]{:S(2)}) collective-permute-start(bf16[256,256]{1,0:T(8,128)(2,1)S(1)} %get-tuple-element.33), channel_id=1, source_target_pairs={{4,8},{8,4},{5,9},{9,5},{6,10},{10,6},{7,11},{11,7},{20,24},{24,20... | collective-permute-start | bytes 393224 | tf_op jit(solution)/shard_map/ppermute | solution.py:600
  22.9 1.6 %collective-permute-start.11 = (bf16[1,4,2,64,256]{4,3,2,1,0:T(8,128)(2,1)S(1)}, bf16[1,4,2,64,256]{4,3,2,1,0:T(8,128)(2,1)S(1)}, u32[]{:S(2)}, u32[]{:S(2)}) collective-permute-start(bf16[1,4,2,64,256]{4,3,2,1,0:T(8,128)(2,1)S(1)} %get-tuple-element.48), channel_id=1, source_target_pairs={{0,4},{4,0},{8,12},{12,8},{1,5},{5,1},{9,13},{13,9},{2,6},{6,2},{1... | collective-permute-start | bytes 786440 | tf_op jit(solution)/shard_map/ppermute | solution.py:553
  23.0 3.2 %collective-permute-start.10 = (bf16[1,4,2,64,256]{4,3,2,1,0:T(8,128)(2,1)S(1)}, bf16[1,4,2,64,256]{4,3,2,1,0:T(8,128)(2,1)S(1)}, u32[]{:S(2)}, u32[]{:S(2)}) collective-permute-start(bf16[1,4,2,64,256]{4,3,2,1,0:T(8,128)(2,1)S(1)} %get-tuple-element.46), channel_id=1, source_target_pairs={{0,4},{4,0},{8,12},{12,8},{1,5},{5,1},{9,13},{13,9},{2,6},{6,2},{1... | collective-permute-start | bytes 786440 | tf_op jit(solution)/shard_map/ppermute | solution.py:554
  24.4 31.3 %copy-start = (bf16[8,256,256]{2,1,0:T(8,128)(2,1)S(1)}, bf16[8,256,256]{2,1,0:T(8,128)(2,1)}, u32[]{:S(2)}) copy-start(bf16[8,256,256]{2,1,0:T(8,128)(2,1)} %mixing.5) | copy-start | bytes 3145732
  24.6 8.4 %collective-permute-start.12 = (bf16[1,4,2,64,256]{4,3,2,1,0:T(8,128)(2,1)S(1)}, bf16[1,4,2,64,256]{4,3,2,1,0:T(8,128)(2,1)S(1)}, u32[]{:S(2)}, u32[]{:S(2)}) collective-permute-start(bf16[1,4,2,64,256]{4,3,2,1,0:T(8,128)(2,1)S(1)} %add_convert_fusion), channel_id=1, source_target_pairs={{0,8},{4,12},{8,0},{12,4},{1,9},{5,13},{9,1},{13,5},{2,10},{6,14},... | collective-permute-start | bytes 786440 | tf_op jit(solution)/shard_map/ppermute | solution.py:559
  33.1 7.4 %collective-permute-start.13 = (bf16[2,64,256]{2,1,0:T(8,128)(2,1)S(1)}, bf16[2,64,256]{2,1,0:T(8,128)(2,1)S(1)}, u32[]{:S(2)}, u32[]{:S(2)}) collective-permute-start(bf16[2,64,256]{2,1,0:T(8,128)(2,1)S(1)} %get-tuple-element.51), channel_id=1, source_target_pairs={{0,1},{1,0},{2,3},{3,2},{4,5},{5,4},{6,7},{7,6},{8,9},{9,8},{10,11... | collective-permute-start | bytes 196616 | tf_op jit(solution)/shard_map/ppermute | solution.py:570
  33.8 6.7 %collective-permute-start.15 = (bf16[2,64,256]{2,1,0:T(8,128)(2,1)S(1)}, bf16[2,64,256]{2,1,0:T(8,128)(2,1)S(1)}, u32[]{:S(2)}, u32[]{:S(2)}) collective-permute-start(bf16[2,64,256]{2,1,0:T(8,128)(2,1)S(1)} %get-tuple-element.52), channel_id=1, source_target_pairs={{0,3},{1,2},{2,1},{3,0},{4,7},{5,6},{6,5},{7,4},{8,11},{9,10},{10,... | collective-permute-start | bytes 196616 | tf_op jit(solution)/shard_map/ppermute | solution.py:570
  36.1 6.9 %collective-permute-start.14 = (bf16[2,64,256]{2,1,0:T(8,128)(2,1)S(1)}, bf16[2,64,256]{2,1,0:T(8,128)(2,1)S(1)}, u32[]{:S(2)}, u32[]{:S(2)}) collective-permute-start(bf16[2,64,256]{2,1,0:T(8,128)(2,1)S(1)} %get-tuple-element.53), channel_id=1, source_target_pairs={{0,2},{1,3},{2,0},{3,1},{4,6},{5,7},{6,4},{7,5},{8,10},{9,11},{10,... | collective-permute-start | bytes 196616 | tf_op jit(solution)/shard_map/ppermute | solution.py:570
  36.7 10.2 %collective-permute-start.6 = (bf16[8,64,256]{2,1,0:T(8,128)(2,1)S(1)}, bf16[8,64,256]{2,1,0:T(8,128)(2,1)S(1)}, u32[]{:S(2)}, u32[]{:S(2)}) collective-permute-start(bf16[8,64,256]{2,1,0:T(8,128)(2,1)S(1)} %get-tuple-element.38), channel_id=1, source_target_pairs={{0,1},{1,0},{2,3},{3,2},{4,5},{5,4},{6,7},{7,6},{8,9},{9,8},{10,11... | collective-permute-start | bytes 786440 | tf_op jit(solution)/shard_map/ppermute | solution.py:594
  38.2 13.8 %collective-permute-start.7 = (bf16[8,64,256]{2,1,0:T(8,128)(2,1)S(1)}, bf16[8,64,256]{2,1,0:T(8,128)(2,1)S(1)}, u32[]{:S(2)}, u32[]{:S(2)}) collective-permute-start(bf16[8,64,256]{2,1,0:T(8,128)(2,1)S(1)} %get-tuple-element.39), channel_id=1, source_target_pairs={{1,2},{3,0},{2,1},{0,3},{5,6},{7,4},{6,5},{4,7},{9,10},{11,8},{10,... | collective-permute-start | bytes 786440 | tf_op jit(solution)/shard_map/ppermute | solution.py:595
  43.0 9.8 %collective-permute-start.16 = (bf16[1,2,64,256]{3,2,1,0:T(8,128)(2,1)S(1)}, bf16[1,2,64,256]{3,2,1,0:T(8,128)(2,1)S(1)}, u32[]{:S(2)}, u32[]{:S(2)}) collective-permute-start(bf16[1,2,64,256]{3,2,1,0:T(8,128)(2,1)S(1)} %fusion.4), channel_id=1, source_target_pairs={{0,8},{4,12},{8,0},{12,4},{1,9},{5,13},{9,1},{13,5},{2,10},{6,14},... | collective-permute-start | bytes 196616 | tf_op jit(solution)/shard_map/ppermute | solution.py:575
  52.0 9.6 %collective-permute-start.8 = (bf16[264,256]{1,0:T(8,128)(2,1)S(1)}, bf16[264,256]{1,0:T(8,128)(2,1)S(1)}, u32[]{:S(2)}, u32[]{:S(2)}) collective-permute-start(bf16[264,256]{1,0:T(8,128)(2,1)S(1)} %get-tuple-element.42), channel_id=1, source_target_pairs={{0,4},{4,0},{8,12},{12,8},{1,5},{5,1},{9,13},{13,9},{2,6},{6,2},{1... | collective-permute-start | bytes 405512 | tf_op jit(solution)/shard_map/ppermute | solution.py:601
  52.1 9.5 %collective-permute-start.9 = (bf16[264,256]{1,0:T(8,128)(2,1)S(1)}, bf16[264,256]{1,0:T(8,128)(2,1)S(1)}, u32[]{:S(2)}, u32[]{:S(2)}) collective-permute-start(bf16[264,256]{1,0:T(8,128)(2,1)S(1)} %get-tuple-element.43), channel_id=1, source_target_pairs={{4,8},{8,4},{5,9},{9,5},{6,10},{10,6},{7,11},{11,7},{20,24},{24,20... | collective-permute-start | bytes 405512 | tf_op jit(solution)/shard_map/ppermute | solution.py:600
  52.8 11.1 %collective-permute-start.17 = (bf16[2,2,64,256]{3,2,1,0:T(8,128)(2,1)S(1)}, bf16[2,2,64,256]{3,2,1,0:T(8,128)(2,1)S(1)}, u32[]{:S(2)}, u32[]{:S(2)}) collective-permute-start(bf16[2,2,64,256]{3,2,1,0:T(8,128)(2,1)S(1)} %pad_maximum_fusion.mine), channel_id=1, source_target_pairs={{0,4},{4,0},{8,12},{12,8},{1,5},{5,1},{9,13},{13,9},{2,6},{6,2},{1... | collective-permute-start | bytes 393224 | tf_op jit(solution)/shard_map/ppermute | solution.py:575

commit v7 on v6

--- a/solution.py
+++ b/solution.py
@@ -493,36 +493,33 @@
     )
 
 
-def back_mix_kernel(mixing, upper, lower, filt, out, stage, sems):
+def back_mix_kernel(mixing, inner, filt, out, stage, sems):
     rows, cols, _ = out.shape
-    split = 1 + upper.shape[0]
     copies = [
-        pltpu.make_async_copy(upper, out.at[pl.ds(1, upper.shape[0])], sems.at[0]),
-        pltpu.make_async_copy(lower, out.at[pl.ds(split, lower.shape[0])], sems.at[1]),
-        pltpu.make_async_copy(stage.at[0], out.at[0], sems.at[2]),
-        pltpu.make_async_copy(stage.at[1], out.at[rows - 1], sems.at[3]),
+        pltpu.make_async_copy(inner, out.at[pl.ds(1, rows - 2)], sems.at[0]),
+        pltpu.make_async_copy(stage.at[0], out.at[0], sems.at[1]),
+        pltpu.make_async_copy(stage.at[1], out.at[rows - 1], sems.at[2]),
     ]
     copies[0].start()
-    copies[1].start()
 
     def store(i, value):
         stage[i] = value
 
     mixed_rows(filt, mixing, 0, 2, cols, store)
+    copies[1].start()
     copies[2].start()
-    copies[3].start()
     for copy in copies:
         copy.wait()
 
 
-def back_mix(mixing, upper, lower, filt, rows):
+def back_mix(mixing, inner, filt, rows):
     _, chans, _ = mixing.shape
     cols = filt.shape[1] // 2
     return kernel_call(
         back_mix_kernel,
-        [mixing, upper, lower, filt],
+        [mixing, inner, filt],
         jax.ShapeDtypeStruct((rows, cols, chans), jnp.bfloat16),
-        [pltpu.VMEM((2, cols, chans), jnp.bfloat16), pltpu.SemaphoreType.DMA((4,))],
+        [pltpu.VMEM((2, cols, chans), jnp.bfloat16), pltpu.SemaphoreType.DMA((3,))],
         8,
         far_out=True,
     )
@@ -548,26 +545,45 @@
     )
 
 
+def far_sum_kernel(skip, mine, other, out):
+    out[...] = (mine[skip:] + other[...].astype(jnp.float32)).astype(out.dtype)
+
+
+def far_sum(mine, other, skip):
+    outs = pltpu.VMEM(other.shape, jnp.bfloat16)
+    body = functools.partial(far_sum_kernel, skip)
+    return kernel_call(body, [mine, other], outs, [], 4)
+
+
 def reduced_gradient(keep, send):
     n_lat, n_lon = lax.axis_size("lat"), lax.axis_size("lon")
     high = lax.ppermute(send[1], "lat", swap("lat", 1))
     low = lax.ppermute(send[0], "lat", swap("lat", 1))
     send = (keep[1] + high.astype(jnp.float32)).astype(jnp.bfloat16)
     keep = keep[0] + low.astype(jnp.float32)
-    mask = 2
-    while True:
-        other = lax.ppermute(send, "lat", swap("lat", mask))
-        total = keep + other.astype(jnp.float32)
-        mask *= 2
-        if mask >= n_lat:
-            break
-        half = total.shape[0] // 2
-        keep, send = total[:half], total[half:].astype(jnp.bfloat16)
-    total = total[0]
-    wire = total.astype(jnp.bfloat16)
-    piece = total[0]
+    cut = n_lon // 2
+    totals = []
+    for part in (slice(cut, n_lon), slice(0, cut)):
+        mine, sent, mask = keep[:, part], send[:, part], 2
+        while True:
+            other = lax.ppermute(sent, "lat", swap("lat", mask))
+            mask *= 2
+            if mask >= n_lat and not totals:
+                source, skip = (keep, cut) if mask == 4 else (mine, 0)
+                wire = far_sum(source[0], other[0], skip)
+                totals.append(None)
+                break
+            total = mine + other.astype(jnp.float32)
+            if mask >= n_lat:
+                totals.append(total[0])
+                break
+            half = total.shape[0] // 2
+            mine, sent = total[:half], total[half:].astype(jnp.bfloat16)
+    near_part = totals[1]
+    piece = near_part[0]
+    wires = [near_part.astype(jnp.bfloat16), wire]
     for s in range(1, n_lon):
-        other = lax.ppermute(wire[s], "lon", swap("lon", s))
+        other = lax.ppermute(wires[s // cut][s % cut], "lon", swap("lon", s))
         piece = piece + other.astype(jnp.float32)
     pieces = piece.astype(jnp.bfloat16)[None]
     while mask > 1:
@@ -640,10 +656,8 @@
     g_core, g_far = bands_beside(sent)
     inner, turned = backward_inner(bands, cot_near, *g_sides, window)
     edge = backward_edges(bands, g_core, g_far, turned, cols, window)
-    half = (rows - 2) // 2
-    upper = inner_mix(mixing, inner, 0, half, cols)
-    lower = inner_mix(mixing, inner, half, rows - 2 - half, cols)
-    input_grad = back_mix(mixing, upper, lower, edge, rows)
+    inner = inner_mix(mixing, inner, 0, rows - 2, cols)
+    input_grad = back_mix(mixing, inner, edge, rows)
     return (
         field_out.reshape(rows, cols, outs),
         input_grad,

time: 64.9 us -> 63.6 us (0.980)
  starting transfers between devices: 22.7 us -> 21.9 us
    ppermute x3, waiting for transfers between devices: 2.93 us -> 4.17 us  [beside(): lax.ppermute(pair[0], 'lon', swap('lon', 1))]
    ppermute x3, starting transfers between devices: 5.28 us -> 4.34 us  [beside(): lax.ppermute(pair[0], 'lon', swap('lon', 1))]
    ppermute x4 -> x5, waiting for transfers between devices: 9.3 us -> 8.49 us  [the longest x2 5.55 us: reduced_gradient(): other = lax.ppermute(sent, 'lat', swap('lat', mask))]
    ppermute x4 -> x5, starting transfers between devices: 5.14 us -> 5.76 us  [the longest x3 3.66 us: reduced_gradient(): other = lax.ppermute(wires[s // cut][s % cut], 'lon', swap('lon', s))]
  transfers between devices with their start and end apart: 18 -> 19, of which waited for: 8 -> 10; matrix products, arithmetic and copies ran while one was open for 0% -> 0% of each run, Pallas kernels for 19% -> 19%
where the time goes in v7:
time: 63.6 us; the launch traced here: 63.4 us
  waiting for transfers between devices  23.3 us (37%)
  starting transfers between devices  21.9 us (34%)
  Pallas kernels  17.1 us (27%)
  between operations  0.86 us (1%)
    pallas_call x14, Pallas kernels, kernel_call(): pl.pallas_call(body, in_specs=specs, out_specs=place if single else [plac...  17.1 us
    ppermute x3, waiting for transfers between devices, beside(): lax.ppermute(pair[1], 'lon', other + [(j, i) for i, j in other])  10.5 us
    ppermute x2, waiting for transfers between devices, reduced_gradient(): other = lax.ppermute(sent, 'lat', swap('lat', mask))  5.55 us
    ppermute x3, starting transfers between devices, beside(): lax.ppermute(pair[1], 'lon', other + [(j, i) for i, j in other])  5.19 us
    ppermute x2, starting transfers between devices, reduced_gradient(): other = lax.ppermute(pieces, 'lat', swap('lat', mask))  4.52 us
    ppermute x3, starting transfers between devices, beside(): lax.ppermute(pair[0], 'lon', swap('lon', 1))  4.34 us
    ppermute x3, waiting for transfers between devices, beside(): lax.ppermute(pair[0], 'lon', swap('lon', 1))  4.17 us
    ppermute x3, starting transfers between devices, reduced_gradient(): other = lax.ppermute(wires[s // cut][s % cut], 'lon', swap('lon', s))  3.66 us
  transfers between devices with their start and end apart: 19, of which 10 were waited for; matrix products, arithmetic and copies ran while one was open for 0% of the time, Pallas kernels for 19%

profile of v7, /device:TPU:0, one launch (start us, length us, event | category | flops | bytes accessed | tf_op | source)
XLA Modules:
  0.0 63.4 jit_solution(2555027998259940044)
XLA Ops:
  0.6 1.3 %shard_map.78 = (bf16[2,64,256]{2,1,0:T(8,128)(2,1)S(1)}, bf16[2,64,256]{2,1,0:T(8,128)(2,1)S(1)}, bf16[6,64,256]{2,1,0:T(8,128)(2,1)S(1)}, bf16[6,64,256]{2,1,0:T(8,128)(2,1)S(1)}) custom-call(bf16[8,128,256]{2,1,0:T(8,128)(2,1)} %field.3), custom_call_target="tpu_custom_call" | custom-call | tf_op jit(solution)/shard_map/pallas_call | solution.py:37
  1.9 3.1 %collective-permute-start = (bf16[2,64,256]{2,1,0:T(8,128)(2,1)S(1)}, bf16[2,64,256]{2,1,0:T(8,128)(2,1)S(1)}, u32[]{:S(2)}, u32[]{:S(2)}) collective-permute-start(bf16[2,64,256]{2,1,0:T(8,128)(2,1)S(1)} %get-tuple-element.30), channel_id=1, source_target_pairs={{0,1},{1,0},{2,3},{3,2},{4,5},{5,4},{6,7},{7,6},{8,9},{9,8},{10,11... | collective-permute-start | bytes 196616 | tf_op jit(solution)/shard_map/ppermute | solution.py:610
  5.0 2.5 %collective-permute-start.1 = (bf16[2,64,256]{2,1,0:T(8,128)(2,1)S(1)}, bf16[2,64,256]{2,1,0:T(8,128)(2,1)S(1)}, u32[]{:S(2)}, u32[]{:S(2)}) collective-permute-start(bf16[2,64,256]{2,1,0:T(8,128)(2,1)S(1)} %get-tuple-element.31), channel_id=1, source_target_pairs={{1,2},{3,0},{2,1},{0,3},{5,6},{7,4},{6,5},{4,7},{9,10},{11,8},{10,... | collective-permute-start | bytes 196616 | tf_op jit(solution)/shard_map/ppermute | solution.py:611
  7.5 0.7 %collective-permute-start.4 = (bf16[6,64,256]{2,1,0:T(8,128)(2,1)S(1)}, bf16[6,64,256]{2,1,0:T(8,128)(2,1)S(1)}, u32[]{:S(2)}, u32[]{:S(2)}) collective-permute-start(bf16[6,64,256]{2,1,0:T(8,128)(2,1)S(1)} %get-tuple-element.35), channel_id=1, source_target_pairs={{0,1},{1,0},{2,3},{3,2},{4,5},{5,4},{6,7},{7,6},{8,9},{9,8},{10,11... | collective-permute-start | bytes 589832 | tf_op jit(solution)/shard_map/ppermute | solution.py:610
  8.2 0.9 %collective-permute-start.5 = (bf16[6,64,256]{2,1,0:T(8,128)(2,1)S(1)}, bf16[6,64,256]{2,1,0:T(8,128)(2,1)S(1)}, u32[]{:S(2)}, u32[]{:S(2)}) collective-permute-start(bf16[6,64,256]{2,1,0:T(8,128)(2,1)S(1)} %get-tuple-element.36), channel_id=1, source_target_pairs={{1,2},{3,0},{2,1},{0,3},{5,6},{7,4},{6,5},{4,7},{9,10},{11,8},{10,... | collective-permute-start | bytes 589832 | tf_op jit(solution)/shard_map/ppermute | solution.py:611
  9.1 1.5 %shard_map.76 = (bf16[8,64,256]{2,1,0:T(8,128)(2,1)S(1)}, bf16[8,64,256]{2,1,0:T(8,128)(2,1)S(1)}, bf16[8,128,256]{2,1,0:T(8,128)(2,1)S(1)}, bf16[8,128,256]{2,1...) custom-call(bf16[8,128,256]{2,1,0:T(8,128)(2,1)} %field.3, bf16[8,128,256]{2,1,0:T(8,128)(2,1)} %cot.1, ...), custom_call_target="tpu_custom_call" | custom-call | tf_op jit(solution)/shard_map/pallas_call | solution.py:37
  10.6 0.0 collective-permute-done.paired.rest_0_
  10.6 1.3 %collective-permute-done.1.other.rest_1_ = bf16[2,64,256]{2,1,0:T(8,128)(2,1)S(1)} collective-permute-done((bf16[2,64,256]{2,1,0:T(8,128)(2,1)S(1)}, bf16[2,64,256]{2,1,0:T(8,128)(2,1)S(1)}, u32[]{:S(2)}, u32[]{:S(2)}) %collective-permute-start.1) | collective-permute-done | bytes 65568 | tf_op jit(solution)/shard_map/ppermute | solution.py:611
  11.9 0.1 collective-permute-start.2
  11.9 0.7 %collective-permute-start.3 = (bf16[256,256]{1,0:T(8,128)(2,1)S(1)}, bf16[256,256]{1,0:T(8,128)(2,1)S(1)}, u32[]{:S(2)}, u32[]{:S(2)}) collective-permute-start(bf16[256,256]{1,0:T(8,128)(2,1)S(1)} %get-tuple-element.33), channel_id=1, source_target_pairs={{4,8},{8,4},{5,9},{9,5},{6,10},{10,6},{7,11},{11,7},{20,24},{24,20... | collective-permute-start | bytes 393224 | tf_op jit(solution)/shard_map/ppermute | solution.py:616
  12.6 1.6 %shard_map.77 = (bf16[8,256,512]{2,1,0:T(8,128)(2,1)S(1)}, bf16[2,8,256]{2,1,0:T(8,128)(2,1)S(1)}) custom-call(s32[8,128]{1,0:T(8,128)S(1)} %get-tuple-element.26.reach, f32[8,3,8,129]{3,2,1,0:T(8,128)S(1)} %get-tuple-element.27.quadrature), custom_call_target="tpu_custom_call" | custom-call | tf_op jit(solution)/shard_map/pallas_call | solution.py:37
  14.2 0.0 collective-permute-done.2.core
  14.2 0.0 collective-permute-done.3.far
  14.3 0.7 %collective-permute-done.4.rest_2_ = bf16[6,64,256]{2,1,0:T(8,128)(2,1)S(1)} collective-permute-done((bf16[6,64,256]{2,1,0:T(8,128)(2,1)S(1)}, bf16[6,64,256]{2,1,0:T(8,128)(2,1)S(1)}, u32[]{:S(2)}, u32[]{:S(2)}) %collective-permute-start.4) | collective-permute-done | bytes 196640 | tf_op jit(solution)/shard_map/ppermute | solution.py:610
  15.0 4.6 %collective-permute-done.5.rest_3_ = bf16[6,64,256]{2,1,0:T(8,128)(2,1)S(1)} collective-permute-done((bf16[6,64,256]{2,1,0:T(8,128)(2,1)S(1)}, bf16[6,64,256]{2,1,0:T(8,128)(2,1)S(1)}, u32[]{:S(2)}, u32[]{:S(2)}) %collective-permute-start.5) | collective-permute-done | bytes 196640 | tf_op jit(solution)/shard_map/ppermute | solution.py:611
  19.6 3.3 %shard_map.80 = (bf16[1024,2048]{1,0:T(8,128)(2,1)S(1)}, bf16[1,4,2,64,256]{4,3,2,1,0:T(8,128)(2,1)S(1)}, bf16[1,4,2,64,256]{4,3,2,1,0:T(8,128)(2,1)S(1)}) custom-call(bf16[8,256,512]{2,1,0:T(8,128)(2,1)S(1)} %get-tuple-element.28.bands, bf16[8,128,256]{2,1,0:T(8,128)(2,1)S(1)} %get-tuple-element.29.own, bf16[256,256]{1,0:T(8,128)(2,1)S(1)} %collective-permute-done.2.core, ...), custom_call_target="tpu_custom_call" | custom-call | tf_op jit(solution)/shard_map/pallas_call | solution.py:37
  22.9 0.1 collective-permute-start.11
  23.0 0.5 collective-permute-start.10
  23.5 0.9 %shard_map.87 = (f32[1,4,2,64,256]{4,3,2,1,0:T(8,128)S(1)}, f32[1,4,2,64,256]{4,3,2,1,0:T(8,128)S(1)}) custom-call(bf16[1024,2048]{1,0:T(8,128)(2,1)S(1)} %get-tuple-element.37.filt, bf16[1024,256]{1,0:T(8,128)(2,1)S(1)} %bitcast.27), custom_call_target="tpu_custom_call" | custom-call | tf_op jit(solution)/shard_map/pallas_call | solution.py:37
  24.4 0.1 collective-permute-done.11
  24.5 0.1 add_convert_fusion
  24.6 1.6 %collective-permute-start.12 = (bf16[1,2,2,64,256]{4,3,2,1,0:T(8,128)(2,1)S(1)}, bf16[1,2,2,64,256]{4,3,2,1,0:T(8,128)(2,1)S(1)}, u32[]{:S(2)}, u32[]{:S(2)}) collective-permute-start(bf16[1,2,2,64,256]{4,3,2,1,0:T(8,128)(2,1)S(1)} %get-tuple-element.49), channel_id=1, source_target_pairs={{0,8},{4,12},{8,0},{12,4},{1,9},{5,13},{9,1},{13,5},{2,10},{6,14},... | collective-permute-start | bytes 393224 | tf_op jit(solution)/shard_map/ppermute | solution.py:569
  26.2 0.5 collective-permute-start.14
  26.7 0.1 convert_add_fusion
  26.8 4.3 %collective-permute-done.12 = bf16[1,2,2,64,256]{4,3,2,1,0:T(8,128)(2,1)S(1)} collective-permute-done((bf16[1,2,2,64,256]{4,3,2,1,0:T(8,128)(2,1)S(1)}, bf16[1,2,2,64,256]{4,3,2,1,0:T(8,128)(2,1)S(1)}, u32[]{:S(2)}, u32[]{:S(2)}) %collective-permute-start.12) | collective-permute-done | bytes 131104 | tf_op jit(solution)/shard_map/ppermute | solution.py:569
  31.1 0.7 %collective-permute-start.13 = (bf16[2,64,256]{2,1,0:T(8,128)(2,1)S(1)}, bf16[2,64,256]{2,1,0:T(8,128)(2,1)S(1)}, u32[]{:S(2)}, u32[]{:S(2)}) collective-permute-start(bf16[2,64,256]{2,1,0:T(8,128)(2,1)S(1)} %fusion.5), channel_id=1, source_target_pairs={{0,1},{1,0},{2,3},{3,2},{4,5},{5,4},{6,7},{7,6},{8,9},{9,8},{10,11... | collective-permute-start | bytes 196616 | tf_op jit(solution)/shard_map/ppermute | solution.py:586
  31.7 1.3 %collective-permute-done.14 = bf16[1,2,2,64,256]{4,3,2,1,0:T(8,128)(2,1)S(1)} collective-permute-done((bf16[1,2,2,64,256]{4,3,2,1,0:T(8,128)(2,1)S(1)}, bf16[1,2,2,64,256]{4,3,2,1,0:T(8,128)(2,1)S(1)}, u32[]{:S(2)}, u32[]{:S(2)}) %collective-permute-start.14) | collective-permute-done | bytes 131104 | tf_op jit(solution)/shard_map/ppermute | solution.py:569
  33.1 1.5 %collective-permute-start.15 = (bf16[2,64,256]{2,1,0:T(8,128)(2,1)S(1)}, bf16[2,64,256]{2,1,0:T(8,128)(2,1)S(1)}, u32[]{:S(2)}, u32[]{:S(2)}) collective-permute-start(bf16[2,64,256]{2,1,0:T(8,128)(2,1)S(1)} %get-tuple-element.51), channel_id=1, source_target_pairs={{0,2},{1,3},{2,0},{3,1},{4,6},{5,7},{6,4},{7,5},{8,10},{9,11},{10,... | collective-permute-start | bytes 196616 | tf_op jit(solution)/shard_map/ppermute | solution.py:586
  34.6 1.5 %collective-permute-start.16 = (bf16[2,64,256]{2,1,0:T(8,128)(2,1)S(1)}, bf16[2,64,256]{2,1,0:T(8,128)(2,1)S(1)}, u32[]{:S(2)}, u32[]{:S(2)}) collective-permute-start(bf16[2,64,256]{2,1,0:T(8,128)(2,1)S(1)} %get-tuple-element.52), channel_id=1, source_target_pairs={{0,3},{1,2},{2,1},{3,0},{4,7},{5,6},{6,5},{7,4},{8,11},{9,10},{10,... | collective-permute-start | bytes 196616 | tf_op jit(solution)/shard_map/ppermute | solution.py:586
  36.1 0.5 collective-permute-start.6
  36.6 1.8 %collective-permute-start.7 = (bf16[8,64,256]{2,1,0:T(8,128)(2,1)S(1)}, bf16[8,64,256]{2,1,0:T(8,128)(2,1)S(1)}, u32[]{:S(2)}, u32[]{:S(2)}) collective-permute-start(bf16[8,64,256]{2,1,0:T(8,128)(2,1)S(1)} %get-tuple-element.39), channel_id=1, source_target_pairs={{1,2},{3,0},{2,1},{0,3},{5,6},{7,4},{6,5},{4,7},{9,10},{11,8},{10,... | collective-permute-start | bytes 786440 | tf_op jit(solution)/shard_map/ppermute | solution.py:611
  38.4 0.0 collective-permute-done.13
  38.4 2.4 %collective-permute-done.15 = bf16[2,64,256]{2,1,0:T(8,128)(2,1)S(1)} collective-permute-done((bf16[2,64,256]{2,1,0:T(8,128)(2,1)S(1)}, bf16[2,64,256]{2,1,0:T(8,128)(2,1)S(1)}, u32[]{:S(2)}, u32[]{:S(2)}) %collective-permute-start.15) | collective-permute-done | bytes 65568 | tf_op jit(solution)/shard_map/ppermute | solution.py:586
  40.8 0.5 collective-permute-done.16
  41.4 1.6 %collective-permute-start.17 = (bf16[1,2,64,256]{3,2,1,0:T(8,128)(2,1)S(1)}, bf16[1,2,64,256]{3,2,1,0:T(8,128)(2,1)S(1)}, u32[]{:S(2)}, u32[]{:S(2)}) collective-permute-start(bf16[1,2,64,256]{3,2,1,0:T(8,128)(2,1)S(1)} %fusion.4), channel_id=1, source_target_pairs={{0,8},{4,12},{8,0},{12,4},{1,9},{5,13},{9,1},{13,5},{2,10},{6,14},... | collective-permute-start | bytes 196616 | tf_op jit(solution)/shard_map/ppermute | solution.py:591
  43.0 3.5 %collective-permute-done.6.paired = bf16[8,64,256]{2,1,0:T(8,128)(2,1)S(1)} collective-permute-done((bf16[8,64,256]{2,1,0:T(8,128)(2,1)S(1)}, bf16[8,64,256]{2,1,0:T(8,128)(2,1)S(1)}, u32[]{:S(2)}, u32[]{:S(2)}) %collective-permute-start.6) | collective-permute-done | bytes 262176 | tf_op jit(solution)/shard_map/ppermute | solution.py:610
  46.5 4.6 %collective-permute-done.7.other = bf16[8,64,256]{2,1,0:T(8,128)(2,1)S(1)} collective-permute-done((bf16[8,64,256]{2,1,0:T(8,128)(2,1)S(1)}, bf16[8,64,256]{2,1,0:T(8,128)(2,1)S(1)}, u32[]{:S(2)}, u32[]{:S(2)}) %collective-permute-start.7) | collective-permute-done | bytes 262176 | tf_op jit(solution)/shard_map/ppermute | solution.py:611
  51.1 0.1 collective-permute-start.8
  51.2 0.7 %collective-permute-start.9 = (bf16[264,256]{1,0:T(8,128)(2,1)S(1)}, bf16[264,256]{1,0:T(8,128)(2,1)S(1)}, u32[]{:S(2)}, u32[]{:S(2)}) collective-permute-start(bf16[264,256]{1,0:T(8,128)(2,1)S(1)} %get-tuple-element.43), channel_id=1, source_target_pairs={{4,8},{8,4},{5,9},{9,5},{6,10},{10,6},{7,11},{11,7},{20,24},{24,20... | collective-permute-start | bytes 405512 | tf_op jit(solution)/shard_map/ppermute | solution.py:616
  51.9 0.0 collective-permute-done.17
  51.9 2.9 %collective-permute-start.18 = (bf16[2,2,64,256]{3,2,1,0:T(8,128)(2,1)S(1)}, bf16[2,2,64,256]{3,2,1,0:T(8,128)(2,1)S(1)}, u32[]{:S(2)}, u32[]{:S(2)}) collective-permute-start(bf16[2,2,64,256]{3,2,1,0:T(8,128)(2,1)S(1)} %pad_maximum_fusion.mine), channel_id=1, source_target_pairs={{0,4},{4,0},{8,12},{12,8},{1,5},{5,1},{9,13},{13,9},{2,6},{6,2},{1... | collective-permute-start | bytes 393224 | tf_op jit(solution)/shard_map/ppermute | solution.py:591
  54.9 2.0 %shard_map.81 = bf16[1024,256]{1,0:T(8,128)(2,1)} custom-call(bf16[1024,2048]{1,0:T(8,128)(2,1)S(1)} %get-tuple-element.37.filt, bf16[2048,256]{1,0:T(8,128)(2,1)S(1)} %bitcast.25), custom_call_target="tpu_custom_call" | custom-call | tf_op jit(solution)/shard_map/pallas_call | solution.py:37
  56.9 2.1 %shard_map.82 = (bf16[8,768,256]{2,1,0:T(8,128)(2,1)S(1)}, bf16[8,256,256]{2,1,0:T(8,128)(2,1)S(1)}) custom-call(bf16[8,256,512]{2,1,0:T(8,128)(2,1)S(1)} %get-tuple-element.28.bands, bf16[8,128,256]{2,1,0:T(8,128)(2,1)S(1)} %get-tuple-element.34.own, bf16[8,64,256]{2,1,0:T(8,128)(2,1)S(1)} %collective-permute-done.6.paired, ...), custom_call_target="tpu_custom_call" | custom-call | tf_op jit(solution)/shard_map/pallas_call | solution.py:37
  59.0 1.3 %shard_map.83.inner = bf16[6,128,256]{2,1,0:T(8,128)(2,1)S(1)} custom-call(bf16[8,256,256]{2,1,0:T(8,128)(2,1)S(1)} %copy-done, bf16[8,768,256]{2,1,0:T(8,128)(2,1)S(1)} %get-tuple-element.40.inner), custom_call_target="tpu_custom_call" | custom-call | tf_op jit(solution)/shard_map/pallas_call | solution.py:37
  60.3 0.9 %shard_map.85.filt = bf16[8,256,256]{2,1,0:T(8,128)(2,1)S(1)} custom-call(bf16[8,256,512]{2,1,0:T(8,128)(2,1)S(1)} %get-tuple-element.28.bands, bf16[264,256]{1,0:T(8,128)(2,1)S(1)} %collective-permute-done.8.core, bf16[264,256]{1,0:T(8,128)(2,1)S(1)} %collective-permute-done.9.far, bf16[8,256,256]{2,1,0:T(8,128)(2,1)S(1)} %get-tuple-element.44.turned), custom_call_target="tpu_custom_call" | custom-call | tf_op jit(solution)/shard_map/pallas_call | solution.py:37
  61.2 1.4 %shard_map.86 = bf16[8,128,256]{2,1,0:T(8,128)(2,1)} custom-call(bf16[8,256,256]{2,1,0:T(8,128)(2,1)S(1)} %copy-done, bf16[6,128,256]{2,1,0:T(8,128)(2,1)S(1)} %shard_map.83.inner, bf16[8,256,256]{2,1,0:T(8,128)(2,1)S(1)} %shard_map.85.filt), custom_call_target="tpu_custom_call" | custom-call | tf_op jit(solution)/shard_map/pallas_call | solution.py:37
  62.5 0.0 collective-permute-done.18.other
  62.6 0.8 %shard_map.89 = f32[2,256,256]{2,1,0:T(8,128)} custom-call(bf16[2,2,64,256]{3,2,1,0:T(8,128)(2,1)S(1)} %pad_maximum_fusion.mine, bf16[2,2,64,256]{3,2,1,0:T(8,128)(2,1)S(1)} %collective-permute-done.18.other), custom_call_target="tpu_custom_call" | custom-call | tf_op jit(solution)/shard_map/pallas_call | solution.py:37
  (14 shorter events, 0.2 us)
Async XLA Ops:
  1.9 8.7 %collective-permute-start = (bf16[2,64,256]{2,1,0:T(8,128)(2,1)S(1)}, bf16[2,64,256]{2,1,0:T(8,128)(2,1)S(1)}, u32[]{:S(2)}, u32[]{:S(2)}) collective-permute-start(bf16[2,64,256]{2,1,0:T(8,128)(2,1)S(1)} %get-tuple-element.30), channel_id=1, source_target_pairs={{0,1},{1,0},{2,3},{3,2},{4,5},{5,4},{6,7},{7,6},{8,9},{9,8},{10,11... | collective-permute-start | bytes 196616 | tf_op jit(solution)/shard_map/ppermute | solution.py:610
  5.0 6.8 %collective-permute-start.1 = (bf16[2,64,256]{2,1,0:T(8,128)(2,1)S(1)}, bf16[2,64,256]{2,1,0:T(8,128)(2,1)S(1)}, u32[]{:S(2)}, u32[]{:S(2)}) collective-permute-start(bf16[2,64,256]{2,1,0:T(8,128)(2,1)S(1)} %get-tuple-element.31), channel_id=1, source_target_pairs={{1,2},{3,0},{2,1},{0,3},{5,6},{7,4},{6,5},{4,7},{9,10},{11,8},{10,... | collective-permute-start | bytes 196616 | tf_op jit(solution)/shard_map/ppermute | solution.py:611
  7.5 7.5 %collective-permute-start.4 = (bf16[6,64,256]{2,1,0:T(8,128)(2,1)S(1)}, bf16[6,64,256]{2,1,0:T(8,128)(2,1)S(1)}, u32[]{:S(2)}, u32[]{:S(2)}) collective-permute-start(bf16[6,64,256]{2,1,0:T(8,128)(2,1)S(1)} %get-tuple-element.35), channel_id=1, source_target_pairs={{0,1},{1,0},{2,3},{3,2},{4,5},{5,4},{6,7},{7,6},{8,9},{9,8},{10,11... | collective-permute-start | bytes 589832 | tf_op jit(solution)/shard_map/ppermute | solution.py:610
  8.2 11.4 %collective-permute-start.5 = (bf16[6,64,256]{2,1,0:T(8,128)(2,1)S(1)}, bf16[6,64,256]{2,1,0:T(8,128)(2,1)S(1)}, u32[]{:S(2)}, u32[]{:S(2)}) collective-permute-start(bf16[6,64,256]{2,1,0:T(8,128)(2,1)S(1)} %get-tuple-element.36), channel_id=1, source_target_pairs={{1,2},{3,0},{2,1},{0,3},{5,6},{7,4},{6,5},{4,7},{9,10},{11,8},{10,... | collective-permute-start | bytes 589832 | tf_op jit(solution)/shard_map/ppermute | solution.py:611
  11.9 2.4 %collective-permute-start.2 = (bf16[256,256]{1,0:T(8,128)(2,1)S(1)}, bf16[256,256]{1,0:T(8,128)(2,1)S(1)}, u32[]{:S(2)}, u32[]{:S(2)}) collective-permute-start(bf16[256,256]{1,0:T(8,128)(2,1)S(1)} %get-tuple-element.32), channel_id=1, source_target_pairs={{0,4},{4,0},{8,12},{12,8},{1,5},{5,1},{9,13},{13,9},{2,6},{6,2},{1... | collective-permute-start | bytes 393224 | tf_op jit(solution)/shard_map/ppermute | solution.py:617
  11.9 2.3 %collective-permute-start.3 = (bf16[256,256]{1,0:T(8,128)(2,1)S(1)}, bf16[256,256]{1,0:T(8,128)(2,1)S(1)}, u32[]{:S(2)}, u32[]{:S(2)}) collective-permute-start(bf16[256,256]{1,0:T(8,128)(2,1)S(1)} %get-tuple-element.33), channel_id=1, source_target_pairs={{4,8},{8,4},{5,9},{9,5},{6,10},{10,6},{7,11},{11,7},{20,24},{24,20... | collective-permute-start | bytes 393224 | tf_op jit(solution)/shard_map/ppermute | solution.py:616
  22.9 1.6 %collective-permute-start.11 = (bf16[1,4,2,64,256]{4,3,2,1,0:T(8,128)(2,1)S(1)}, bf16[1,4,2,64,256]{4,3,2,1,0:T(8,128)(2,1)S(1)}, u32[]{:S(2)}, u32[]{:S(2)}) collective-permute-start(bf16[1,4,2,64,256]{4,3,2,1,0:T(8,128)(2,1)S(1)} %get-tuple-element.48), channel_id=1, source_target_pairs={{0,4},{4,0},{8,12},{12,8},{1,5},{5,1},{9,13},{13,9},{2,6},{6,2},{1... | collective-permute-start | bytes 786440 | tf_op jit(solution)/shard_map/ppermute | solution.py:560
  23.0 3.7 %collective-permute-start.10 = (bf16[1,4,2,64,256]{4,3,2,1,0:T(8,128)(2,1)S(1)}, bf16[1,4,2,64,256]{4,3,2,1,0:T(8,128)(2,1)S(1)}, u32[]{:S(2)}, u32[]{:S(2)}) collective-permute-start(bf16[1,4,2,64,256]{4,3,2,1,0:T(8,128)(2,1)S(1)} %get-tuple-element.46), channel_id=1, source_target_pairs={{0,4},{4,0},{8,12},{12,8},{1,5},{5,1},{9,13},{13,9},{2,6},{6,2},{1... | collective-permute-start | bytes 786440 | tf_op jit(solution)/shard_map/ppermute | solution.py:561
  24.5 30.3 %copy-start = (bf16[8,256,256]{2,1,0:T(8,128)(2,1)S(1)}, bf16[8,256,256]{2,1,0:T(8,128)(2,1)}, u32[]{:S(2)}) copy-start(bf16[8,256,256]{2,1,0:T(8,128)(2,1)} %mixing.3) | copy-start | bytes 3145732
  24.6 6.4 %collective-permute-start.12 = (bf16[1,2,2,64,256]{4,3,2,1,0:T(8,128)(2,1)S(1)}, bf16[1,2,2,64,256]{4,3,2,1,0:T(8,128)(2,1)S(1)}, u32[]{:S(2)}, u32[]{:S(2)}) collective-permute-start(bf16[1,2,2,64,256]{4,3,2,1,0:T(8,128)(2,1)S(1)} %get-tuple-element.49), channel_id=1, source_target_pairs={{0,8},{4,12},{8,0},{12,4},{1,9},{5,13},{9,1},{13,5},{2,10},{6,14},... | collective-permute-start | bytes 393224 | tf_op jit(solution)/shard_map/ppermute | solution.py:569
  26.2 6.8 %collective-permute-start.14 = (bf16[1,2,2,64,256]{4,3,2,1,0:T(8,128)(2,1)S(1)}, bf16[1,2,2,64,256]{4,3,2,1,0:T(8,128)(2,1)S(1)}, u32[]{:S(2)}, u32[]{:S(2)}) collective-permute-start(bf16[1,2,2,64,256]{4,3,2,1,0:T(8,128)(2,1)S(1)} %get-tuple-element.50), channel_id=1, source_target_pairs={{0,8},{4,12},{8,0},{12,4},{1,9},{5,13},{9,1},{13,5},{2,10},{6,14},... | collective-permute-start | bytes 393224 | tf_op jit(solution)/shard_map/ppermute | solution.py:569
  31.1 7.4 %collective-permute-start.13 = (bf16[2,64,256]{2,1,0:T(8,128)(2,1)S(1)}, bf16[2,64,256]{2,1,0:T(8,128)(2,1)S(1)}, u32[]{:S(2)}, u32[]{:S(2)}) collective-permute-start(bf16[2,64,256]{2,1,0:T(8,128)(2,1)S(1)} %fusion.5), channel_id=1, source_target_pairs={{0,1},{1,0},{2,3},{3,2},{4,5},{5,4},{6,7},{7,6},{8,9},{9,8},{10,11... | collective-permute-start | bytes 196616 | tf_op jit(solution)/shard_map/ppermute | solution.py:586
  33.1 7.8 %collective-permute-start.15 = (bf16[2,64,256]{2,1,0:T(8,128)(2,1)S(1)}, bf16[2,64,256]{2,1,0:T(8,128)(2,1)S(1)}, u32[]{:S(2)}, u32[]{:S(2)}) collective-permute-start(bf16[2,64,256]{2,1,0:T(8,128)(2,1)S(1)} %get-tuple-element.51), channel_id=1, source_target_pairs={{0,2},{1,3},{2,0},{3,1},{4,6},{5,7},{6,4},{7,5},{8,10},{9,11},{10,... | collective-permute-start | bytes 196616 | tf_op jit(solution)/shard_map/ppermute | solution.py:586
  34.6 6.8 %collective-permute-start.16 = (bf16[2,64,256]{2,1,0:T(8,128)(2,1)S(1)}, bf16[2,64,256]{2,1,0:T(8,128)(2,1)S(1)}, u32[]{:S(2)}, u32[]{:S(2)}) collective-permute-start(bf16[2,64,256]{2,1,0:T(8,128)(2,1)S(1)} %get-tuple-element.52), channel_id=1, source_target_pairs={{0,3},{1,2},{2,1},{3,0},{4,7},{5,6},{6,5},{7,4},{8,11},{9,10},{10,... | collective-permute-start | bytes 196616 | tf_op jit(solution)/shard_map/ppermute | solution.py:586
  36.1 10.4 %collective-permute-start.6 = (bf16[8,64,256]{2,1,0:T(8,128)(2,1)S(1)}, bf16[8,64,256]{2,1,0:T(8,128)(2,1)S(1)}, u32[]{:S(2)}, u32[]{:S(2)}) collective-permute-start(bf16[8,64,256]{2,1,0:T(8,128)(2,1)S(1)} %get-tuple-element.38), channel_id=1, source_target_pairs={{0,1},{1,0},{2,3},{3,2},{4,5},{5,4},{6,7},{7,6},{8,9},{9,8},{10,11... | collective-permute-start | bytes 786440 | tf_op jit(solution)/shard_map/ppermute | solution.py:610
  36.6 14.5 %collective-permute-start.7 = (bf16[8,64,256]{2,1,0:T(8,128)(2,1)S(1)}, bf16[8,64,256]{2,1,0:T(8,128)(2,1)S(1)}, u32[]{:S(2)}, u32[]{:S(2)}) collective-permute-start(bf16[8,64,256]{2,1,0:T(8,128)(2,1)S(1)} %get-tuple-element.39), channel_id=1, source_target_pairs={{1,2},{3,0},{2,1},{0,3},{5,6},{7,4},{6,5},{4,7},{9,10},{11,8},{10,... | collective-permute-start | bytes 786440 | tf_op jit(solution)/shard_map/ppermute | solution.py:611
  41.4 10.5 %collective-permute-start.17 = (bf16[1,2,64,256]{3,2,1,0:T(8,128)(2,1)S(1)}, bf16[1,2,64,256]{3,2,1,0:T(8,128)(2,1)S(1)}, u32[]{:S(2)}, u32[]{:S(2)}) collective-permute-start(bf16[1,2,64,256]{3,2,1,0:T(8,128)(2,1)S(1)} %fusion.4), channel_id=1, source_target_pairs={{0,8},{4,12},{8,0},{12,4},{1,9},{5,13},{9,1},{13,5},{2,10},{6,14},... | collective-permute-start | bytes 196616 | tf_op jit(solution)/shard_map/ppermute | solution.py:591
  51.1 9.2 %collective-permute-start.8 = (bf16[264,256]{1,0:T(8,128)(2,1)S(1)}, bf16[264,256]{1,0:T(8,128)(2,1)S(1)}, u32[]{:S(2)}, u32[]{:S(2)}) collective-permute-start(bf16[264,256]{1,0:T(8,128)(2,1)S(1)} %get-tuple-element.42), channel_id=1, source_target_pairs={{0,4},{4,0},{8,12},{12,8},{1,5},{5,1},{9,13},{13,9},{2,6},{6,2},{1... | collective-permute-start | bytes 405512 | tf_op jit(solution)/shard_map/ppermute | solution.py:617
  51.2 9.1 %collective-permute-start.9 = (bf16[264,256]{1,0:T(8,128)(2,1)S(1)}, bf16[264,256]{1,0:T(8,128)(2,1)S(1)}, u32[]{:S(2)}, u32[]{:S(2)}) collective-permute-start(bf16[264,256]{1,0:T(8,128)(2,1)S(1)} %get-tuple-element.43), channel_id=1, source_target_pairs={{4,8},{8,4},{5,9},{9,5},{6,10},{10,6},{7,11},{11,7},{20,24},{24,20... | collective-permute-start | bytes 405512 | tf_op jit(solution)/shard_map/ppermute | solution.py:616
  51.9 10.6 %collective-permute-start.18 = (bf16[2,2,64,256]{3,2,1,0:T(8,128)(2,1)S(1)}, bf16[2,2,64,256]{3,2,1,0:T(8,128)(2,1)S(1)}, u32[]{:S(2)}, u32[]{:S(2)}) collective-permute-start(bf16[2,2,64,256]{3,2,1,0:T(8,128)(2,1)S(1)} %pad_maximum_fusion.mine), channel_id=1, source_target_pairs={{0,4},{4,0},{8,12},{12,8},{1,5},{5,1},{9,13},{13,9},{2,6},{6,2},{1... | collective-permute-start | bytes 393224 | tf_op jit(solution)/shard_map/ppermute | solution.py:591
